TPU v7x, 128 devices: a whole 4x4x4 slice. The times are simulated.
128 devices in a mesh: dp: 16 (over y, z), head: 4 (over x_lo, core), group: 2 (over x_hi).
Axes of the slice: x: 4 (x_hi: 2, x_lo: 2; x = x_hi * 2 + x_lo), y: 4, z: 4, core: 2. Of those that a mesh axis runs over, the one named last changes fastest.
Arguments:
- tokens: bfloat16 [8192, 2048], P(('dp', 'head')), may hold values from -6 to 6
- grad_out: bfloat16 [8192, 2048], P(('dp', 'head')), may hold values from -6 to 6
- w_qkv: bfloat16 [3, 2048, 1024], P(None, None, ('head', 'group')), may hold values from -4 to 4
- w_attn_out: bfloat16 [1024, 2048], P(('head', 'group')), may hold values from -0.1875 to 0.1875
- gain_attn: float32 [2048], replicated, may hold values from 0.25 to 1.75
- gain_ffn: float32 [2048], replicated, may hold values from 0.25 to 1.75
- w_gate_up: bfloat16 [64, 2, 2048, 1408], P(('dp', 'head'), None, None, 'group'), may hold values from -0.125 to 0.125
- w_down: bfloat16 [64, 1408, 2048], P(('dp', 'head'), 'group'), may hold values from -0.15625 to 0.15625
- expert_ids: int32 [8192, 2], P(('dp', 'head')), may hold values from 0 to 63, all different within a row; in each aligned block of 128 rows (0 to 127, 128 to 255, ...) at most 5 rows name the same one
- gates: float32 [8192, 2], P(('dp', 'head')), may hold values from 0.05 to 0.5
Outputs:
- grad_tokens: bfloat16 [8192, 2048], P(('dp', 'head'))
- grad_qkv: float32 [3, 2048, 1024], P(None, 'dp', ('head', 'group'))
- grad_attn_out: float32 [1024, 2048], P(('head', 'group'), 'dp')
- grad_gate_up: bfloat16 [64, 2, 2048, 1408], P(('dp', 'head'), None, None, 'group')
- grad_down: bfloat16 [64, 1408, 2048], P(('dp', 'head'), 'group')
Inputs may be any that keep to these rules, and one draw needn't show every extreme that they name: `expert_ids`: each row names 2 different experts; in each aligned block of 128 rows no expert is named by more than 5 rows.
All inputs are finite; a program needn't handle non-finite values.
Results may differ from a plain program's by a relative error of at most 0.012.
Values may be sent and summed in bfloat16 or wider, within the bound.
No kernel may reach another device: no remote copies, remote signals or barrier semaphores. Data moves between devices by JAX's collectives and lax.ppermute only.
A program may use at most 128 MiB of HBM per device.

v0:
```python
import jax
import jax.numpy as jnp
from jax import lax
from jax.experimental import pallas as pl
from jax.experimental.pallas import tpu as pltpu
from jax.sharding import PartitionSpec as P


HD = 128
CAP = 5
BF = jnp.bfloat16
F32 = jnp.float32
ALL = ("group", "dp", "head")
HG = ("head", "group")
EPSILON = 1e-06
VMEM = pl.BlockSpec(memory_space=pltpu.VMEM)
SMEM = pl.BlockSpec(memory_space=pltpu.SMEM)
HBM = pl.BlockSpec(memory_space=pl.ANY)


def inverse_rms(values):
    return lax.rsqrt(jnp.mean(values * values, axis=-1, keepdims=True) + EPSILON)


def norm_backward(values, scaling, gain, upstream):
    weighted = upstream * gain
    normed = values * scaling
    return scaling * (weighted - normed * jnp.mean(weighted * normed, axis=-1, keepdims=True))


def dot(a, b, dims=((1,), (0,))):
    return lax.dot_general(a, b, (dims, ((), ())), preferred_element_type=F32)


def shaped(shape, dtype):
    return jax.ShapeDtypeStruct(shape, dtype)


def call(kernel, outs, specs, scratch=(), flops=0, moved=0):
    return pl.pallas_call(
        kernel,
        out_shape=outs,
        in_specs=specs,
        out_specs=jax.tree.map(lambda _: VMEM, outs),
        scratch_shapes=list(scratch),
        cost_estimate=pl.CostEstimate(flops=flops, bytes_accessed=moved, transcendentals=0),
    )


def spread(scratch, values):
    slots, wide = values.shape
    n = wide // 128
    for c in range(n):
        scratch[pl.ds(c, slots, stride=n), :] = values[:, c * 128 : (c + 1) * 128]


def targets_of(along_rows, along_cols, axis):
    rows = along_rows.shape[1]
    row_id = lax.broadcasted_iota(jnp.int32, (rows, rows), 0)
    col_id = lax.broadcasted_iota(jnp.int32, (rows, rows), 1)
    before = row_id < col_id if axis == 0 else col_id < row_id
    found = []
    for k in range(2):
        if axis == 0:
            named = along_rows[k : k + 1, :]
            same = (along_cols[:, 0:1] == named) | (along_cols[:, 1:2] == named)
        else:
            named = along_cols[:, k : k + 1]
            same = (along_rows[0:1, :] == named) | (along_rows[1:2, :] == named)
        count = jnp.sum(jnp.where(same & before, 1.0, 0.0), axis=axis, keepdims=True)
        found.append(named * CAP + count.astype(jnp.int32))
    return found


def pick_matrix(along_rows, along_cols, slots):
    rows = along_rows.shape[1]
    targets = targets_of(along_rows[...], along_cols[...], 0)
    slot = lax.broadcasted_iota(jnp.int32, (slots, rows), 0)
    return slot == targets[0], slot == targets[1]


def attention_kernel(me, t0, t1, t2, t3, gain, w, query, key, value, chances, mixed, normed):
    rows = t0.shape[0]
    for k, t in enumerate((t0, t1, t2, t3)):
        values = t[...].astype(F32)
        normed[k * rows : (k + 1) * rows, :] = (values * inverse_rms(values) * gain[...]).astype(BF)
    weights = jnp.concatenate([w[0], w[1], w[2]], axis=1)
    proj = dot(normed[...], weights).astype(BF)
    q, k, v = proj[:, :HD], proj[:, HD : 2 * HD], proj[:, 2 * HD :]
    query[...] = q
    key[...] = k
    value[...] = v
    length = 4 * rows
    scores = dot(q, k, ((1,), (1,))) * HD ** (-0.5)
    row = lax.broadcasted_iota(jnp.int32, (length, length), 0)
    col = lax.broadcasted_iota(jnp.int32, (length, length), 1)
    row = ((row // rows) ^ me[0]) * rows + row % rows
    col = ((col // rows) ^ me[0]) * rows + col % rows
    scores = jnp.where(col <= row, scores, -1e30)
    powered = jnp.exp(scores - jnp.max(scores, axis=-1, keepdims=True))
    probs = powered / jnp.sum(powered, axis=-1, keepdims=True)
    chances[...] = probs
    mixed[...] = dot(probs.astype(BF), v).astype(BF)


def attention(me, blocks, gain, w_qkv):
    rows, width = blocks[0].shape
    length = 4 * rows
    head = shaped((length, HD), BF)
    return call(
        attention_kernel,
        (head, head, head, shaped((length, length), F32), head, shaped((length, width), BF)),
        [SMEM] + [VMEM] * 6,
        flops=2 * length * (3 * width + 2 * length) * HD,
        moved=2 * length * width * 2 + 3 * width * HD * 2 + length * length * 4,
    )(me, *blocks, gain, w_qkv)


def project_kernel(me, m0, m1, m2, m3, w0, w1, w2, w3, mine, other):
    half = w0.shape[1] // 2
    total = []
    for j in range(2):
        part = None
        for m, w in ((m0, w0), (m1, w1), (m2, w2), (m3, w3)):
            term = dot(m[...], w[:, j * half : (j + 1) * half])
            part = term if part is None else part + term
        total.append(part)
    first = me[1] == 0
    mine[...] = jnp.where(first, total[0], total[1])
    other[...] = jnp.where(first, total[1], total[0]).astype(BF)


def project(me, mixed, weights):
    rows, width = mixed[0].shape[0], weights[0].shape[1]
    return call(
        project_kernel,
        (shaped((rows, width // 2), F32), shaped((rows, width // 2), BF)),
        [SMEM] + [VMEM] * 8,
        flops=8 * rows * HD * width,
        moved=8 * HD * width,
    )(me, *mixed, *weights)


def grads_kernel(me, ids, ids_t, gates, grad_out, sent, scratch):
    half = grad_out.shape[1] // 2
    slots = CAP * sent.shape[0] // (2 * CAP * half // 128)
    first, second = pick_matrix(ids_t, ids, slots)
    scale = jnp.sum(
        jnp.where(first, gates[0:1, :], 0.0) + jnp.where(second, gates[1:2, :], 0.0),
        axis=1,
        keepdims=True,
    )
    picker = (first | second).astype(BF)
    chosen = jnp.where(me[1] == 0, grad_out[:, :half], grad_out[:, half:])
    spread(scratch, dot(picker, chosen) * scale)
    tiles = scratch[...].astype(BF)
    count = tiles.shape[0]
    sent[:count, :] = tiles
    sent[count:, :] = tiles


def hidden_kernel(me, ids, ids_t, tokens, mine, other, hidden, sent, scratch):
    half = mine.shape[1]
    slots = CAP * sent.shape[0] // (2 * CAP * half // 128)
    first, second = pick_matrix(ids_t, ids, slots)
    picker = (first | second).astype(BF)
    chosen = jnp.where(me[1] == 0, tokens[:, :half], tokens[:, half:]).astype(F32)
    rows = (chosen + (mine[...] + other[...].astype(F32))).astype(BF)
    hidden[...] = rows
    spread(scratch, dot(picker, rows))
    tiles = scratch[...].astype(BF)
    count = tiles.shape[0]
    sent[:count, :] = tiles
    sent[count:, :] = tiles


def send_grads(me, ids, ids_t, gates, grad_out, experts):
    rows, width = grad_out.shape
    tiles = experts * CAP * width // 2 // 128
    return call(
        grads_kernel,
        shaped((2 * tiles, 128), BF),
        [SMEM] + [VMEM] * 4,
        [pltpu.VMEM((tiles, 128), F32)],
        flops=2 * experts * CAP * rows * width // 2,
        moved=tiles * 512,
    )(me, ids, ids_t, gates, grad_out)


def send_hidden(me, ids, ids_t, tokens, mine, other, experts):
    rows, width = tokens.shape
    tiles = experts * CAP * width // 2 // 128
    return call(
        hidden_kernel,
        (shaped((rows, width // 2), BF), shaped((2 * tiles, 128), BF)),
        [SMEM] + [VMEM] * 5,
        [pltpu.VMEM((tiles, 128), F32)],
        flops=2 * experts * CAP * rows * width // 2,
        moved=tiles * 512,
    )(me, ids, ids_t, tokens, mine, other)


def gathered(scratch, got, slots, wide):
    n = wide // 2 // 128
    tiles = slots * n
    pieces = []
    for g in range(2):
        scratch[...] = got[g * tiles : (g + 1) * tiles, :].astype(F32)
        pieces.extend(scratch[pl.ds(c, slots, stride=n), :] for c in range(n))
    return jnp.concatenate(pieces, axis=1)


def expert_kernel(
    got_hidden, got_grads, gain, w_pair, w_down, sent, in_rows, in_grads, product, gate_grad,
    up_grad, scratch, pair_ref, down_ref, sems
):
    copies = [
        pltpu.make_async_copy(w_pair.at[0, 0], pair_ref.at[0], sems.at[0]),
        pltpu.make_async_copy(w_pair.at[0, 1], pair_ref.at[1], sems.at[1]),
        pltpu.make_async_copy(w_down.at[0], down_ref, sems.at[2]),
    ]
    for copy in copies:
        copy.start()
    slots, width = in_rows.shape
    values = gathered(scratch, got_hidden, slots, width)
    in_rows[...] = (values * inverse_rms(values) * gain[...]).astype(BF)
    in_grads[...] = gathered(scratch, got_grads, slots, width).astype(BF)
    rows = in_rows[...]
    copies[0].wait()
    gate_pre = dot(rows, pair_ref[0], ((1,), (1,)))
    copies[1].wait()
    up_pre = dot(rows, pair_ref[1], ((1,), (1,)))
    copies[2].wait()
    upstream = dot(in_grads[...], down_ref[...], ((1,), (1,)))
    sigma = 1.0 / (1.0 + jnp.exp(-gate_pre))
    active = gate_pre * sigma
    product[...] = (active * up_pre).astype(BF)
    gate_grad[...] = (upstream * up_pre * sigma * (1.0 + gate_pre * (1.0 - sigma))).astype(BF)
    up_grad[...] = (upstream * active).astype(BF)
    half = width // 2
    tiles = scratch.shape[0]
    for g in range(2):
        piece = slice(g * half, (g + 1) * half)
        returned = dot(gate_grad[...], pair_ref[0, :, piece]) + dot(
            up_grad[...], pair_ref[1, :, piece]
        )
        spread(scratch, returned)
        sent[g * tiles : (g + 1) * tiles, :] = scratch[...].astype(BF)


def experts_forward(got_hidden, got_grads, gain, w_pair, w_down):
    inner, width = w_pair.shape[2:]
    tiles = got_hidden.shape[0] // 2
    slots = tiles * 256 // width
    row, unit = shaped((slots, width), BF), shaped((slots, inner), BF)
    return call(
        expert_kernel,
        (shaped((2 * tiles, 128), BF), row, row, unit, unit, unit),
        [VMEM] * 3 + [HBM] * 2,
        [
            pltpu.VMEM((tiles, 128), F32),
            pltpu.VMEM((2, inner, width), BF),
            pltpu.VMEM((inner, width), BF),
            pltpu.SemaphoreType.DMA((3,)),
        ],
        flops=10 * slots * width * inner,
        moved=6 * width * inner,
    )(got_hidden, got_grads, gain, w_pair, w_down)


def expert_grads_kernel(in_rows, in_grads, product, gate_grad, up_grad, pair, down):
    rows = in_rows[...]
    pair[0, 0] = dot(gate_grad[...], rows, ((0,), (0,))).astype(BF)
    pair[0, 1] = dot(up_grad[...], rows, ((0,), (0,))).astype(BF)
    down[0] = dot(product[...], in_grads[...], ((0,), (0,))).astype(BF)


def expert_grads(in_rows, in_grads, product, gate_grad, up_grad):
    slots, width = in_rows.shape
    inner = product.shape[1]
    parts = 4
    row = pl.BlockSpec((slots, width // parts), lambda i: (0, i))
    unit = pl.BlockSpec((slots, inner), lambda i: (0, 0))
    return pl.pallas_call(
        expert_grads_kernel,
        out_shape=(shaped((1, 2, inner, width), BF), shaped((1, inner, width), BF)),
        grid=(parts,),
        in_specs=[row, row, unit, unit, unit],
        out_specs=(
            pl.BlockSpec((1, 2, inner, width // parts), lambda i: (0, 0, 0, i)),
            pl.BlockSpec((1, inner, width // parts), lambda i: (0, 0, i)),
        ),
        cost_estimate=pl.CostEstimate(
            flops=6 * slots * width * inner, bytes_accessed=6 * width * inner, transcendentals=0
        ),
    )(in_rows, in_grads, product, gate_grad, up_grad)


def combine_kernel(ids, ids_t, got, out, scratch):
    rows, half = out.shape
    tiles = scratch.shape[0]
    n = half // 128
    slots = tiles // n
    scratch[...] = got[:tiles, :].astype(F32) + got[tiles:, :].astype(F32)
    values = jnp.concatenate(
        [scratch[pl.ds(c, slots, stride=n), :] for c in range(n)], axis=1
    ).astype(BF)
    slot = lax.broadcasted_iota(jnp.int32, (rows, slots), 1)
    targets = targets_of(ids_t[...], ids[...], 1)
    picker = ((slot == targets[0]) | (slot == targets[1])).astype(BF)
    out[...] = dot(picker, values).astype(BF)


def combine(ids, ids_t, got, half):
    rows = ids.shape[0]
    tiles = got.shape[0] // 2
    return call(
        combine_kernel,
        shaped((rows, half), BF),
        [VMEM] * 3,
        [pltpu.VMEM((tiles, 128), F32)],
        flops=2 * rows * tiles * 128,
        moved=tiles * 512,
    )(ids, ids_t, got)


def hidden_grad_kernel(
    me, grad_out, hidden_mine, hidden_other, normed_mine, normed_other, gain, w0, w1, w2, w3,
    grad, rounded, p0, p1, p2, p3
):
    first = me[1] == 0

    def whole(mine, other):
        a, b = mine[...].astype(F32), other[...].astype(F32)
        return jnp.concatenate([jnp.where(first, a, b), jnp.where(first, b, a)], axis=1)

    hidden = whole(hidden_mine, hidden_other)
    upstream = whole(normed_mine, normed_other)
    value = grad_out[...].astype(F32) + norm_backward(
        hidden, inverse_rms(hidden), gain[...], upstream
    )
    grad[...] = value
    low = value.astype(BF)
    rounded[...] = low
    for p, w in ((p0, w0), (p1, w1), (p2, w2), (p3, w3)):
        p[...] = dot(low, w[...], ((1,), (1,))).astype(BF)


def hidden_grad(me, grad_out, halves, gain, weights):
    rows, width = grad_out.shape
    piece = shaped((rows, HD), BF)
    return call(
        hidden_grad_kernel,
        (shaped((rows, width), F32), shaped((rows, width), BF), piece, piece, piece, piece),
        [SMEM] + [VMEM] * 10,
        flops=8 * rows * width * HD,
        moved=8 * HD * width + 10 * rows * width,
    )(me, grad_out, *halves, gain, *weights)


def attention_back_kernel(
    g0, g1, g2, g3, query, key, value, chances, w, acts, near, far, near_out, far_out
):
    rows = g0.shape[0]
    grad = jnp.concatenate([g0[...], g1[...], g2[...], g3[...]], axis=0)
    probs = chances[...]
    grad_weights = dot(grad, value[...], ((1,), (1,)))
    total = jnp.sum(probs * grad_weights, axis=-1, keepdims=True)
    scores = (probs * (grad_weights - total) * HD ** (-0.5)).astype(BF)
    acts[:, :HD] = dot(scores, key[...]).astype(BF)
    acts[:, HD : 2 * HD] = dot(scores, query[...], ((0,), (0,))).astype(BF)
    acts[:, 2 * HD :] = dot(probs.astype(BF), grad, ((0,), (0,))).astype(BF)
    weights = jnp.concatenate([w[0], w[1], w[2]], axis=1)
    for k, out in enumerate((near, near_out, far, far_out)):
        part = dot(acts[k * rows : (k + 1) * rows, :], weights, ((1,), (1,)))
        out[...] = part.astype(out.dtype)


def attention_back(grads, query, key, value, chances, w_qkv):
    rows = grads[0].shape[0]
    width = w_qkv.shape[1]
    length = 4 * rows
    kept, sent = shaped((rows, width), F32), shaped((rows, width), BF)
    return call(
        attention_back_kernel,
        (shaped((length, 3 * HD), BF), kept, kept, sent, sent),
        [VMEM] * 9,
        flops=2 * length * (3 * width + 4 * length) * HD,
        moved=3 * width * HD * 2 + length * length * 4 + 3 * length * width,
    )(*grads, query, key, value, chances, w_qkv)


def weight_kernel(acts, normed, mixed, g0, g1, g2, g3, sent):
    pieces = sent.shape[0]
    wide = acts.shape[1]
    left = dot(acts[...], normed[...], ((0,), (0,))).astype(BF)
    grads = jnp.concatenate([g0[...], g1[...], g2[...], g3[...]], axis=0)
    right = dot(mixed[...], grads, ((0,), (0,))).astype(BF)
    for j in range(pieces):
        sent[j, :wide, :] = left[:, j * 128 : (j + 1) * 128]
        sent[j, wide:, :] = right[:, j * 128 : (j + 1) * 128]


def weight_grads(acts, normed, mixed, grads, pieces):
    length, width = normed.shape
    return call(
        weight_kernel,
        shaped((pieces, 4 * HD, width // pieces), BF),
        [VMEM] * 7,
        flops=8 * length * width * HD,
        moved=4 * length * width + 8 * HD * width,
    )(acts, normed, mixed, *grads)


def weight_sum_kernel(got, qkv, out):
    total = jnp.sum(got[...].astype(F32), axis=0)
    for i in range(3):
        qkv[i] = total[i * HD : (i + 1) * HD, :].T
    out[...] = total[3 * HD :, :]


def weight_sum(got):
    piece = got.shape[2]
    return call(
        weight_sum_kernel,
        (shaped((3, piece, HD), F32), shaped((HD, piece), F32)),
        [VMEM],
        flops=got.size,
        moved=got.size * 2,
    )(got)


def split_kernel(me, near, near_in, far, far_in, mine, near_other, far_mine, far_other):
    small = mine.shape[0]
    here = near[...] + near_in[...].astype(F32)
    there = far[...] + far_in[...].astype(F32)
    first = me[1] == 0
    mine[...] = jnp.where(first, here[:small], here[small:])
    near_other[...] = jnp.where(first, here[small:], here[:small]).astype(BF)
    far_mine[...] = jnp.where(first, there[:small], there[small:]).astype(BF)
    far_other[...] = jnp.where(first, there[small:], there[:small]).astype(BF)


def split_sums(me, near, near_in, far, far_in):
    rows, width = near.shape
    low = shaped((rows // 2, width), BF)
    return call(
        split_kernel,
        (shaped((rows // 2, width), F32), low, low, low),
        [SMEM] + [VMEM] * 4,
        flops=4 * rows * width,
        moved=20 * rows * width,
    )(me, near, near_in, far, far_in)


def tokens_kernel(me, mine, a, b, c, tokens, grad_hidden, gain, out):
    small = mine.shape[0]
    first = me[1] == 0
    upstream = (
        mine[...] + a[...].astype(F32) + b[...].astype(F32) + c[...].astype(F32)
    )
    values = jnp.where(first, tokens[:small], tokens[small:]).astype(F32)
    before = jnp.where(first, grad_hidden[:small], grad_hidden[small:])
    back = norm_backward(values, inverse_rms(values), gain[...], upstream)
    out[...] = (before + back).astype(BF)


def tokens_grad(me, mine, arrived, tokens, grad_hidden, gain):
    small, width = mine.shape
    return call(
        tokens_kernel,
        shaped((small, width), BF),
        [SMEM] + [VMEM] * 7,
        flops=20 * small * width,
        moved=30 * small * width,
    )(me, mine, *arrived, tokens, grad_hidden, gain)


def join_kernel(me, mine, other, out):
    small = mine.shape[0]
    first = me[1] == 0
    out[:small] = jnp.where(first, mine[...], other[...])
    out[small:] = jnp.where(first, other[...], mine[...])


def join(me, mine, other):
    small, width = mine.shape
    return call(
        join_kernel,
        shaped((2 * small, width), BF),
        [SMEM] + [VMEM] * 2,
        moved=8 * small * width,
    )(me, mine, other)


def swap(x, head_bits, group_bit):
    flip = head_bits * 2 + group_bit
    return lax.ppermute(x, HG, [(i, i ^ flip) for i in range(8)])


def sequence(x):
    small = x.shape[0] // 2
    top, bottom = x[:small], x[small:]
    far = jnp.concatenate([swap(top, 2, 0), swap(bottom, 2, 1)], axis=0)
    return [x, swap(x, 1, 0), far, swap(far, 1, 0)]


def exchange(tiles):
    count = lax.axis_size(ALL)
    tiles = tiles.reshape(count, -1, 128)
    return lax.all_to_all(tiles, ALL, 0, 0, tiled=True).reshape(-1, 128)


def body(
    tokens, grad_out, w_qkv, w_attn_out, gain_attn, gain_ffn, w_gate_up, w_down, ids, gates
):
    rows, width = tokens.shape
    half = width // 2
    experts = lax.axis_size("dp") * lax.axis_size("head")
    me = jnp.stack([lax.axis_index("head"), lax.axis_index("group")]).astype(jnp.int32)
    gain_attn, gain_ffn = gain_attn[None], gain_ffn[None]
    w_pair = w_gate_up.transpose(0, 1, 3, 2)
    ids_t, gates_t = ids.T, gates.T

    blocks = sequence(tokens)
    tiles = send_grads(me, ids, ids_t, gates_t, grad_out, experts)
    got_grads = exchange(tiles)
    w_far, blocks[2] = lax.optimization_barrier((w_attn_out, blocks[2]))
    w_far = swap(w_far, 2, 0)
    weights = [w_attn_out, swap(w_attn_out, 1, 0), w_far, swap(w_far, 1, 0)]

    query, key, value, chances, mixed, normed = attention(me, blocks, gain_attn, w_qkv)
    heads = [mixed[k * rows : (k + 1) * rows] for k in range(4)]
    heads = [heads[0]] + [swap(heads[k], k, 0) for k in range(1, 4)]
    mine, other = project(me, heads, weights)
    other = swap(other, 0, 1)
    hidden, tiles = send_hidden(me, ids, ids_t, tokens, mine, other, experts)
    tiles, got_grads = lax.optimization_barrier((tiles, got_grads))
    hidden_other = swap(hidden, 0, 1)
    got_hidden = exchange(tiles)
    got_hidden, hidden_other = lax.optimization_barrier((got_hidden, hidden_other))

    tiles, *saved = experts_forward(got_hidden, got_grads, gain_ffn, w_pair, w_down)
    grad_pair, grad_down = expert_grads(*saved)
    got_back = exchange(tiles)
    got_back, grad_pair, grad_down = lax.optimization_barrier((got_back, grad_pair, grad_down))

    upstream = combine(ids, ids_t, got_back, half)
    halves = (hidden, hidden_other, upstream, swap(upstream, 0, 1))
    grad_hidden, rounded, *grads = hidden_grad(me, grad_out, halves, gain_ffn, weights)
    grads = [grads[0]] + [swap(grads[k], k, 0) for k in range(1, 4)]
    all_grads = sequence(rounded)

    acts, near, far, near_out, far_out = attention_back(grads, query, key, value, chances, w_qkv)
    near_in = swap(near_out, 1, 0)
    far_in = swap(far_out, 1, 0)
    sent = weight_grads(acts, normed, mixed, all_grads, lax.axis_size("dp"))
    got = lax.all_to_all(sent, "dp", 0, 0, tiled=True)
    mine, near_other, far_mine, far_other = split_sums(me, near, near_in, far, far_in)
    arrived = (swap(near_other, 0, 1), swap(far_mine, 2, 0), swap(far_other, 2, 1))
    done = tokens_grad(me, mine, arrived, tokens, grad_hidden, gain_attn)
    done_other = swap(done, 0, 1)
    grad_tokens = join(me, done, done_other)
    grad_qkv, grad_attn_out = weight_sum(got)
    return (grad_tokens, grad_qkv, grad_attn_out, grad_pair.transpose(0, 1, 3, 2), grad_down)


def solution(mesh):
    return jax.shard_map(
        body,
        mesh=mesh,
        in_specs=(
            P(("dp", "head"), None),
            P(("dp", "head"), None),
            P(None, None, ("head", "group")),
            P(("head", "group"), None),
            P(),
            P(),
            P(("dp", "head"), None, None, "group"),
            P(("dp", "head"), "group", None),
            P(("dp", "head"), None),
            P(("dp", "head"), None),
        ),
        out_specs=(
            P(("dp", "head"), None),
            P(None, "dp", ("head", "group")),
            P(("head", "group"), "dp"),
            P(("dp", "head"), None, None, "group"),
            P(("dp", "head"), "group", None),
        ),
        check_vma=False,
    )
```

profile of v0, /device:TPU:0, one launch (start us, length us, event | category | flops | bytes accessed | tf_op | source)
XLA Modules:
  0.0 229.7 jit_solution(372544156539158673)
XLA Ops:
  5.6 4.2 %collective-permute-done.1 = bf16[64,2048]{1,0:T(8,128)(2,1)S(1)} collective-permute-done((bf16[64,2048]{1,0:T(8,128)(2,1)S(1)}, bf16[64,2048]{1,0:T(8,128)(2,1)S(1)}, u32[]{:S(2)}, u32[]{:S(2)}) %collective-permute-start.1) | collective-permute-done | bytes 262176 | tf_op jit(solution)/shard_map/ppermute | solution.py:498
  9.8 2.6 %collective-permute-done.2 = bf16[64,2048]{1,0:T(8,128)(2,1)S(1)} collective-permute-done((bf16[64,2048]{1,0:T(8,128)(2,1)S(1)}, bf16[64,2048]{1,0:T(8,128)(2,1)S(1)}, u32[]{:S(2)}, u32[]{:S(2)}) %collective-permute-start.2) | collective-permute-done | bytes 262176 | tf_op jit(solution)/shard_map/ppermute | solution.py:498
  13.9 2.8 %shard_map.140 = bf16[5120,128]{1,0:T(8,128)(2,1)} custom-call(s32[2]{0:T(128)} %pad_add_fusion.me, s32[128,2]{1,0:T(8,128)} %copy.15.ids, s32[2,128]{1,0:T(2,128)} %bitcast.21, f32[2,128]{1,0:T(2,128)} %bitcast.26, bf16[128,2048]{1,0:T(8,128)(2,1)} %grad_out.3), custom_call_target="tpu_custom_call" | custom-call | flops 83886080 | bytes 1310720 | tf_op jit(solution)/shard_map/pallas_call | solution.py:180
  16.7 12.0 %all-to-all-start = ((bf16[128,40,128]{2,1,0:T(8,128)(2,1)}), bf16[128,40,128]{2,1,0:T(8,128)(2,1)}, u32[]{:S(2)}, u32[]{:S(2)}) async-start(bf16[128,40,128]{2,1,0:T(8,128)(2,1)} %bitcast.14), calls=%async_computation | async-start | bytes 2621440 | tf_op jit(solution)/shard_map/all_to_all | solution.py:511
  32.4 5.5 %shard_map.137 = (bf16[512,128]{1,0:T(8,128)(2,1)}, bf16[512,128]{1,0:T(8,128)(2,1)}, bf16[512,128]{1,0:T(8,128)(2,1)}, f32[512,512]{1,0:T(8,128)}, bf16[512,128]{1,0:T(8,128)(2,1)}, /*index=5*/bf16[512,2048]{1,0:T(8,128)(2,1)}) custom-call(s32[2]{0:T(128)} %pad_add_fusion.me, bf16[128,2048]{1,0:T(8,128)(2,1)} %tokens.3, bf16[128,2048]{1,0:T(8,128)(2,1)} %copy-done.10, ...), custom_call_target="tpu_custom_call" | custom-call | flops 939524096 | bytes 6815744 | tf_op jit(solution)/shard_map/pallas_call | solution.py:110
  41.1 2.6 %collective-permute-done.6.m3 = bf16[128,128]{1,0:T(8,128)(2,1)S(1)} collective-permute-done((bf16[128,128]{1,0:T(8,128)(2,1)S(1)}, bf16[128,128]{1,0:T(8,128)(2,1)S(1)}, u32[]{:S(2)}, u32[]{:S(2)}) %collective-permute-start.6) | collective-permute-done | bytes 32800 | tf_op jit(solution)/shard_map/ppermute | solution.py:498
  45.8 3.2 %shard_map.138 = (f32[128,1024]{1,0:T(8,128)}, bf16[128,1024]{1,0:T(8,128)(2,1)}) custom-call(s32[2]{0:T(128)} %pad_add_fusion.me, bf16[128,128]{1,0:T(8,128)(2,1)} %get-tuple-element.100.m0, bf16[128,128]{1,0:T(8,128)(2,1)} %copy-done.26, bf16[128,128]{1,0:T(8,128)(2,1)} %copy-done.25, bf16[128,128]{1,0:T(8,128)(2,1)} %copy-done.24, bf16[128,2048]{1,0:T(8,128)(2,1)} %w0.3, ...), custom_call_target="tpu_custom_call" | custom-call | flops 268435456 | bytes 2097152 | tf_op jit(solution)/shard_map/pallas_call | solution.py:135
  49.0 2.7 %collective-permute-start.10 = (bf16[128,1024]{1,0:T(8,128)(2,1)}, bf16[128,1024]{1,0:T(8,128)(2,1)S(1)}, u32[]{:S(2)}, u32[]{:S(2)}) collective-permute-start(bf16[128,1024]{1,0:T(8,128)(2,1)} %get-tuple-element.53), channel_id=1, source_target_pairs={{0,1},{1,0},{2,3},{3,2},{4,5},{5,4},{6,7},{7,6},{8,9},{9,8},{10,11... | collective-permute-start | bytes 786440 | tf_op jit(solution)/shard_map/ppermute | solution.py:498
  51.7 7.1 %collective-permute-done.10.other = bf16[128,1024]{1,0:T(8,128)(2,1)S(1)} collective-permute-done((bf16[128,1024]{1,0:T(8,128)(2,1)}, bf16[128,1024]{1,0:T(8,128)(2,1)S(1)}, u32[]{:S(2)}, u32[]{:S(2)}) %collective-permute-start.10) | collective-permute-done | bytes 262176 | tf_op jit(solution)/shard_map/ppermute | solution.py:498
  59.5 3.0 %shard_map.139 = (bf16[128,1024]{1,0:T(8,128)(2,1)}, bf16[5120,128]{1,0:T(8,128)(2,1)}) custom-call(s32[2]{0:T(128)} %pad_add_fusion.me, s32[128,2]{1,0:T(8,128)} %copy.15.ids, s32[2,128]{1,0:T(2,128)} %bitcast.22, bf16[128,2048]{1,0:T(8,128)(2,1)} %tokens.3, f32[128,1024]{1,0:T(8,128)} %get-tuple-element.52.mine, bf16[128,1024]{1,0:T(8,128)(2,1)} %copy-done.16), custom_call_target="tpu_custom_call" | custom-call | flops 83886080 | bytes 1310720 | tf_op jit(solution)/shard_map/pallas_call | solution.py:193
  62.5 10.0 %all-to-all-start.1 = ((bf16[128,40,128]{2,1,0:T(8,128)(2,1)}), bf16[128,40,128]{2,1,0:T(8,128)(2,1)S(1)}, u32[]{:S(2)}, u32[]{:S(2)}) async-start(bf16[128,40,128]{2,1,0:T(8,128)(2,1)} %bitcast.17), calls=%async_computation.1 | async-start | bytes 2621440 | tf_op jit(solution)/shard_map/all_to_all | solution.py:511
  72.5 2.7 %collective-permute-start.11 = (bf16[128,1024]{1,0:T(8,128)(2,1)S(1)}, bf16[128,1024]{1,0:T(8,128)(2,1)S(1)}, u32[]{:S(2)}, u32[]{:S(2)}) collective-permute-start(bf16[128,1024]{1,0:T(8,128)(2,1)S(1)} %copy-done.18), channel_id=1, source_target_pairs={{0,1},{1,0},{2,3},{3,2},{4,5},{5,4},{6,7},{7,6},{8,9},{9,8},{10,11... | collective-permute-start | bytes 786440 | tf_op jit(solution)/shard_map/ppermute | solution.py:498
  75.2 19.7 %collective-permute-done.11.hidden_other = bf16[128,1024]{1,0:T(8,128)(2,1)S(1)} collective-permute-done((bf16[128,1024]{1,0:T(8,128)(2,1)S(1)}, bf16[128,1024]{1,0:T(8,128)(2,1)S(1)}, u32[]{:S(2)}, u32[]{:S(2)}) %collective-permute-start.11) | collective-permute-done | bytes 262176 | tf_op jit(solution)/shard_map/ppermute | solution.py:498
  96.0 11.4 %shard_map.141 = (bf16[5120,128]{1,0:T(8,128)(2,1)}, bf16[320,2048]{1,0:T(8,128)(2,1)}, bf16[320,2048]{1,0:T(8,128)(2,1)}, bf16[320,704]{1,0:T(8,128)(2,1)}, bf1...) custom-call(bf16[5120,128]{1,0:T(8,128)(2,1)} %bitcast.16, bf16[5120,128]{1,0:T(8,128)(2,1)} %bitcast.6.got_grads, ...), custom_call_target="tpu_custom_call" | custom-call | flops 4613734400 | bytes 8650752 | tf_op jit(solution)/shard_map/pallas_call | solution.py:256
  107.4 9.3 %all-to-all-start.2 = ((bf16[128,40,128]{2,1,0:T(8,128)(2,1)}), bf16[128,40,128]{2,1,0:T(8,128)(2,1)S(1)}, u32[]{:S(2)}, u32[]{:S(2)}) async-start(bf16[128,40,128]{2,1,0:T(8,128)(2,1)} %bitcast.18), calls=%async_computation.2 | async-start | bytes 2621440 | tf_op jit(solution)/shard_map/all_to_all | solution.py:511
  116.7 8.0 %shard_map.142 = (bf16[1,2,704,2048]{3,2,1,0:T(8,128)(2,1)}, bf16[1,704,2048]{2,1,0:T(8,128)(2,1)}) custom-call(bf16[320,2048]{1,0:T(8,128)(2,1)} %get-tuple-element.61.in_rows, bf16[320,2048]{1,0:T(8,128)(2,1)} %get-tuple-element.62.in_grads, bf16[320,704]{1,0:T(8,128)(2,1)} %get-tuple-element.63.product, bf16[320,704]{1,0:T(8,128)(2,1)} %get-tuple-element.64.gate_grad, ...), custom_call_target="tpu_custom_call" | custom-call | flops 2768240640 | bytes 8650752 | tf_op jit(solution)/shard_map/pallas_call | solution.py:284
  124.7 14.0 %all-to-all-done.2 = bf16[128,40,128]{2,1,0:T(8,128)(2,1)S(1)} async-done(((bf16[128,40,128]{2,1,0:T(8,128)(2,1)}), bf16[128,40,128]{2,1,0:T(8,128)(2,1)S(1)}, u32[]{:S(2)}, u32[]{:S(2)}) %all-to-all-start.2) | async-done | bytes 1310752 | tf_op jit(solution)/shard_map/all_to_all | solution.py:511
  139.8 2.7 %shard_map.143.normed_mine = bf16[128,1024]{1,0:T(8,128)(2,1)} custom-call(s32[128,2]{1,0:T(8,128)} %copy.15.ids, s32[2,128]{1,0:T(2,128)} %bitcast.23, bf16[5120,128]{1,0:T(8,128)(2,1)} %bitcast.15), custom_call_target="tpu_custom_call" | custom-call | flops 83886080 | bytes 1310720 | tf_op jit(solution)/shard_map/pallas_call | solution.py:317
  143.2 8.5 %collective-permute-done.12.normed_other = bf16[128,1024]{1,0:T(8,128)(2,1)S(1)} collective-permute-done((bf16[128,1024]{1,0:T(8,128)(2,1)}, bf16[128,1024]{1,0:T(8,128)(2,1)S(1)}, u32[]{:S(2)}, u32[]{:S(2)}) %collective-permute-start.12) | collective-permute-done | bytes 262176 | tf_op jit(solution)/shard_map/ppermute | solution.py:498
  152.4 4.0 %shard_map.144 = (f32[128,2048]{1,0:T(8,128)}, bf16[128,2048]{1,0:T(8,128)(2,1)}, bf16[128,128]{1,0:T(8,128)(2,1)}, bf16[128,128]{1,0:T(8,128)(2,1)}, bf16[128,1...) custom-call(s32[2]{0:T(128)} %pad_add_fusion.me, bf16[128,2048]{1,0:T(8,128)(2,1)} %grad_out.3, ...), custom_call_target="tpu_custom_call" | custom-call | flops 268435456 | bytes 4718592 | tf_op jit(solution)/shard_map/pallas_call | solution.py:352
  159.5 4.5 %collective-permute-done.23 = bf16[64,2048]{1,0:T(8,128)(2,1)S(1)} collective-permute-done((bf16[64,2048]{1,0:T(8,128)(2,1)S(1)}, bf16[64,2048]{1,0:T(8,128)(2,1)S(1)}, u32[]{:S(2)}, u32[]{:S(2)}) %collective-permute-start.23) | collective-permute-done | bytes 262176 | tf_op jit(solution)/shard_map/ppermute | solution.py:498
  168.0 2.3 collective-permute-done.14.g2
  170.9 5.5 %shard_map.145 = (bf16[512,384]{1,0:T(8,128)(2,1)}, f32[128,2048]{1,0:T(8,128)}, f32[128,2048]{1,0:T(8,128)}, bf16[128,2048]{1,0:T(8,128)(2,1)}, bf16[128,2048]{1,0:T(8,128)(2,1)}) custom-call(bf16[128,128]{1,0:T(8,128)(2,1)} %get-tuple-element.69.g0, bf16[128,128]{1,0:T(8,128)(2,1)} %copy-done.31, bf16[128,128]{1,0:T(8,128)(2,1)} %copy-done.32, ...), custom_call_target="tpu_custom_call" | custom-call | flops 1073741824 | bytes 5767168 | tf_op jit(solution)/shard_map/pallas_call | solution.py:384
  177.4 4.9 %shard_map.149 = bf16[16,512,128]{2,1,0:T(8,128)(2,1)} custom-call(bf16[512,384]{1,0:T(8,128)(2,1)} %get-tuple-element.86.acts, bf16[512,2048]{1,0:T(8,128)(2,1)} %get-tuple-element.87.normed, bf16[512,128]{1,0:T(8,128)(2,1)} %get-tuple-element.50.mixed, bf16[128,2048]{1,0:T(8,128)(2,1)} %get-tuple-element.88.g0, bf16[128,2048]{1,0:T(8,128)(2,1)} %copy-done.14, ...), custom_call_target="tpu_custom_call" | custom-call | flops 1073741824 | bytes 6291456 | tf_op jit(solution)/shard_map/pallas_call | solution.py:406
  182.4 4.8 %all-to-all-start.3 = ((bf16[16,512,128]{2,1,0:T(8,128)(2,1)}), bf16[16,512,128]{2,1,0:T(8,128)(2,1)S(1)}, u32[]{:S(2)}, u32[]{:S(2)}) async-start(bf16[16,512,128]{2,1,0:T(8,128)(2,1)} %shard_map.149), calls=%async_computation.3 | async-start | bytes 4194304 | tf_op jit(solution)/shard_map/all_to_all | solution.py:558
  190.9 3.0 %shard_map.146 = (f32[64,2048]{1,0:T(8,128)}, bf16[64,2048]{1,0:T(8,128)(2,1)}, bf16[64,2048]{1,0:T(8,128)(2,1)}, bf16[64,2048]{1,0:T(8,128)(2,1)}) custom-call(s32[2]{0:T(128)} %pad_add_fusion.me, f32[128,2048]{1,0:T(8,128)} %get-tuple-element.77.near, bf16[128,2048]{1,0:T(8,128)(2,1)} %copy-done.12, f32[128,2048]{1,0:T(8,128)} %get-tuple-element.79.far, ...), custom_call_target="tpu_custom_call" | custom-call | flops 1048576 | bytes 5242880 | tf_op jit(solution)/shard_map/pallas_call | solution.py:447
  198.2 6.7 %collective-permute-done.18.a = bf16[64,2048]{1,0:T(8,128)(2,1)S(1)} collective-permute-done((bf16[64,2048]{1,0:T(8,128)(2,1)}, bf16[64,2048]{1,0:T(8,128)(2,1)S(1)}, u32[]{:S(2)}, u32[]{:S(2)}) %collective-permute-start.18) | collective-permute-done | bytes 262176 | tf_op jit(solution)/shard_map/ppermute | solution.py:498
  204.9 3.2 %collective-permute-done.19.b = bf16[64,2048]{1,0:T(8,128)(2,1)S(1)} collective-permute-done((bf16[64,2048]{1,0:T(8,128)(2,1)}, bf16[64,2048]{1,0:T(8,128)(2,1)S(1)}, u32[]{:S(2)}, u32[]{:S(2)}) %collective-permute-start.19) | collective-permute-done | bytes 262176 | tf_op jit(solution)/shard_map/ppermute | solution.py:498
  210.3 3.0 %shard_map.147.mine = bf16[64,2048]{1,0:T(8,128)(2,1)} custom-call(s32[2]{0:T(128)} %pad_add_fusion.me, f32[64,2048]{1,0:T(8,128)} %get-tuple-element.81.mine, bf16[64,2048]{1,0:T(8,128)(2,1)} %copy-done.20, bf16[64,2048]{1,0:T(8,128)(2,1)} %copy-done.21, bf16[64,2048]{1,0:T(8,128)(2,1)} %copy-done.22, bf16[128,2048]{1,0:T(8,128)(2,1)} %tokens.3, ...), custom_call_target="tpu_custom_call" | custom-call | flops 2621440 | bytes 3932160 | tf_op jit(solution)/shard_map/pallas_call | solution.py:470
  213.3 2.3 collective-permute-start.21
  215.6 7.7 %collective-permute-done.21.other = bf16[64,2048]{1,0:T(8,128)(2,1)S(1)} collective-permute-done((bf16[64,2048]{1,0:T(8,128)(2,1)}, bf16[64,2048]{1,0:T(8,128)(2,1)S(1)}, u32[]{:S(2)}, u32[]{:S(2)}) %collective-permute-start.21) | collective-permute-done | bytes 262176 | tf_op jit(solution)/shard_map/ppermute | solution.py:498
  227.1 2.6 %shard_map.150 = (f32[3,128,128]{2,1,0:T(8,128)}, f32[128,128]{1,0:T(8,128)}) custom-call(bf16[16,512,128]{2,1,0:T(8,128)(2,1)} %copy-done), custom_call_target="tpu_custom_call" | custom-call | flops 1048576 | bytes 2097152 | tf_op jit(solution)/shard_map/pallas_call | solution.py:424
  (119 shorter events, 42.4 us)
Async XLA Ops:
  0.6 12.5 %copy-start.27 = (s32[128,2]{0,1:T(2,128)S(1)}, s32[128,2]{0,1:T(2,128)}, u32[]{:S(2)}) copy-start(s32[128,2]{0,1:T(2,128)} %param.18) | copy-start | bytes 3076
  1.8 8.0 %collective-permute-start.1 = (bf16[64,2048]{1,0:T(8,128)(2,1)S(1)}, bf16[64,2048]{1,0:T(8,128)(2,1)S(1)}, u32[]{:S(2)}, u32[]{:S(2)}) collective-permute-start(bf16[64,2048]{1,0:T(8,128)(2,1)S(1)} %get-tuple-element.96), channel_id=1, source_target_pairs={{0,4},{1,5},{2,6},{3,7},{4,0},{5,1},{6,2},{7,3},{8,12},{9,13},{10,... | collective-permute-start | bytes 786440 | tf_op jit(solution)/shard_map/ppermute | solution.py:498
  3.5 9.0 %collective-permute-start.2 = (bf16[64,2048]{1,0:T(8,128)(2,1)S(1)}, bf16[64,2048]{1,0:T(8,128)(2,1)S(1)}, u32[]{:S(2)}, u32[]{:S(2)}) collective-permute-start(bf16[64,2048]{1,0:T(8,128)(2,1)S(1)} %get-tuple-element.95), channel_id=1, source_target_pairs={{0,5},{1,4},{2,7},{3,6},{4,1},{5,0},{6,3},{7,2},{8,13},{9,12},{10,... | collective-permute-start | bytes 786440 | tf_op jit(solution)/shard_map/ppermute | solution.py:498
  12.5 16.4 %copy-start.8 = (bf16[128,2048]{1,0:T(8,128)(2,1)}, bf16[128,2048]{1,0:T(8,128)(2,1)S(1)}, u32[]{:S(2)}) copy-start(bf16[128,2048]{1,0:T(8,128)(2,1)S(1)} %constant_dynamic-update-slice_fusion.t2) | copy-start | bytes 1572868
  12.5 17.0 %collective-permute-start.8 = (bf16[128,2048]{1,0:T(8,128)(2,1)S(1)}, bf16[128,2048]{1,0:T(8,128)(2,1)S(1)}, u32[]{:S(2)}, u32[]{:S(2)}) collective-permute-start(bf16[128,2048]{1,0:T(8,128)(2,1)S(1)} %copy-done.3), channel_id=1, source_target_pairs={{0,4},{1,5},{2,6},{3,7},{4,0},{5,1},{6,2},{7,3},{8,12},{9,13},{10,... | collective-permute-start | bytes 1572872 | tf_op jit(solution)/shard_map/ppermute | solution.py:498
  16.7 45.8 %all-to-all-start = ((bf16[128,40,128]{2,1,0:T(8,128)(2,1)}), bf16[128,40,128]{2,1,0:T(8,128)(2,1)}, u32[]{:S(2)}, u32[]{:S(2)}) async-start(bf16[128,40,128]{2,1,0:T(8,128)(2,1)} %bitcast.14), calls=%async_computation | async-start | bytes 2621440 | tf_op jit(solution)/shard_map/all_to_all | solution.py:511
  28.8 2.0 collective-permute-start
  28.9 2.6 %collective-permute-start.3 = (bf16[128,2048]{1,0:T(8,128)(2,1)S(1)}, bf16[128,2048]{1,0:T(8,128)(2,1)S(1)}, u32[]{:S(2)}, u32[]{:S(2)}) collective-permute-start(bf16[128,2048]{1,0:T(8,128)(2,1)S(1)} %constant_dynamic-update-slice_fusion.t2), channel_id=1, source_target_pairs={{0,2},{1,3},{2,0},{3,1},{4,6},{5,7},{6,4},{7,5},{8,10},{9,11},{10,... | collective-permute-start | bytes 1572872 | tf_op jit(solution)/shard_map/ppermute | solution.py:498
  29.4 11.8 %collective-permute-start.7 = (bf16[128,2048]{1,0:T(8,128)(2,1)S(1)}, bf16[128,2048]{1,0:T(8,128)(2,1)S(1)}, u32[]{:S(2)}, u32[]{:S(2)}) collective-permute-start(bf16[128,2048]{1,0:T(8,128)(2,1)S(1)} %copy-done.3), channel_id=1, source_target_pairs={{0,2},{1,3},{2,0},{3,1},{4,6},{5,7},{6,4},{7,5},{8,10},{9,11},{10,... | collective-permute-start | bytes 1572872 | tf_op jit(solution)/shard_map/ppermute | solution.py:498
  29.5 15.5 %collective-permute-start.9 = (bf16[128,2048]{1,0:T(8,128)(2,1)S(1)}, bf16[128,2048]{1,0:T(8,128)(2,1)S(1)}, u32[]{:S(2)}, u32[]{:S(2)}) collective-permute-start(bf16[128,2048]{1,0:T(8,128)(2,1)S(1)} %collective-permute-done.8.w2), channel_id=1, source_target_pairs={{0,2},{1,3},{2,0},{3,1},{4,6},{5,7},{6,4},{7,5},{8,10},{9,11},{10,... | collective-permute-start | bytes 1572872 | tf_op jit(solution)/shard_map/ppermute | solution.py:498
  39.3 4.4 %collective-permute-start.6 = (bf16[128,128]{1,0:T(8,128)(2,1)S(1)}, bf16[128,128]{1,0:T(8,128)(2,1)S(1)}, u32[]{:S(2)}, u32[]{:S(2)}) collective-permute-start(bf16[128,128]{1,0:T(8,128)(2,1)S(1)} %get-tuple-element.97), channel_id=1, source_target_pairs={{0,6},{1,7},{2,4},{3,5},{4,2},{5,3},{6,0},{7,1},{8,14},{9,15},{10,... | collective-permute-start | bytes 98312 | tf_op jit(solution)/shard_map/ppermute | solution.py:498
  39.9 5.1 %collective-permute-start.5 = (bf16[128,128]{1,0:T(8,128)(2,1)S(1)}, bf16[128,128]{1,0:T(8,128)(2,1)S(1)}, u32[]{:S(2)}, u32[]{:S(2)}) collective-permute-start(bf16[128,128]{1,0:T(8,128)(2,1)S(1)} %get-tuple-element.98), channel_id=1, source_target_pairs={{0,4},{1,5},{2,6},{3,7},{4,0},{5,1},{6,2},{7,3},{8,12},{9,13},{10,... | collective-permute-start | bytes 98312 | tf_op jit(solution)/shard_map/ppermute | solution.py:498
  41.0 4.0 %collective-permute-start.4 = (bf16[128,128]{1,0:T(8,128)(2,1)S(1)}, bf16[128,128]{1,0:T(8,128)(2,1)S(1)}, u32[]{:S(2)}, u32[]{:S(2)}) collective-permute-start(bf16[128,128]{1,0:T(8,128)(2,1)S(1)} %get-tuple-element.99), channel_id=1, source_target_pairs={{0,2},{1,3},{2,0},{3,1},{4,6},{5,7},{6,4},{7,5},{8,10},{9,11},{10,... | collective-permute-start | bytes 98312 | tf_op jit(solution)/shard_map/ppermute | solution.py:498
  49.0 9.8 %collective-permute-start.10 = (bf16[128,1024]{1,0:T(8,128)(2,1)}, bf16[128,1024]{1,0:T(8,128)(2,1)S(1)}, u32[]{:S(2)}, u32[]{:S(2)}) collective-permute-start(bf16[128,1024]{1,0:T(8,128)(2,1)} %get-tuple-element.53), channel_id=1, source_target_pairs={{0,1},{1,0},{2,3},{3,2},{4,5},{5,4},{6,7},{7,6},{8,9},{9,8},{10,11... | collective-permute-start | bytes 786440 | tf_op jit(solution)/shard_map/ppermute | solution.py:498
  62.5 32.5 %all-to-all-start.1 = ((bf16[128,40,128]{2,1,0:T(8,128)(2,1)}), bf16[128,40,128]{2,1,0:T(8,128)(2,1)S(1)}, u32[]{:S(2)}, u32[]{:S(2)}) async-start(bf16[128,40,128]{2,1,0:T(8,128)(2,1)} %bitcast.17), calls=%async_computation.1 | async-start | bytes 2621440 | tf_op jit(solution)/shard_map/all_to_all | solution.py:511
  72.5 22.4 %collective-permute-start.11 = (bf16[128,1024]{1,0:T(8,128)(2,1)S(1)}, bf16[128,1024]{1,0:T(8,128)(2,1)S(1)}, u32[]{:S(2)}, u32[]{:S(2)}) collective-permute-start(bf16[128,1024]{1,0:T(8,128)(2,1)S(1)} %copy-done.18), channel_id=1, source_target_pairs={{0,1},{1,0},{2,3},{3,2},{4,5},{5,4},{6,7},{7,6},{8,9},{9,8},{10,11... | collective-permute-start | bytes 786440 | tf_op jit(solution)/shard_map/ppermute | solution.py:498
  107.4 31.4 %all-to-all-start.2 = ((bf16[128,40,128]{2,1,0:T(8,128)(2,1)}), bf16[128,40,128]{2,1,0:T(8,128)(2,1)S(1)}, u32[]{:S(2)}, u32[]{:S(2)}) async-start(bf16[128,40,128]{2,1,0:T(8,128)(2,1)} %bitcast.18), calls=%async_computation.2 | async-start | bytes 2621440 | tf_op jit(solution)/shard_map/all_to_all | solution.py:511
  142.6 9.1 %collective-permute-start.12 = (bf16[128,1024]{1,0:T(8,128)(2,1)}, bf16[128,1024]{1,0:T(8,128)(2,1)S(1)}, u32[]{:S(2)}, u32[]{:S(2)}) collective-permute-start(bf16[128,1024]{1,0:T(8,128)(2,1)} %shard_map.143.normed_mine), channel_id=1, source_target_pairs={{0,1},{1,0},{2,3},{3,2},{4,5},{5,4},{6,7},{7,6},{8,9},{9,8},{10,11... | collective-permute-start | bytes 786440 | tf_op jit(solution)/shard_map/ppermute | solution.py:498
  157.4 6.6 %collective-permute-start.23 = (bf16[64,2048]{1,0:T(8,128)(2,1)S(1)}, bf16[64,2048]{1,0:T(8,128)(2,1)S(1)}, u32[]{:S(2)}, u32[]{:S(2)}) collective-permute-start(bf16[64,2048]{1,0:T(8,128)(2,1)S(1)} %get-tuple-element.94), channel_id=1, source_target_pairs={{0,4},{1,5},{2,6},{3,7},{4,0},{5,1},{6,2},{7,3},{8,12},{9,13},{10,... | collective-permute-start | bytes 786440 | tf_op jit(solution)/shard_map/ppermute | solution.py:498
  158.1 7.6 %collective-permute-start.24 = (bf16[64,2048]{1,0:T(8,128)(2,1)S(1)}, bf16[64,2048]{1,0:T(8,128)(2,1)S(1)}, u32[]{:S(2)}, u32[]{:S(2)}) collective-permute-start(bf16[64,2048]{1,0:T(8,128)(2,1)S(1)} %get-tuple-element.93), channel_id=1, source_target_pairs={{0,5},{1,4},{2,7},{3,6},{4,1},{5,0},{6,3},{7,2},{8,13},{9,12},{10,... | collective-permute-start | bytes 786440 | tf_op jit(solution)/shard_map/ppermute | solution.py:498
  159.5 16.9 %collective-permute-start.22 = (bf16[128,2048]{1,0:T(8,128)(2,1)}, bf16[128,2048]{1,0:T(8,128)(2,1)S(1)}, u32[]{:S(2)}, u32[]{:S(2)}) collective-permute-start(bf16[128,2048]{1,0:T(8,128)(2,1)} %get-tuple-element.88.g0), channel_id=1, source_target_pairs={{0,2},{1,3},{2,0},{3,1},{4,6},{5,7},{6,4},{7,5},{8,10},{9,11},{10,... | collective-permute-start | bytes 1572872 | tf_op jit(solution)/shard_map/ppermute | solution.py:498
  165.7 10.7 %collective-permute-start.25 = (bf16[128,2048]{1,0:T(8,128)(2,1)S(1)}, bf16[128,2048]{1,0:T(8,128)(2,1)S(1)}, u32[]{:S(2)}, u32[]{:S(2)}) collective-permute-start(bf16[128,2048]{1,0:T(8,128)(2,1)S(1)} %constant_dynamic-update-slice_fusion.2.g2), channel_id=1, source_target_pairs={{0,2},{1,3},{2,0},{3,1},{4,6},{5,7},{6,4},{7,5},{8,10},{9,11},{10,... | collective-permute-start | bytes 1572872 | tf_op jit(solution)/shard_map/ppermute | solution.py:498
  165.8 2.2 collective-permute-start.13
  166.3 4.0 %collective-permute-start.14 = (bf16[128,128]{1,0:T(8,128)(2,1)S(1)}, bf16[128,128]{1,0:T(8,128)(2,1)S(1)}, u32[]{:S(2)}, u32[]{:S(2)}) collective-permute-start(bf16[128,128]{1,0:T(8,128)(2,1)S(1)} %copy-done.29), channel_id=1, source_target_pairs={{0,4},{1,5},{2,6},{3,7},{4,0},{5,1},{6,2},{7,3},{8,12},{9,13},{10,... | collective-permute-start | bytes 98312 | tf_op jit(solution)/shard_map/ppermute | solution.py:498
  166.6 3.7 %collective-permute-start.15 = (bf16[128,128]{1,0:T(8,128)(2,1)S(1)}, bf16[128,128]{1,0:T(8,128)(2,1)S(1)}, u32[]{:S(2)}, u32[]{:S(2)}) collective-permute-start(bf16[128,128]{1,0:T(8,128)(2,1)S(1)} %copy-done.28), channel_id=1, source_target_pairs={{0,6},{1,7},{2,4},{3,5},{4,2},{5,3},{6,0},{7,1},{8,14},{9,15},{10,... | collective-permute-start | bytes 98312 | tf_op jit(solution)/shard_map/ppermute | solution.py:498
  182.4 43.5 %all-to-all-start.3 = ((bf16[16,512,128]{2,1,0:T(8,128)(2,1)}), bf16[16,512,128]{2,1,0:T(8,128)(2,1)S(1)}, u32[]{:S(2)}, u32[]{:S(2)}) async-start(bf16[16,512,128]{2,1,0:T(8,128)(2,1)} %shard_map.149), calls=%async_computation.3 | async-start | bytes 4194304 | tf_op jit(solution)/shard_map/all_to_all | solution.py:558
  187.2 2.2 collective-permute-start.16
  187.2 2.9 %collective-permute-start.17 = (bf16[128,2048]{1,0:T(8,128)(2,1)}, bf16[128,2048]{1,0:T(8,128)(2,1)S(1)}, u32[]{:S(2)}, u32[]{:S(2)}) collective-permute-start(bf16[128,2048]{1,0:T(8,128)(2,1)} %get-tuple-element.80), channel_id=1, source_target_pairs={{0,2},{1,3},{2,0},{3,1},{4,6},{5,7},{6,4},{7,5},{8,10},{9,11},{10,... | collective-permute-start | bytes 1572872 | tf_op jit(solution)/shard_map/ppermute | solution.py:498
  194.0 10.9 %collective-permute-start.18 = (bf16[64,2048]{1,0:T(8,128)(2,1)}, bf16[64,2048]{1,0:T(8,128)(2,1)S(1)}, u32[]{:S(2)}, u32[]{:S(2)}) collective-permute-start(bf16[64,2048]{1,0:T(8,128)(2,1)} %get-tuple-element.82), channel_id=1, source_target_pairs={{0,1},{1,0},{2,3},{3,2},{4,5},{5,4},{6,7},{7,6},{8,9},{9,8},{10,11... | collective-permute-start | bytes 786440 | tf_op jit(solution)/shard_map/ppermute | solution.py:498
  196.0 12.2 %collective-permute-start.19 = (bf16[64,2048]{1,0:T(8,128)(2,1)}, bf16[64,2048]{1,0:T(8,128)(2,1)S(1)}, u32[]{:S(2)}, u32[]{:S(2)}) collective-permute-start(bf16[64,2048]{1,0:T(8,128)(2,1)} %get-tuple-element.83), channel_id=1, source_target_pairs={{0,4},{1,5},{2,6},{3,7},{4,0},{5,1},{6,2},{7,3},{8,12},{9,13},{10,... | collective-permute-start | bytes 786440 | tf_op jit(solution)/shard_map/ppermute | solution.py:498
  196.0 13.7 %collective-permute-start.20 = (bf16[64,2048]{1,0:T(8,128)(2,1)}, bf16[64,2048]{1,0:T(8,128)(2,1)S(1)}, u32[]{:S(2)}, u32[]{:S(2)}) collective-permute-start(bf16[64,2048]{1,0:T(8,128)(2,1)} %get-tuple-element.84), channel_id=1, source_target_pairs={{0,5},{1,4},{2,7},{3,6},{4,1},{5,0},{6,3},{7,2},{8,13},{9,12},{10,... | collective-permute-start | bytes 786440 | tf_op jit(solution)/shard_map/ppermute | solution.py:498
  213.3 9.9 %collective-permute-start.21 = (bf16[64,2048]{1,0:T(8,128)(2,1)}, bf16[64,2048]{1,0:T(8,128)(2,1)S(1)}, u32[]{:S(2)}, u32[]{:S(2)}) collective-permute-start(bf16[64,2048]{1,0:T(8,128)(2,1)} %shard_map.147.mine), channel_id=1, source_target_pairs={{0,1},{1,0},{2,3},{3,2},{4,5},{5,4},{6,7},{7,6},{8,9},{9,8},{10,11... | collective-permute-start | bytes 786440 | tf_op jit(solution)/shard_map/ppermute | solution.py:498
  (32 other events, 123.5 us)
where the time goes:
time: 231 us; the launch traced here: 230 us
  waiting for transfers between devices  91.7 us (40%)
  Pallas kernels  61.3 us (27%)
  starting transfers between devices  60.3 us (26%)
  local copies, waits for them, and re-layouts  14.9 us (6%)
    ppermute x26, waiting for transfers between devices, swap(): return lax.ppermute(x, HG, [(i, i ^ flip) for i in range(8)])  77.6 us
    all_to_all x3, starting transfers between devices, exchange(): return lax.all_to_all(tiles, ALL, 0, 0, tiled=True).reshape(-1, 128)  31.3 us
    ppermute x26, starting transfers between devices, swap(): return lax.ppermute(x, HG, [(i, i ^ flip) for i in range(8)])  24.2 us
    all_to_all x3, waiting for transfers between devices, exchange(): return lax.all_to_all(tiles, ALL, 0, 0, tiled=True).reshape(-1, 128)  14.1 us
    pallas_call x1, Pallas kernels, experts_forward(): call(expert_kernel, (shaped((2 * tiles, 128), BF), row, row, unit, unit,...  11.4 us
    unnamed x71, local copies, waits for them, and re-layouts  11.2 us
    pallas_call x1, Pallas kernels, expert_grads(): pl.pallas_call(expert_grads_kernel, out_shape=(shaped((1, 2, inner, width...  7.99 us
    pallas_call x1, Pallas kernels, attention(): call(attention_kernel, (head, head, head, shaped((length, length), F32),...  5.49 us
  transfers between devices with their start and end apart: 30, of which 20 were waited for; matrix products, arithmetic and copies ran while one was open for 1% of the time, Pallas kernels for 16%

commit v1 on v0

--- a/solution.py
+++ b/solution.py
@@ -79,10 +79,16 @@
     return slot == targets[0], slot == targets[1]
 
 
-def attention_kernel(me, t0, t1, t2, t3, gain, w, query, key, value, chances, mixed, normed):
+def attention_kernel(me, t0, t1, t2, t3, gain, w, query, key, value, chances, m0, m1, m2, m3, normed, held, sems):
     rows = t0.shape[0]
-    for k, t in enumerate((t0, t1, t2, t3)):
-        values = t[...].astype(F32)
+    copies = [
+        pltpu.make_async_copy(t, held.at[k], sems.at[k]) for k, t in enumerate((t0, t1, t2, t3))
+    ]
+    for copy in copies:
+        copy.start()
+    for k, copy in enumerate(copies):
+        copy.wait()
+        values = held[k].astype(F32)
         normed[k * rows : (k + 1) * rows, :] = (values * inverse_rms(values) * gain[...]).astype(BF)
     weights = jnp.concatenate([w[0], w[1], w[2]], axis=1)
     proj = dot(normed[...], weights).astype(BF)
@@ -100,7 +106,9 @@
     powered = jnp.exp(scores - jnp.max(scores, axis=-1, keepdims=True))
     probs = powered / jnp.sum(powered, axis=-1, keepdims=True)
     chances[...] = probs
-    mixed[...] = dot(probs.astype(BF), v).astype(BF)
+    mixed = dot(probs.astype(BF), v).astype(BF)
+    for k, m in enumerate((m0, m1, m2, m3)):
+        m[...] = mixed[k * rows : (k + 1) * rows]
 
 
 def attention(me, blocks, gain, w_qkv):
@@ -109,8 +117,11 @@
     head = shaped((length, HD), BF)
     return call(
         attention_kernel,
-        (head, head, head, shaped((length, length), F32), head, shaped((length, width), BF)),
-        [SMEM] + [VMEM] * 6,
+        (head, head, head, shaped((length, length), F32))
+        + (shaped((rows, HD), BF),) * 4
+        + (shaped((length, width), BF),),
+        [SMEM] + [HBM] * 4 + [VMEM] * 2,
+        [pltpu.VMEM((4, rows, width), BF), pltpu.SemaphoreType.DMA((4,))],
         flops=2 * length * (3 * width + 2 * length) * HD,
         moved=2 * length * width * 2 + 3 * width * HD * 2 + length * length * 4,
     )(me, *blocks, gain, w_qkv)
@@ -151,7 +162,7 @@
         keepdims=True,
     )
     picker = (first | second).astype(BF)
-    chosen = jnp.where(me[1] == 0, grad_out[:, :half], grad_out[:, half:])
+    chosen = grad_out[:, pl.ds(pl.multiple_of(me[1] * half, half), half)]
     spread(scratch, dot(picker, chosen) * scale)
     tiles = scratch[...].astype(BF)
     count = tiles.shape[0]
@@ -164,7 +175,7 @@
     slots = CAP * sent.shape[0] // (2 * CAP * half // 128)
     first, second = pick_matrix(ids_t, ids, slots)
     picker = (first | second).astype(BF)
-    chosen = jnp.where(me[1] == 0, tokens[:, :half], tokens[:, half:]).astype(F32)
+    chosen = tokens[:, pl.ds(pl.multiple_of(me[1] * half, half), half)].astype(F32)
     rows = (chosen + (mine[...] + other[...].astype(F32))).astype(BF)
     hidden[...] = rows
     spread(scratch, dot(picker, rows))
@@ -210,28 +221,48 @@
     return jnp.concatenate(pieces, axis=1)
 
 
+def early_kernel(got_grads, w_down, in_grads, upstream, scratch, down_ref, sem):
+    copy = pltpu.make_async_copy(w_down.at[0], down_ref, sem)
+    copy.start()
+    slots, width = in_grads.shape
+    in_grads[...] = gathered(scratch, got_grads, slots, width).astype(BF)
+    copy.wait()
+    upstream[...] = dot(in_grads[...], down_ref[...], ((1,), (1,)))
+
+
+def experts_early(got_grads, w_down):
+    inner, width = w_down.shape[1:]
+    tiles = got_grads.shape[0] // 2
+    slots = tiles * 256 // width
+    return call(
+        early_kernel,
+        (shaped((slots, width), BF), shaped((slots, inner), F32)),
+        [VMEM, HBM],
+        [pltpu.VMEM((tiles, 128), F32), pltpu.VMEM((inner, width), BF), pltpu.SemaphoreType.DMA],
+        flops=2 * slots * width * inner,
+        moved=2 * width * inner,
+    )(got_grads, w_down)
+
+
 def expert_kernel(
-    got_hidden, got_grads, gain, w_pair, w_down, sent, in_rows, in_grads, product, gate_grad,
-    up_grad, scratch, pair_ref, down_ref, sems
+    got_hidden, upstream_ref, gain, w_pair, sent, in_rows, product, gate_grad, up_grad, scratch,
+    pair_ref, sems
 ):
     copies = [
         pltpu.make_async_copy(w_pair.at[0, 0], pair_ref.at[0], sems.at[0]),
         pltpu.make_async_copy(w_pair.at[0, 1], pair_ref.at[1], sems.at[1]),
-        pltpu.make_async_copy(w_down.at[0], down_ref, sems.at[2]),
     ]
     for copy in copies:
         copy.start()
     slots, width = in_rows.shape
     values = gathered(scratch, got_hidden, slots, width)
     in_rows[...] = (values * inverse_rms(values) * gain[...]).astype(BF)
-    in_grads[...] = gathered(scratch, got_grads, slots, width).astype(BF)
     rows = in_rows[...]
     copies[0].wait()
     gate_pre = dot(rows, pair_ref[0], ((1,), (1,)))
     copies[1].wait()
     up_pre = dot(rows, pair_ref[1], ((1,), (1,)))
-    copies[2].wait()
-    upstream = dot(in_grads[...], down_ref[...], ((1,), (1,)))
+    upstream = upstream_ref[...]
     sigma = 1.0 / (1.0 + jnp.exp(-gate_pre))
     active = gate_pre * sigma
     product[...] = (active * up_pre).astype(BF)
@@ -248,24 +279,23 @@
         sent[g * tiles : (g + 1) * tiles, :] = scratch[...].astype(BF)
 
 
-def experts_forward(got_hidden, got_grads, gain, w_pair, w_down):
+def experts_forward(got_hidden, upstream, gain, w_pair):
     inner, width = w_pair.shape[2:]
     tiles = got_hidden.shape[0] // 2
     slots = tiles * 256 // width
     row, unit = shaped((slots, width), BF), shaped((slots, inner), BF)
     return call(
         expert_kernel,
-        (shaped((2 * tiles, 128), BF), row, row, unit, unit, unit),
-        [VMEM] * 3 + [HBM] * 2,
+        (shaped((2 * tiles, 128), BF), row, unit, unit, unit),
+        [VMEM] * 3 + [HBM],
         [
             pltpu.VMEM((tiles, 128), F32),
             pltpu.VMEM((2, inner, width), BF),
-            pltpu.VMEM((inner, width), BF),
-            pltpu.SemaphoreType.DMA((3,)),
+            pltpu.SemaphoreType.DMA((2,)),
         ],
-        flops=10 * slots * width * inner,
-        moved=6 * width * inner,
-    )(got_hidden, got_grads, gain, w_pair, w_down)
+        flops=8 * slots * width * inner,
+        moved=4 * width * inner,
+    )(got_hidden, upstream, gain, w_pair)
 
 
 def expert_grads_kernel(in_rows, in_grads, product, gate_grad, up_grad, pair, down):
@@ -326,7 +356,7 @@
 
 def hidden_grad_kernel(
     me, grad_out, hidden_mine, hidden_other, normed_mine, normed_other, gain, w0, w1, w2, w3,
-    grad, rounded, p0, p1, p2, p3
+    grad, rounded, top, bottom, p0, p1, p2, p3
 ):
     first = me[1] == 0
 
@@ -342,6 +372,8 @@
     grad[...] = value
     low = value.astype(BF)
     rounded[...] = low
+    top[...] = low[: top.shape[0]]
+    bottom[...] = low[top.shape[0] :]
     for p, w in ((p0, w0), (p1, w1), (p2, w2), (p3, w3)):
         p[...] = dot(low, w[...], ((1,), (1,))).astype(BF)
 
@@ -351,7 +383,9 @@
     piece = shaped((rows, HD), BF)
     return call(
         hidden_grad_kernel,
-        (shaped((rows, width), F32), shaped((rows, width), BF), piece, piece, piece, piece),
+        (shaped((rows, width), F32), shaped((rows, width), BF))
+        + (shaped((rows // 2, width), BF),) * 2
+        + (piece,) * 4,
         [SMEM] + [VMEM] * 10,
         flops=8 * rows * width * HD,
         moved=8 * HD * width + 10 * rows * width,
@@ -390,12 +424,13 @@
     )(*grads, query, key, value, chances, w_qkv)
 
 
-def weight_kernel(acts, normed, mixed, g0, g1, g2, g3, sent):
+def weight_kernel(acts, normed, m0, m1, m2, m3, g0, g1, g2, g3, sent):
     pieces = sent.shape[0]
     wide = acts.shape[1]
     left = dot(acts[...], normed[...], ((0,), (0,))).astype(BF)
     grads = jnp.concatenate([g0[...], g1[...], g2[...], g3[...]], axis=0)
-    right = dot(mixed[...], grads, ((0,), (0,))).astype(BF)
+    mixed = jnp.concatenate([m0[...], m1[...], m2[...], m3[...]], axis=0)
+    right = dot(mixed, grads, ((0,), (0,))).astype(BF)
     for j in range(pieces):
         sent[j, :wide, :] = left[:, j * 128 : (j + 1) * 128]
         sent[j, wide:, :] = right[:, j * 128 : (j + 1) * 128]
@@ -406,14 +441,22 @@
     return call(
         weight_kernel,
         shaped((pieces, 4 * HD, width // pieces), BF),
-        [VMEM] * 7,
+        [VMEM] * 10,
         flops=8 * length * width * HD,
         moved=4 * length * width + 8 * HD * width,
-    )(acts, normed, mixed, *grads)
-
-
-def weight_sum_kernel(got, qkv, out):
-    total = jnp.sum(got[...].astype(F32), axis=0)
+    )(acts, normed, *mixed, *grads)
+
+
+def weight_sum_kernel(got, qkv, out, held, sems):
+    count = got.shape[0]
+    copies = [pltpu.make_async_copy(got.at[j], held.at[j], sems.at[j]) for j in range(count)]
+    for copy in copies:
+        copy.start()
+    total = None
+    for j, copy in enumerate(copies):
+        copy.wait()
+        term = held[j].astype(F32)
+        total = term if total is None else total + term
     for i in range(3):
         qkv[i] = total[i * HD : (i + 1) * HD, :].T
     out[...] = total[3 * HD :, :]
@@ -424,73 +467,43 @@
     return call(
         weight_sum_kernel,
         (shaped((3, piece, HD), F32), shaped((HD, piece), F32)),
-        [VMEM],
+        [HBM],
+        [pltpu.VMEM(got.shape, BF), pltpu.SemaphoreType.DMA((got.shape[0],))],
         flops=got.size,
         moved=got.size * 2,
     )(got)
 
 
-def split_kernel(me, near, near_in, far, far_in, mine, near_other, far_mine, far_other):
+def split_sums(me, near, near_in, far, far_in):
+    small = near.shape[0] // 2
+
+    def half(x, group):
+        return lax.dynamic_slice_in_dim(x, group * small, small, axis=0)
+
+    near = near + near_in.astype(F32)
+    far = far + far_in.astype(F32)
+    g = me[1]
+    return (
+        half(near, g),
+        half(near, 1 - g).astype(BF),
+        half(far, g).astype(BF),
+        half(far, 1 - g).astype(BF),
+    )
+
+
+def tokens_grad(me, mine, arrived, tokens, grad_hidden, gain):
     small = mine.shape[0]
-    here = near[...] + near_in[...].astype(F32)
-    there = far[...] + far_in[...].astype(F32)
+    upstream = mine + sum(a.astype(F32) for a in arrived)
+    own = lax.dynamic_slice_in_dim(tokens, me[1] * small, small, axis=0).astype(F32)
+    own_grad = lax.dynamic_slice_in_dim(grad_hidden, me[1] * small, small, axis=0)
+    return (own_grad + norm_backward(own, inverse_rms(own), gain, upstream)).astype(BF)
+
+
+def join(me, mine, other):
     first = me[1] == 0
-    mine[...] = jnp.where(first, here[:small], here[small:])
-    near_other[...] = jnp.where(first, here[small:], here[:small]).astype(BF)
-    far_mine[...] = jnp.where(first, there[:small], there[small:]).astype(BF)
-    far_other[...] = jnp.where(first, there[small:], there[:small]).astype(BF)
-
-
-def split_sums(me, near, near_in, far, far_in):
-    rows, width = near.shape
-    low = shaped((rows // 2, width), BF)
-    return call(
-        split_kernel,
-        (shaped((rows // 2, width), F32), low, low, low),
-        [SMEM] + [VMEM] * 4,
-        flops=4 * rows * width,
-        moved=20 * rows * width,
-    )(me, near, near_in, far, far_in)
-
-
-def tokens_kernel(me, mine, a, b, c, tokens, grad_hidden, gain, out):
-    small = mine.shape[0]
-    first = me[1] == 0
-    upstream = (
-        mine[...] + a[...].astype(F32) + b[...].astype(F32) + c[...].astype(F32)
+    return jnp.concatenate(
+        [jnp.where(first, mine, other), jnp.where(first, other, mine)], axis=0
     )
-    values = jnp.where(first, tokens[:small], tokens[small:]).astype(F32)
-    before = jnp.where(first, grad_hidden[:small], grad_hidden[small:])
-    back = norm_backward(values, inverse_rms(values), gain[...], upstream)
-    out[...] = (before + back).astype(BF)
-
-
-def tokens_grad(me, mine, arrived, tokens, grad_hidden, gain):
-    small, width = mine.shape
-    return call(
-        tokens_kernel,
-        shaped((small, width), BF),
-        [SMEM] + [VMEM] * 7,
-        flops=20 * small * width,
-        moved=30 * small * width,
-    )(me, mine, *arrived, tokens, grad_hidden, gain)
-
-
-def join_kernel(me, mine, other, out):
-    small = mine.shape[0]
-    first = me[1] == 0
-    out[:small] = jnp.where(first, mine[...], other[...])
-    out[small:] = jnp.where(first, other[...], mine[...])
-
-
-def join(me, mine, other):
-    small, width = mine.shape
-    return call(
-        join_kernel,
-        shaped((2 * small, width), BF),
-        [SMEM] + [VMEM] * 2,
-        moved=8 * small * width,
-    )(me, mine, other)
 
 
 def swap(x, head_bits, group_bit):
@@ -498,10 +511,9 @@
     return lax.ppermute(x, HG, [(i, i ^ flip) for i in range(8)])
 
 
-def sequence(x):
-    small = x.shape[0] // 2
-    top, bottom = x[:small], x[small:]
-    far = jnp.concatenate([swap(top, 2, 0), swap(bottom, 2, 1)], axis=0)
+def sequence(x, top, bottom):
+    top, bottom = swap(top, 2, 0), swap(bottom, 2, 1)
+    far = jnp.concatenate([top, bottom], axis=0)
     return [x, swap(x, 1, 0), far, swap(far, 1, 0)]
 
 
@@ -522,34 +534,33 @@
     w_pair = w_gate_up.transpose(0, 1, 3, 2)
     ids_t, gates_t = ids.T, gates.T
 
-    blocks = sequence(tokens)
+    blocks = sequence(tokens, tokens[: rows // 2], tokens[rows // 2 :])
     tiles = send_grads(me, ids, ids_t, gates_t, grad_out, experts)
     got_grads = exchange(tiles)
-    w_far, blocks[2] = lax.optimization_barrier((w_attn_out, blocks[2]))
-    w_far = swap(w_far, 2, 0)
+    w_far = swap(w_attn_out, 2, 0)
     weights = [w_attn_out, swap(w_attn_out, 1, 0), w_far, swap(w_far, 1, 0)]
 
-    query, key, value, chances, mixed, normed = attention(me, blocks, gain_attn, w_qkv)
-    heads = [mixed[k * rows : (k + 1) * rows] for k in range(4)]
-    heads = [heads[0]] + [swap(heads[k], k, 0) for k in range(1, 4)]
+    query, key, value, chances, *mixed, normed = attention(me, blocks, gain_attn, w_qkv)
+    heads = [mixed[0]] + [swap(mixed[k], k, 0) for k in range(1, 4)]
     mine, other = project(me, heads, weights)
     other = swap(other, 0, 1)
     hidden, tiles = send_hidden(me, ids, ids_t, tokens, mine, other, experts)
-    tiles, got_grads = lax.optimization_barrier((tiles, got_grads))
+    in_grads, in_upstream = experts_early(got_grads, w_down)
+    tiles, in_grads = lax.optimization_barrier((tiles, in_grads))
+    got_hidden = exchange(tiles)
+    got_hidden, hidden = lax.optimization_barrier((got_hidden, hidden))
     hidden_other = swap(hidden, 0, 1)
-    got_hidden = exchange(tiles)
-    got_hidden, hidden_other = lax.optimization_barrier((got_hidden, hidden_other))
-
-    tiles, *saved = experts_forward(got_hidden, got_grads, gain_ffn, w_pair, w_down)
-    grad_pair, grad_down = expert_grads(*saved)
+
+    tiles, in_rows, *saved = experts_forward(got_hidden, in_upstream, gain_ffn, w_pair)
     got_back = exchange(tiles)
-    got_back, grad_pair, grad_down = lax.optimization_barrier((got_back, grad_pair, grad_down))
+    grad_pair, grad_down = expert_grads(in_rows, in_grads, *saved)
 
     upstream = combine(ids, ids_t, got_back, half)
     halves = (hidden, hidden_other, upstream, swap(upstream, 0, 1))
-    grad_hidden, rounded, *grads = hidden_grad(me, grad_out, halves, gain_ffn, weights)
+    grad_hidden, rounded, top, bottom, *grads = hidden_grad(
+        me, grad_out, halves, gain_ffn, weights)
     grads = [grads[0]] + [swap(grads[k], k, 0) for k in range(1, 4)]
-    all_grads = sequence(rounded)
+    all_grads = sequence(rounded, top, bottom)
 
     acts, near, far, near_out, far_out = attention_back(grads, query, key, value, chances, w_qkv)
     near_in = swap(near_out, 1, 0)

time: 231 us -> 222 us (0.961)
  blocking collectives: 0 us -> 32.2 us
  waiting for transfers between devices: 91.7 us -> 63.2 us
  starting transfers between devices: 60.3 us -> 43.8 us
  other arithmetic: 0.6 us -> 7.37 us
  Pallas kernels: 61.3 us -> 58.8 us
    ppermute x26, waiting for transfers between devices: 77.6 us -> 27.8 us  [swap(): return lax.ppermute(x, HG, [(i, i ^ flip) for i in range(8)])]
    all_to_all x0 -> x1, blocking collectives: none -> 32.2 us  [exchange(): return lax.all_to_all(tiles, ALL, 0, 0, tiled=True).reshape(-1, 128)]
    all_to_all x3 -> x2, starting transfers between devices: 31.3 us -> 14.8 us  [exchange(): return lax.all_to_all(tiles, ALL, 0, 0, tiled=True).reshape(-1, 128)]
    all_to_all x1, waiting for transfers between devices: 0.01 us -> 15.4 us  [body(): got = lax.all_to_all(sent, 'dp', 0, 0, tiled=True)]
    all_to_all x3 -> x2, waiting for transfers between devices: 14.1 us -> 20.1 us  [exchange(): return lax.all_to_all(tiles, ALL, 0, 0, tiled=True).reshape(-1, 128)]
    pallas_call x5 -> x3, Pallas kernels: 24.7 us -> 22 us  [the longest x1 9.92 us: experts_forward(): call(expert_kernel, (shaped((2 * tiles, 128), BF), row, unit, unit, unit)...]
    slice x3 -> x1, local copies, waits for them, and re-layouts: 3.62 us -> 1.07 us  [body(): blocks = sequence(tokens, tokens[:rows // 2], tokens[rows // 2:])]
    unnamed x71 -> x63, local copies, waits for them, and re-layouts: 11.2 us -> 12.2 us
  transfers between devices with their start and end apart: 30 -> 29, of which waited for: 20 -> 9; matrix products, arithmetic and copies ran while one was open for 1% -> 5% of each run, Pallas kernels for 16% -> 18%
where the time goes in v1:
time: 222 us; the launch traced here: 221 us
  waiting for transfers between devices  63.2 us (28%)
  Pallas kernels  58.8 us (26%)
  starting transfers between devices  43.8 us (20%)
  blocking collectives  32.2 us (15%)
  local copies, waits for them, and re-layouts  14.9 us (7%)
  other arithmetic  7.37 us (3%)
    all_to_all x1, blocking collectives, exchange(): return lax.all_to_all(tiles, ALL, 0, 0, tiled=True).reshape(-1, 128)  32.2 us
    ppermute x26, waiting for transfers between devices, swap(): return lax.ppermute(x, HG, [(i, i ^ flip) for i in range(8)])  27.8 us
    ppermute x26, starting transfers between devices, swap(): return lax.ppermute(x, HG, [(i, i ^ flip) for i in range(8)])  23.6 us
    all_to_all x2, waiting for transfers between devices, exchange(): return lax.all_to_all(tiles, ALL, 0, 0, tiled=True).reshape(-1, 128)  20.1 us
    all_to_all x1, waiting for transfers between devices, body(): got = lax.all_to_all(sent, 'dp', 0, 0, tiled=True)  15.4 us
    all_to_all x2, starting transfers between devices, exchange(): return lax.all_to_all(tiles, ALL, 0, 0, tiled=True).reshape(-1, 128)  14.8 us
    unnamed x63, local copies, waits for them, and re-layouts  12.2 us
    pallas_call x1, Pallas kernels, experts_forward(): call(expert_kernel, (shaped((2 * tiles, 128), BF), row, unit, unit, unit)...  9.92 us
  transfers between devices with their start and end apart: 29, of which 9 were waited for; matrix products, arithmetic and copies ran while one was open for 5% of the time, Pallas kernels for 18%

profile of v1, /device:TPU:0, one launch (start us, length us, event | category | flops | bytes accessed | tf_op | source)
XLA Modules:
  0.0 221.5 jit_solution(13769133571718434633)
XLA Ops:
  1.7 1.7 collective-permute-start.1
  3.4 2.1 collective-permute-start.2
  8.1 2.8 %shard_map.140 = bf16[5120,128]{1,0:T(8,128)(2,1)} custom-call(s32[2]{0:T(128)} %pad_add_fusion.me, s32[128,2]{1,0:T(8,128)} %copy.15.ids, s32[2,128]{1,0:T(2,128)} %bitcast.21, f32[2,128]{1,0:T(2,128)} %bitcast.26, bf16[128,2048]{1,0:T(8,128)(2,1)} %grad_out.3), custom_call_target="tpu_custom_call" | custom-call | flops 83886080 | bytes 1310720 | tf_op jit(solution)/shard_map/pallas_call | solution.py:191
  10.9 10.0 %all-to-all-start = ((bf16[128,40,128]{2,1,0:T(8,128)(2,1)}), bf16[128,40,128]{2,1,0:T(8,128)(2,1)S(1)}, u32[]{:S(2)}, u32[]{:S(2)}) async-start(bf16[128,40,128]{2,1,0:T(8,128)(2,1)} %bitcast.15), calls=%async_computation | async-start | bytes 2621440 | tf_op jit(solution)/shard_map/all_to_all | solution.py:523
  23.8 6.8 %shard_map.137 = (bf16[512,128]{1,0:T(8,128)(2,1)}, bf16[512,128]{1,0:T(8,128)(2,1)}, bf16[512,128]{1,0:T(8,128)(2,1)}, f32[512,512]{1,0:T(8,128)}, bf16[128,128...) custom-call(s32[2]{0:T(128)} %pad_add_fusion.me, ...), custom_call_target="tpu_custom_call" | custom-call | flops 939524096 | bytes 6815744 | tf_op jit(solution)/shard_map/pallas_call | solution.py:118
  32.6 4.7 %collective-permute-done.5.m2 = bf16[128,128]{1,0:T(8,128)(2,1)S(1)} collective-permute-done((bf16[128,128]{1,0:T(8,128)(2,1)}, bf16[128,128]{1,0:T(8,128)(2,1)S(1)}, u32[]{:S(2)}, u32[]{:S(2)}) %collective-permute-start.5) | collective-permute-done | bytes 32800 | tf_op jit(solution)/shard_map/ppermute | solution.py:511
  38.1 3.2 %shard_map.138 = (f32[128,1024]{1,0:T(8,128)}, bf16[128,1024]{1,0:T(8,128)(2,1)}) custom-call(s32[2]{0:T(128)} %pad_add_fusion.me, bf16[128,128]{1,0:T(8,128)(2,1)} %get-tuple-element.46.m0, bf16[128,128]{1,0:T(8,128)(2,1)} %copy-done.23, bf16[128,128]{1,0:T(8,128)(2,1)} %copy-done.24, bf16[128,128]{1,0:T(8,128)(2,1)} %copy-done.25, bf16[128,2048]{1,0:T(8,128)(2,1)} %w0.3, ...), custom_call_target="tpu_custom_call" | custom-call | flops 268435456 | bytes 2097152 | tf_op jit(solution)/shard_map/pallas_call | solution.py:146
  41.3 2.7 %collective-permute-start.10 = (bf16[128,1024]{1,0:T(8,128)(2,1)}, bf16[128,1024]{1,0:T(8,128)(2,1)S(1)}, u32[]{:S(2)}, u32[]{:S(2)}) collective-permute-start(bf16[128,1024]{1,0:T(8,128)(2,1)} %get-tuple-element.51), channel_id=1, source_target_pairs={{0,1},{1,0},{2,3},{3,2},{4,5},{5,4},{6,7},{7,6},{8,9},{9,8},{10,11... | collective-permute-start | bytes 786440 | tf_op jit(solution)/shard_map/ppermute | solution.py:511
  45.0 5.3 %shard_map.141 = (bf16[320,2048]{1,0:T(8,128)(2,1)}, f32[320,704]{1,0:T(8,128)}) custom-call(bf16[5120,128]{1,0:T(8,128)(2,1)} %bitcast.14, bf16[1,704,2048]{2,1,0:T(8,128)(2,1)} %w_down.1), custom_call_target="tpu_custom_call" | custom-call | flops 922746880 | bytes 2883584 | tf_op jit(solution)/shard_map/pallas_call | solution.py:237
  52.4 3.0 %shard_map.139 = (bf16[128,1024]{1,0:T(8,128)(2,1)}, bf16[5120,128]{1,0:T(8,128)(2,1)}) custom-call(s32[2]{0:T(128)} %pad_add_fusion.me, s32[128,2]{1,0:T(8,128)} %copy.15.ids, s32[2,128]{1,0:T(2,128)} %bitcast.22, bf16[128,2048]{1,0:T(8,128)(2,1)} %tokens.1, f32[128,1024]{1,0:T(8,128)} %get-tuple-element.50.mine, bf16[128,1024]{1,0:T(8,128)(2,1)} %copy-done.18), custom_call_target="tpu_custom_call" | custom-call | flops 83886080 | bytes 1310720 | tf_op jit(solution)/shard_map/pallas_call | solution.py:204
  55.4 32.2 %all_to_all.20 = bf16[128,40,128]{2,1,0:T(8,128)(2,1)} all-to-all(bf16[128,40,128]{2,1,0:T(8,128)(2,1)} %bitcast.19), channel_id=1, replica_groups=mesh['dp'=16,'head'=4,'group'=2] {'group','dp','head'}, dimensions={0} | all-to-all | bytes 2621440 | tf_op jit(solution)/shard_map/all_to_all | solution.py:523
  87.6 9.9 %shard_map.142 = (bf16[5120,128]{1,0:T(8,128)(2,1)}, bf16[320,2048]{1,0:T(8,128)(2,1)}, bf16[320,704]{1,0:T(8,128)(2,1)}, bf16[320,704]{1,0:T(8,128)(2,1)}, bf16[320,704]{1,0:T(8,128)(2,1)}) custom-call(bf16[5120,128]{1,0:T(8,128)(2,1)} %bitcast.18, f32[320,704]{1,0:T(8,128)} %get-tuple-element.58.upstream_ref, f32[1,2048]{1,0:T(1,128)} %bitcast.24, ...), custom_call_target="tpu_custom_call" | custom-call | flops 3690987520 | bytes 5767168 | tf_op jit(solution)/shard_map/pallas_call | solution.py:287
  97.5 4.8 %all-to-all-start.2 = ((bf16[128,40,128]{2,1,0:T(8,128)(2,1)}), bf16[128,40,128]{2,1,0:T(8,128)(2,1)S(1)}, u32[]{:S(2)}, u32[]{:S(2)}) async-start(bf16[128,40,128]{2,1,0:T(8,128)(2,1)} %bitcast.17), calls=%async_computation.2 | async-start | bytes 2621440 | tf_op jit(solution)/shard_map/all_to_all | solution.py:523
  102.3 2.4 %collective-permute-start.11 = (bf16[128,1024]{1,0:T(8,128)(2,1)S(1)}, bf16[128,1024]{1,0:T(8,128)(2,1)S(1)}, u32[]{:S(2)}, u32[]{:S(2)}) collective-permute-start(bf16[128,1024]{1,0:T(8,128)(2,1)S(1)} %copy-done.19), channel_id=1, source_target_pairs={{0,1},{1,0},{2,3},{3,2},{4,5},{5,4},{6,7},{7,6},{8,9},{9,8},{10,11... | collective-permute-start | bytes 786440 | tf_op jit(solution)/shard_map/ppermute | solution.py:511
  104.7 20.1 %all-to-all-done.2 = bf16[128,40,128]{2,1,0:T(8,128)(2,1)S(1)} async-done(((bf16[128,40,128]{2,1,0:T(8,128)(2,1)}), bf16[128,40,128]{2,1,0:T(8,128)(2,1)S(1)}, u32[]{:S(2)}, u32[]{:S(2)}) %all-to-all-start.2) | async-done | bytes 1310752 | tf_op jit(solution)/shard_map/all_to_all | solution.py:523
  125.8 2.7 %shard_map.143.normed_mine = bf16[128,1024]{1,0:T(8,128)(2,1)} custom-call(s32[128,2]{1,0:T(8,128)} %copy.15.ids, s32[2,128]{1,0:T(2,128)} %bitcast.23, bf16[5120,128]{1,0:T(8,128)(2,1)} %bitcast.16), custom_call_target="tpu_custom_call" | custom-call | flops 83886080 | bytes 1310720 | tf_op jit(solution)/shard_map/pallas_call | solution.py:347
  129.1 8.1 %collective-permute-done.12.normed_other = bf16[128,1024]{1,0:T(8,128)(2,1)S(1)} collective-permute-done((bf16[128,1024]{1,0:T(8,128)(2,1)}, bf16[128,1024]{1,0:T(8,128)(2,1)S(1)}, u32[]{:S(2)}, u32[]{:S(2)}) %collective-permute-start.12) | collective-permute-done | bytes 262176 | tf_op jit(solution)/shard_map/ppermute | solution.py:511
  137.9 4.1 %shard_map.144 = (f32[128,2048]{1,0:T(8,128)}, bf16[128,2048]{1,0:T(8,128)(2,1)}, bf16[64,2048]{1,0:T(8,128)(2,1)}, bf16[64,2048]{1,0:T(8,128)(2,1)}, bf16[128,1...) custom-call(s32[2]{0:T(128)} %pad_add_fusion.me, ...), custom_call_target="tpu_custom_call" | custom-call | flops 268435456 | bytes 4718592 | tf_op jit(solution)/shard_map/pallas_call | solution.py:384
  142.6 1.4 collective-permute-start.14
  144.5 5.2 %collective-permute-done.14.g2 = bf16[128,128]{1,0:T(8,128)(2,1)S(1)} collective-permute-done((bf16[128,128]{1,0:T(8,128)(2,1)}, bf16[128,128]{1,0:T(8,128)(2,1)S(1)}, u32[]{:S(2)}, u32[]{:S(2)}) %collective-permute-start.14) | collective-permute-done | bytes 32800 | tf_op jit(solution)/shard_map/ppermute | solution.py:511
  150.3 5.5 %shard_map.145 = (bf16[512,384]{1,0:T(8,128)(2,1)}, f32[128,2048]{1,0:T(8,128)}, f32[128,2048]{1,0:T(8,128)}, bf16[128,2048]{1,0:T(8,128)(2,1)}, bf16[128,2048]{1,0:T(8,128)(2,1)}) custom-call(bf16[128,128]{1,0:T(8,128)(2,1)} %get-tuple-element.61.g0, bf16[128,128]{1,0:T(8,128)(2,1)} %copy-done.27, bf16[128,128]{1,0:T(8,128)(2,1)} %copy-done.28, ...), custom_call_target="tpu_custom_call" | custom-call | flops 1073741824 | bytes 5767168 | tf_op jit(solution)/shard_map/pallas_call | solution.py:418
  156.0 2.0 collective-permute-start.24
  158.8 7.0 %collective-permute-done.24 = bf16[64,2048]{1,0:T(8,128)(2,1)S(1)} collective-permute-done((bf16[64,2048]{1,0:T(8,128)(2,1)S(1)}, bf16[64,2048]{1,0:T(8,128)(2,1)S(1)}, u32[]{:S(2)}, u32[]{:S(2)}) %collective-permute-start.24) | collective-permute-done | bytes 262176 | tf_op jit(solution)/shard_map/ppermute | solution.py:511
  168.9 1.9 collective-permute-start.20
  172.7 2.8 %collective-permute-start.17 = (bf16[64,2048]{1,0:T(8,128)(2,1)}, bf16[64,2048]{1,0:T(8,128)(2,1)S(1)}, u32[]{:S(2)}, u32[]{:S(2)}) collective-permute-start(bf16[64,2048]{1,0:T(8,128)(2,1)} %dynamic-slice_convert_fusion.2), channel_id=1, source_target_pairs={{0,1},{1,0},{2,3},{3,2},{4,5},{5,4},{6,7},{7,6},{8,9},{9,8},{10,11... | collective-permute-start | bytes 786440 | tf_op jit(solution)/shard_map/ppermute | solution.py:511
  177.1 4.9 %shard_map.146 = bf16[16,512,128]{2,1,0:T(8,128)(2,1)} custom-call(bf16[512,384]{1,0:T(8,128)(2,1)} %get-tuple-element.73.acts, bf16[512,2048]{1,0:T(8,128)(2,1)} %get-tuple-element.74.normed, bf16[128,128]{1,0:T(8,128)(2,1)} %get-tuple-element.46.m0, bf16[128,128]{1,0:T(8,128)(2,1)} %get-tuple-element.47.m1, bf16[128,128]{1,0:T(8,128)(2,1)} %get-tuple-element.48.m2, ...), custom_call_target="tpu_custom_call" | custom-call | flops 1073741824 | bytes 6291456 | tf_op jit(solution)/shard_map/pallas_call | solution.py:441
  182.1 5.4 %all-to-all-start.3 = ((bf16[16,512,128]{2,1,0:T(8,128)(2,1)}), bf16[16,512,128]{2,1,0:T(8,128)(2,1)S(1)}, u32[]{:S(2)}, u32[]{:S(2)}) async-start(bf16[16,512,128]{2,1,0:T(8,128)(2,1)} %shard_map.146), calls=%async_computation.3 | async-start | bytes 4194304 | tf_op jit(solution)/shard_map/all_to_all | solution.py:569
  187.5 1.4 fusion.2
  189.0 2.0 fusion.6
  191.9 8.0 %shard_map.148 = (bf16[1,2,704,2048]{3,2,1,0:T(8,128)(2,1)}, bf16[1,704,2048]{2,1,0:T(8,128)(2,1)}) custom-call(bf16[320,2048]{1,0:T(8,128)(2,1)} %get-tuple-element.80.in_rows, bf16[320,2048]{1,0:T(8,128)(2,1)} %get-tuple-element.81.in_grads, bf16[320,704]{1,0:T(8,128)(2,1)} %get-tuple-element.82.product, bf16[320,704]{1,0:T(8,128)(2,1)} %get-tuple-element.83.gate_grad, ...), custom_call_target="tpu_custom_call" | custom-call | flops 2768240640 | bytes 8650752 | tf_op jit(solution)/shard_map/pallas_call | solution.py:314
  202.0 15.4 %all-to-all-done.3.got = bf16[16,512,128]{2,1,0:T(8,128)(2,1)S(1)} async-done(((bf16[16,512,128]{2,1,0:T(8,128)(2,1)}), bf16[16,512,128]{2,1,0:T(8,128)(2,1)S(1)}, u32[]{:S(2)}, u32[]{:S(2)}) %all-to-all-start.3) | async-done | bytes 2097184 | tf_op jit(solution)/shard_map/all_to_all | solution.py:569
  218.7 2.5 %shard_map.147 = (f32[3,128,128]{2,1,0:T(8,128)}, f32[128,128]{1,0:T(8,128)}) custom-call(bf16[16,512,128]{2,1,0:T(8,128)(2,1)} %copy-done.1), custom_call_target="tpu_custom_call" | custom-call | flops 1048576 | bytes 2097152 | tf_op jit(solution)/shard_map/pallas_call | solution.py:467
  (117 shorter events, 28.3 us)
Async XLA Ops:
  1.7 19.2 %collective-permute-start.1 = (bf16[64,2048]{1,0:T(8,128)(2,1)S(1)}, bf16[64,2048]{1,0:T(8,128)(2,1)S(1)}, u32[]{:S(2)}, u32[]{:S(2)}) collective-permute-start(bf16[64,2048]{1,0:T(8,128)(2,1)S(1)} %get-tuple-element.92), channel_id=1, source_target_pairs={{0,4},{1,5},{2,6},{3,7},{4,0},{5,1},{6,2},{7,3},{8,12},{9,13},{10,... | collective-permute-start | bytes 786440 | tf_op jit(solution)/shard_map/ppermute | solution.py:511
  3.4 18.4 %collective-permute-start = (bf16[128,2048]{1,0:T(8,128)(2,1)}, bf16[128,2048]{1,0:T(8,128)(2,1)}, u32[]{:S(2)}, u32[]{:S(2)}) collective-permute-start(bf16[128,2048]{1,0:T(8,128)(2,1)} %tokens.1), channel_id=1, source_target_pairs={{0,2},{1,3},{2,0},{3,1},{4,6},{5,7},{6,4},{7,5},{8,10},{9,11},{10,... | collective-permute-start | bytes 1572872 | tf_op jit(solution)/shard_map/ppermute | solution.py:511
  3.4 17.6 %collective-permute-start.2 = (bf16[64,2048]{1,0:T(8,128)(2,1)S(1)}, bf16[64,2048]{1,0:T(8,128)(2,1)S(1)}, u32[]{:S(2)}, u32[]{:S(2)}) collective-permute-start(bf16[64,2048]{1,0:T(8,128)(2,1)S(1)} %get-tuple-element.91), channel_id=1, source_target_pairs={{0,5},{1,4},{2,7},{3,6},{4,1},{5,0},{6,3},{7,2},{8,13},{9,12},{10,... | collective-permute-start | bytes 786440 | tf_op jit(solution)/shard_map/ppermute | solution.py:511
  5.5 16.1 %collective-permute-start.8 = (bf16[128,2048]{1,0:T(8,128)(2,1)}, bf16[128,2048]{1,0:T(8,128)(2,1)S(1)}, u32[]{:S(2)}, u32[]{:S(2)}) collective-permute-start(bf16[128,2048]{1,0:T(8,128)(2,1)} %w0.3), channel_id=1, source_target_pairs={{0,4},{1,5},{2,6},{3,7},{4,0},{5,1},{6,2},{7,3},{8,12},{9,13},{10,... | collective-permute-start | bytes 1572872 | tf_op jit(solution)/shard_map/ppermute | solution.py:511
  10.9 10.2 %copy-start.6 = (bf16[128,2048]{1,0:T(8,128)(2,1)S(1)}, bf16[128,2048]{1,0:T(8,128)(2,1)}, u32[]{:S(2)}) copy-start(bf16[128,2048]{1,0:T(8,128)(2,1)} %w0.3) | copy-start | bytes 1572868
  10.9 33.1 %all-to-all-start = ((bf16[128,40,128]{2,1,0:T(8,128)(2,1)}), bf16[128,40,128]{2,1,0:T(8,128)(2,1)S(1)}, u32[]{:S(2)}, u32[]{:S(2)}) async-start(bf16[128,40,128]{2,1,0:T(8,128)(2,1)} %bitcast.15), calls=%async_computation | async-start | bytes 2621440 | tf_op jit(solution)/shard_map/all_to_all | solution.py:523
  21.0 2.0 collective-permute-start.3
  21.1 11.5 %collective-permute-start.7 = (bf16[128,2048]{1,0:T(8,128)(2,1)S(1)}, bf16[128,2048]{1,0:T(8,128)(2,1)S(1)}, u32[]{:S(2)}, u32[]{:S(2)}) collective-permute-start(bf16[128,2048]{1,0:T(8,128)(2,1)S(1)} %copy-done.6), channel_id=1, source_target_pairs={{0,2},{1,3},{2,0},{3,1},{4,6},{5,7},{6,4},{7,5},{8,10},{9,11},{10,... | collective-permute-start | bytes 1572872 | tf_op jit(solution)/shard_map/ppermute | solution.py:511
  21.8 8.8 %copy-start.7 = (bf16[128,2048]{1,0:T(8,128)(2,1)}, bf16[128,2048]{1,0:T(8,128)(2,1)S(1)}, u32[]{:S(2)}) copy-start(bf16[128,2048]{1,0:T(8,128)(2,1)S(1)} %collective-permute-done.8.w2) | copy-start | bytes 1572868
  21.8 15.5 %collective-permute-start.9 = (bf16[128,2048]{1,0:T(8,128)(2,1)S(1)}, bf16[128,2048]{1,0:T(8,128)(2,1)S(1)}, u32[]{:S(2)}, u32[]{:S(2)}) collective-permute-start(bf16[128,2048]{1,0:T(8,128)(2,1)S(1)} %collective-permute-done.8.w2), channel_id=1, source_target_pairs={{0,2},{1,3},{2,0},{3,1},{4,6},{5,7},{6,4},{7,5},{8,10},{9,11},{10,... | collective-permute-start | bytes 1572872 | tf_op jit(solution)/shard_map/ppermute | solution.py:511
  30.6 1.9 collective-permute-start.4
  30.8 6.4 %collective-permute-start.5 = (bf16[128,128]{1,0:T(8,128)(2,1)}, bf16[128,128]{1,0:T(8,128)(2,1)S(1)}, u32[]{:S(2)}, u32[]{:S(2)}) collective-permute-start(bf16[128,128]{1,0:T(8,128)(2,1)} %get-tuple-element.48.m2), channel_id=1, source_target_pairs={{0,4},{1,5},{2,6},{3,7},{4,0},{5,1},{6,2},{7,3},{8,12},{9,13},{10,... | collective-permute-start | bytes 98312 | tf_op jit(solution)/shard_map/ppermute | solution.py:511
  31.8 5.5 %collective-permute-start.6 = (bf16[128,128]{1,0:T(8,128)(2,1)}, bf16[128,128]{1,0:T(8,128)(2,1)S(1)}, u32[]{:S(2)}, u32[]{:S(2)}) collective-permute-start(bf16[128,128]{1,0:T(8,128)(2,1)} %get-tuple-element.49.m3), channel_id=1, source_target_pairs={{0,6},{1,7},{2,4},{3,5},{4,2},{5,3},{6,0},{7,1},{8,14},{9,15},{10,... | collective-permute-start | bytes 98312 | tf_op jit(solution)/shard_map/ppermute | solution.py:511
  41.3 10.4 %collective-permute-start.10 = (bf16[128,1024]{1,0:T(8,128)(2,1)}, bf16[128,1024]{1,0:T(8,128)(2,1)S(1)}, u32[]{:S(2)}, u32[]{:S(2)}) collective-permute-start(bf16[128,1024]{1,0:T(8,128)(2,1)} %get-tuple-element.51), channel_id=1, source_target_pairs={{0,1},{1,0},{2,3},{3,2},{4,5},{5,4},{6,7},{7,6},{8,9},{9,8},{10,11... | collective-permute-start | bytes 786440 | tf_op jit(solution)/shard_map/ppermute | solution.py:511
  97.5 27.3 %all-to-all-start.2 = ((bf16[128,40,128]{2,1,0:T(8,128)(2,1)}), bf16[128,40,128]{2,1,0:T(8,128)(2,1)S(1)}, u32[]{:S(2)}, u32[]{:S(2)}) async-start(bf16[128,40,128]{2,1,0:T(8,128)(2,1)} %bitcast.17), calls=%async_computation.2 | async-start | bytes 2621440 | tf_op jit(solution)/shard_map/all_to_all | solution.py:523
  102.3 26.8 %collective-permute-start.11 = (bf16[128,1024]{1,0:T(8,128)(2,1)S(1)}, bf16[128,1024]{1,0:T(8,128)(2,1)S(1)}, u32[]{:S(2)}, u32[]{:S(2)}) collective-permute-start(bf16[128,1024]{1,0:T(8,128)(2,1)S(1)} %copy-done.19), channel_id=1, source_target_pairs={{0,1},{1,0},{2,3},{3,2},{4,5},{5,4},{6,7},{7,6},{8,9},{9,8},{10,11... | collective-permute-start | bytes 786440 | tf_op jit(solution)/shard_map/ppermute | solution.py:511
  128.6 8.6 %collective-permute-start.12 = (bf16[128,1024]{1,0:T(8,128)(2,1)}, bf16[128,1024]{1,0:T(8,128)(2,1)S(1)}, u32[]{:S(2)}, u32[]{:S(2)}) collective-permute-start(bf16[128,1024]{1,0:T(8,128)(2,1)} %shard_map.143.normed_mine), channel_id=1, source_target_pairs={{0,1},{1,0},{2,3},{3,2},{4,5},{5,4},{6,7},{7,6},{8,9},{9,8},{10,11... | collective-permute-start | bytes 786440 | tf_op jit(solution)/shard_map/ppermute | solution.py:511
  142.0 16.8 %collective-permute-start.23 = (bf16[64,2048]{1,0:T(8,128)(2,1)}, bf16[64,2048]{1,0:T(8,128)(2,1)S(1)}, u32[]{:S(2)}, u32[]{:S(2)}) collective-permute-start(bf16[64,2048]{1,0:T(8,128)(2,1)} %get-tuple-element.76), channel_id=1, source_target_pairs={{0,4},{1,5},{2,6},{3,7},{4,0},{5,1},{6,2},{7,3},{8,12},{9,13},{10,... | collective-permute-start | bytes 786440 | tf_op jit(solution)/shard_map/ppermute | solution.py:511
  142.6 1.9 collective-permute-start.13
  142.6 7.0 %collective-permute-start.14 = (bf16[128,128]{1,0:T(8,128)(2,1)}, bf16[128,128]{1,0:T(8,128)(2,1)S(1)}, u32[]{:S(2)}, u32[]{:S(2)}) collective-permute-start(bf16[128,128]{1,0:T(8,128)(2,1)} %get-tuple-element.63), channel_id=1, source_target_pairs={{0,4},{1,5},{2,6},{3,7},{4,0},{5,1},{6,2},{7,3},{8,12},{9,13},{10,... | collective-permute-start | bytes 98312 | tf_op jit(solution)/shard_map/ppermute | solution.py:511
  144.1 5.6 %collective-permute-start.15 = (bf16[128,128]{1,0:T(8,128)(2,1)}, bf16[128,128]{1,0:T(8,128)(2,1)S(1)}, u32[]{:S(2)}, u32[]{:S(2)}) collective-permute-start(bf16[128,128]{1,0:T(8,128)(2,1)} %get-tuple-element.64), channel_id=1, source_target_pairs={{0,6},{1,7},{2,4},{3,5},{4,2},{5,3},{6,0},{7,1},{8,14},{9,15},{10,... | collective-permute-start | bytes 98312 | tf_op jit(solution)/shard_map/ppermute | solution.py:511
  155.9 10.9 %copy-start.13 = (f32[128,2048]{1,0:T(8,128)S(1)}, f32[128,2048]{1,0:T(8,128)}, u32[]{:S(2)}) copy-start(f32[128,2048]{1,0:T(8,128)} %get-tuple-element.71) | copy-start | bytes 3145732
  155.9 10.1 %collective-permute-start.18 = (bf16[128,2048]{1,0:T(8,128)(2,1)}, bf16[128,2048]{1,0:T(8,128)(2,1)S(1)}, u32[]{:S(2)}, u32[]{:S(2)}) collective-permute-start(bf16[128,2048]{1,0:T(8,128)(2,1)} %get-tuple-element.72), channel_id=1, source_target_pairs={{0,2},{1,3},{2,0},{3,1},{4,6},{5,7},{6,4},{7,5},{8,10},{9,11},{10,... | collective-permute-start | bytes 1572872 | tf_op jit(solution)/shard_map/ppermute | solution.py:511
  156.0 9.8 %collective-permute-start.24 = (bf16[64,2048]{1,0:T(8,128)(2,1)S(1)}, bf16[64,2048]{1,0:T(8,128)(2,1)S(1)}, u32[]{:S(2)}, u32[]{:S(2)}) collective-permute-start(bf16[64,2048]{1,0:T(8,128)(2,1)S(1)} %copy-done.26), channel_id=1, source_target_pairs={{0,5},{1,4},{2,7},{3,6},{4,1},{5,0},{6,3},{7,2},{8,13},{9,12},{10,... | collective-permute-start | bytes 786440 | tf_op jit(solution)/shard_map/ppermute | solution.py:511
  158.2 17.3 %collective-permute-start.22 = (bf16[128,2048]{1,0:T(8,128)(2,1)}, bf16[128,2048]{1,0:T(8,128)(2,1)S(1)}, u32[]{:S(2)}, u32[]{:S(2)}) collective-permute-start(bf16[128,2048]{1,0:T(8,128)(2,1)} %get-tuple-element.75.g0), channel_id=1, source_target_pairs={{0,2},{1,3},{2,0},{3,1},{4,6},{5,7},{6,4},{7,5},{8,10},{9,11},{10,... | collective-permute-start | bytes 1572872 | tf_op jit(solution)/shard_map/ppermute | solution.py:511
  158.3 12.5 %collective-permute-start.16 = (bf16[128,2048]{1,0:T(8,128)(2,1)}, bf16[128,2048]{1,0:T(8,128)(2,1)S(1)}, u32[]{:S(2)}, u32[]{:S(2)}) collective-permute-start(bf16[128,2048]{1,0:T(8,128)(2,1)} %get-tuple-element.70), channel_id=1, source_target_pairs={{0,2},{1,3},{2,0},{3,1},{4,6},{5,7},{6,4},{7,5},{8,10},{9,11},{10,... | collective-permute-start | bytes 1572872 | tf_op jit(solution)/shard_map/ppermute | solution.py:511
  165.8 9.7 %collective-permute-start.25 = (bf16[128,2048]{1,0:T(8,128)(2,1)S(1)}, bf16[128,2048]{1,0:T(8,128)(2,1)S(1)}, u32[]{:S(2)}, u32[]{:S(2)}) collective-permute-start(bf16[128,2048]{1,0:T(8,128)(2,1)S(1)} %constant_dynamic-update-slice_fusion.2.g2), channel_id=1, source_target_pairs={{0,2},{1,3},{2,0},{3,1},{4,6},{5,7},{6,4},{7,5},{8,10},{9,11},{10,... | collective-permute-start | bytes 1572872 | tf_op jit(solution)/shard_map/ppermute | solution.py:511
  168.9 18.5 %collective-permute-start.20 = (bf16[64,2048]{1,0:T(8,128)(2,1)}, bf16[64,2048]{1,0:T(8,128)(2,1)S(1)}, u32[]{:S(2)}, u32[]{:S(2)}) collective-permute-start(bf16[64,2048]{1,0:T(8,128)(2,1)} %get-tuple-element.90), channel_id=1, source_target_pairs={{0,5},{1,4},{2,7},{3,6},{4,1},{5,0},{6,3},{7,2},{8,13},{9,12},{10,... | collective-permute-start | bytes 786440 | tf_op jit(solution)/shard_map/ppermute | solution.py:511
  170.8 16.7 %collective-permute-start.19 = (bf16[64,2048]{1,0:T(8,128)(2,1)}, bf16[64,2048]{1,0:T(8,128)(2,1)S(1)}, u32[]{:S(2)}, u32[]{:S(2)}) collective-permute-start(bf16[64,2048]{1,0:T(8,128)(2,1)} %get-tuple-element.89), channel_id=1, source_target_pairs={{0,4},{1,5},{2,6},{3,7},{4,0},{5,1},{6,2},{7,3},{8,12},{9,13},{10,... | collective-permute-start | bytes 786440 | tf_op jit(solution)/shard_map/ppermute | solution.py:511
  172.7 14.8 %collective-permute-start.17 = (bf16[64,2048]{1,0:T(8,128)(2,1)}, bf16[64,2048]{1,0:T(8,128)(2,1)S(1)}, u32[]{:S(2)}, u32[]{:S(2)}) collective-permute-start(bf16[64,2048]{1,0:T(8,128)(2,1)} %dynamic-slice_convert_fusion.2), channel_id=1, source_target_pairs={{0,1},{1,0},{2,3},{3,2},{4,5},{5,4},{6,7},{7,6},{8,9},{9,8},{10,11... | collective-permute-start | bytes 786440 | tf_op jit(solution)/shard_map/ppermute | solution.py:511
  182.1 35.3 %all-to-all-start.3 = ((bf16[16,512,128]{2,1,0:T(8,128)(2,1)}), bf16[16,512,128]{2,1,0:T(8,128)(2,1)S(1)}, u32[]{:S(2)}, u32[]{:S(2)}) async-start(bf16[16,512,128]{2,1,0:T(8,128)(2,1)} %shard_map.146), calls=%async_computation.3 | async-start | bytes 4194304 | tf_op jit(solution)/shard_map/all_to_all | solution.py:569
  191.0 9.2 %collective-permute-start.21 = (bf16[64,2048]{1,0:T(8,128)(2,1)}, bf16[64,2048]{1,0:T(8,128)(2,1)S(1)}, u32[]{:S(2)}, u32[]{:S(2)}) collective-permute-start(bf16[64,2048]{1,0:T(8,128)(2,1)} %fusion.6), channel_id=1, source_target_pairs={{0,1},{1,0},{2,3},{3,2},{4,5},{5,4},{6,7},{7,6},{8,9},{9,8},{10,11... | collective-permute-start | bytes 786440 | tf_op jit(solution)/shard_map/ppermute | solution.py:511
  (27 other events, 68.3 us)

commit v2 on v1

--- a/solution.py
+++ b/solution.py
@@ -36,7 +36,7 @@
     return jax.ShapeDtypeStruct(shape, dtype)
 
 
-def call(kernel, outs, specs, scratch=(), flops=0, moved=0):
+def call(kernel, outs, specs, scratch=(), flops=0, moved=0, limit=None):
     return pl.pallas_call(
         kernel,
         out_shape=outs,
@@ -44,6 +44,7 @@
         out_specs=jax.tree.map(lambda _: VMEM, outs),
         scratch_shapes=list(scratch),
         cost_estimate=pl.CostEstimate(flops=flops, bytes_accessed=moved, transcendentals=0),
+        compiler_params=pltpu.CompilerParams(vmem_limit_bytes=limit),
     )
 
 
@@ -54,41 +55,33 @@
         scratch[pl.ds(c, slots, stride=n), :] = values[:, c * 128 : (c + 1) * 128]
 
 
-def targets_of(along_rows, along_cols, axis):
-    rows = along_rows.shape[1]
+def targets_of(ids, axis):
+    rows = ids.shape[1]
+    flat = [ids[k : k + 1, :].astype(F32) for k in range(2)]
+    tall = [jnp.broadcast_to(f, (rows, rows)).T for f in flat]
     row_id = lax.broadcasted_iota(jnp.int32, (rows, rows), 0)
     col_id = lax.broadcasted_iota(jnp.int32, (rows, rows), 1)
+    named, others = (flat, tall) if axis == 0 else (tall, flat)
     before = row_id < col_id if axis == 0 else col_id < row_id
     found = []
     for k in range(2):
-        if axis == 0:
-            named = along_rows[k : k + 1, :]
-            same = (along_cols[:, 0:1] == named) | (along_cols[:, 1:2] == named)
-        else:
-            named = along_cols[:, k : k + 1]
-            same = (along_rows[0:1, :] == named) | (along_rows[1:2, :] == named)
+        same = (others[0] == named[k]) | (others[1] == named[k])
         count = jnp.sum(jnp.where(same & before, 1.0, 0.0), axis=axis, keepdims=True)
-        found.append(named * CAP + count.astype(jnp.int32))
+        name = named[k] if axis == 0 else named[k][:, 0:1]
+        found.append((name * CAP + count).astype(jnp.int32))
     return found
 
 
-def pick_matrix(along_rows, along_cols, slots):
-    rows = along_rows.shape[1]
-    targets = targets_of(along_rows[...], along_cols[...], 0)
-    slot = lax.broadcasted_iota(jnp.int32, (slots, rows), 0)
+def pick_matrix(ids, slots):
+    targets = targets_of(ids[...], 0)
+    slot = lax.broadcasted_iota(jnp.int32, (slots, ids.shape[1]), 0)
     return slot == targets[0], slot == targets[1]
 
 
-def attention_kernel(me, t0, t1, t2, t3, gain, w, query, key, value, chances, m0, m1, m2, m3, normed, held, sems):
+def attention_kernel(me, t0, t1, t2, t3, gain, w, query, key, value, chances, m0, m1, m2, m3, normed):
     rows = t0.shape[0]
-    copies = [
-        pltpu.make_async_copy(t, held.at[k], sems.at[k]) for k, t in enumerate((t0, t1, t2, t3))
-    ]
-    for copy in copies:
-        copy.start()
-    for k, copy in enumerate(copies):
-        copy.wait()
-        values = held[k].astype(F32)
+    for k, t in enumerate((t0, t1, t2, t3)):
+        values = t[...].astype(F32)
         normed[k * rows : (k + 1) * rows, :] = (values * inverse_rms(values) * gain[...]).astype(BF)
     weights = jnp.concatenate([w[0], w[1], w[2]], axis=1)
     proj = dot(normed[...], weights).astype(BF)
@@ -120,8 +113,7 @@
         (head, head, head, shaped((length, length), F32))
         + (shaped((rows, HD), BF),) * 4
         + (shaped((length, width), BF),),
-        [SMEM] + [HBM] * 4 + [VMEM] * 2,
-        [pltpu.VMEM((4, rows, width), BF), pltpu.SemaphoreType.DMA((4,))],
+        [SMEM] + [VMEM] * 6,
         flops=2 * length * (3 * width + 2 * length) * HD,
         moved=2 * length * width * 2 + 3 * width * HD * 2 + length * length * 4,
     )(me, *blocks, gain, w_qkv)
@@ -152,10 +144,10 @@
     )(me, *mixed, *weights)
 
 
-def grads_kernel(me, ids, ids_t, gates, grad_out, sent, scratch):
+def grads_kernel(me, ids, gates, grad_out, sent, scratch):
     half = grad_out.shape[1] // 2
     slots = CAP * sent.shape[0] // (2 * CAP * half // 128)
-    first, second = pick_matrix(ids_t, ids, slots)
+    first, second = pick_matrix(ids, slots)
     scale = jnp.sum(
         jnp.where(first, gates[0:1, :], 0.0) + jnp.where(second, gates[1:2, :], 0.0),
         axis=1,
@@ -170,10 +162,10 @@
     sent[count:, :] = tiles
 
 
-def hidden_kernel(me, ids, ids_t, tokens, mine, other, hidden, sent, scratch):
+def hidden_kernel(me, ids, tokens, mine, other, hidden, sent, scratch):
     half = mine.shape[1]
     slots = CAP * sent.shape[0] // (2 * CAP * half // 128)
-    first, second = pick_matrix(ids_t, ids, slots)
+    first, second = pick_matrix(ids, slots)
     picker = (first | second).astype(BF)
     chosen = tokens[:, pl.ds(pl.multiple_of(me[1] * half, half), half)].astype(F32)
     rows = (chosen + (mine[...] + other[...].astype(F32))).astype(BF)
@@ -185,30 +177,30 @@
     sent[count:, :] = tiles
 
 
-def send_grads(me, ids, ids_t, gates, grad_out, experts):
+def send_grads(me, ids, gates, grad_out, experts):
     rows, width = grad_out.shape
     tiles = experts * CAP * width // 2 // 128
     return call(
         grads_kernel,
         shaped((2 * tiles, 128), BF),
+        [SMEM] + [VMEM] * 3,
+        [pltpu.VMEM((tiles, 128), F32)],
+        flops=2 * experts * CAP * rows * width // 2,
+        moved=tiles * 512,
+    )(me, ids, gates, grad_out)
+
+
+def send_hidden(me, ids, tokens, mine, other, experts):
+    rows, width = tokens.shape
+    tiles = experts * CAP * width // 2 // 128
+    return call(
+        hidden_kernel,
+        (shaped((rows, width // 2), BF), shaped((2 * tiles, 128), BF)),
         [SMEM] + [VMEM] * 4,
         [pltpu.VMEM((tiles, 128), F32)],
         flops=2 * experts * CAP * rows * width // 2,
         moved=tiles * 512,
-    )(me, ids, ids_t, gates, grad_out)
-
-
-def send_hidden(me, ids, ids_t, tokens, mine, other, experts):
-    rows, width = tokens.shape
-    tiles = experts * CAP * width // 2 // 128
-    return call(
-        hidden_kernel,
-        (shaped((rows, width // 2), BF), shaped((2 * tiles, 128), BF)),
-        [SMEM] + [VMEM] * 5,
-        [pltpu.VMEM((tiles, 128), F32)],
-        flops=2 * experts * CAP * rows * width // 2,
-        moved=tiles * 512,
-    )(me, ids, ids_t, tokens, mine, other)
+    )(me, ids, tokens, mine, other)
 
 
 def gathered(scratch, got, slots, wide):
@@ -326,7 +318,7 @@
     )(in_rows, in_grads, product, gate_grad, up_grad)
 
 
-def combine_kernel(ids, ids_t, got, out, scratch):
+def combine_kernel(ids, got, out, scratch):
     rows, half = out.shape
     tiles = scratch.shape[0]
     n = half // 128
@@ -336,27 +328,27 @@
         [scratch[pl.ds(c, slots, stride=n), :] for c in range(n)], axis=1
     ).astype(BF)
     slot = lax.broadcasted_iota(jnp.int32, (rows, slots), 1)
-    targets = targets_of(ids_t[...], ids[...], 1)
+    targets = targets_of(ids[...], 1)
     picker = ((slot == targets[0]) | (slot == targets[1])).astype(BF)
     out[...] = dot(picker, values).astype(BF)
 
 
-def combine(ids, ids_t, got, half):
-    rows = ids.shape[0]
+def combine(ids, got, half):
+    rows = ids.shape[1]
     tiles = got.shape[0] // 2
     return call(
         combine_kernel,
         shaped((rows, half), BF),
-        [VMEM] * 3,
+        [VMEM] * 2,
         [pltpu.VMEM((tiles, 128), F32)],
         flops=2 * rows * tiles * 128,
         moved=tiles * 512,
-    )(ids, ids_t, got)
+    )(ids, got)
 
 
 def hidden_grad_kernel(
     me, grad_out, hidden_mine, hidden_other, normed_mine, normed_other, gain, w0, w1, w2, w3,
-    grad, rounded, top, bottom, p0, p1, p2, p3
+    grad, rounded, p0, p1, p2, p3
 ):
     first = me[1] == 0
 
@@ -372,8 +364,6 @@
     grad[...] = value
     low = value.astype(BF)
     rounded[...] = low
-    top[...] = low[: top.shape[0]]
-    bottom[...] = low[top.shape[0] :]
     for p, w in ((p0, w0), (p1, w1), (p2, w2), (p3, w3)):
         p[...] = dot(low, w[...], ((1,), (1,))).astype(BF)
 
@@ -384,7 +374,6 @@
     return call(
         hidden_grad_kernel,
         (shaped((rows, width), F32), shaped((rows, width), BF))
-        + (shaped((rows // 2, width), BF),) * 2
         + (piece,) * 4,
         [SMEM] + [VMEM] * 10,
         flops=8 * rows * width * HD,
@@ -471,6 +460,7 @@
         [pltpu.VMEM(got.shape, BF), pltpu.SemaphoreType.DMA((got.shape[0],))],
         flops=got.size,
         moved=got.size * 2,
+        limit=65_000_000,
     )(got)
 
 
@@ -511,10 +501,11 @@
     return lax.ppermute(x, HG, [(i, i ^ flip) for i in range(8)])
 
 
-def sequence(x, top, bottom):
-    top, bottom = swap(top, 2, 0), swap(bottom, 2, 1)
-    far = jnp.concatenate([top, bottom], axis=0)
-    return [x, swap(x, 1, 0), far, swap(far, 1, 0)]
+def sequence(x):
+    pairs = [(i, i ^ 4 ^ (i >> 1 & 1)) for i in range(8)]
+    far = lax.ppermute(x, HG, pairs)
+    core = swap(x, 1, 0)
+    return [x, core, far, swap(far, 1, 0)]
 
 
 def exchange(tiles):
@@ -526,16 +517,16 @@
 def body(
     tokens, grad_out, w_qkv, w_attn_out, gain_attn, gain_ffn, w_gate_up, w_down, ids, gates
 ):
-    rows, width = tokens.shape
+    _, width = tokens.shape
     half = width // 2
     experts = lax.axis_size("dp") * lax.axis_size("head")
     me = jnp.stack([lax.axis_index("head"), lax.axis_index("group")]).astype(jnp.int32)
     gain_attn, gain_ffn = gain_attn[None], gain_ffn[None]
     w_pair = w_gate_up.transpose(0, 1, 3, 2)
-    ids_t, gates_t = ids.T, gates.T
-
-    blocks = sequence(tokens, tokens[: rows // 2], tokens[rows // 2 :])
-    tiles = send_grads(me, ids, ids_t, gates_t, grad_out, experts)
+    ids, gates = ids.T, gates.T
+
+    blocks = sequence(tokens)
+    tiles = send_grads(me, ids, gates, grad_out, experts)
     got_grads = exchange(tiles)
     w_far = swap(w_attn_out, 2, 0)
     weights = [w_attn_out, swap(w_attn_out, 1, 0), w_far, swap(w_far, 1, 0)]
@@ -544,7 +535,7 @@
     heads = [mixed[0]] + [swap(mixed[k], k, 0) for k in range(1, 4)]
     mine, other = project(me, heads, weights)
     other = swap(other, 0, 1)
-    hidden, tiles = send_hidden(me, ids, ids_t, tokens, mine, other, experts)
+    hidden, tiles = send_hidden(me, ids, tokens, mine, other, experts)
     in_grads, in_upstream = experts_early(got_grads, w_down)
     tiles, in_grads = lax.optimization_barrier((tiles, in_grads))
     got_hidden = exchange(tiles)
@@ -555,12 +546,12 @@
     got_back = exchange(tiles)
     grad_pair, grad_down = expert_grads(in_rows, in_grads, *saved)
 
-    upstream = combine(ids, ids_t, got_back, half)
+    upstream = combine(ids, got_back, half)
     halves = (hidden, hidden_other, upstream, swap(upstream, 0, 1))
-    grad_hidden, rounded, top, bottom, *grads = hidden_grad(
+    grad_hidden, rounded, *grads = hidden_grad(
         me, grad_out, halves, gain_ffn, weights)
     grads = [grads[0]] + [swap(grads[k], k, 0) for k in range(1, 4)]
-    all_grads = sequence(rounded, top, bottom)
+    all_grads = sequence(rounded)
 
     acts, near, far, near_out, far_out = attention_back(grads, query, key, value, chances, w_qkv)
     near_in = swap(near_out, 1, 0)

time: 222 us -> 226 us (1.018)
  waiting for transfers between devices: 63.2 us -> 76.5 us
  local copies, waits for them, and re-layouts: 14.9 us -> 10.5 us
  other arithmetic: 7.37 us -> 3.68 us
    ppermute x26 -> x22, waiting for transfers between devices: 27.8 us -> 39.1 us  [swap(): return lax.ppermute(x, HG, [(i, i ^ flip) for i in range(8)])]
    ppermute x26 -> x22, starting transfers between devices: 23.6 us -> 19.8 us  [swap(): return lax.ppermute(x, HG, [(i, i ^ flip) for i in range(8)])]
    unnamed x63 -> x52, local copies, waits for them, and re-layouts: 12.2 us -> 8.86 us
    ppermute x0 -> x2, starting transfers between devices: none -> 2.26 us  [sequence(): far = lax.ppermute(x, HG, pairs)]
  transfers between devices with their start and end apart: 29 -> 27, of which waited for: 9 -> 8; matrix products, arithmetic and copies ran while one was open for 5% -> 2% of each run, Pallas kernels for 18% -> 17%
where the time goes in v2:
time: 226 us; the launch traced here: 225 us
  waiting for transfers between devices  76.5 us (34%)
  Pallas kernels  57.9 us (26%)
  starting transfers between devices  43 us (19%)
  blocking collectives  32.5 us (14%)
  local copies, waits for them, and re-layouts  10.5 us (5%)
  other arithmetic  3.68 us (2%)
    ppermute x22, waiting for transfers between devices, swap(): return lax.ppermute(x, HG, [(i, i ^ flip) for i in range(8)])  39.1 us
    all_to_all x1, blocking collectives, exchange(): return lax.all_to_all(tiles, ALL, 0, 0, tiled=True).reshape(-1, 128)  32.5 us
    all_to_all x2, waiting for transfers between devices, exchange(): return lax.all_to_all(tiles, ALL, 0, 0, tiled=True).reshape(-1, 128)  20.1 us
    ppermute x22, starting transfers between devices, swap(): return lax.ppermute(x, HG, [(i, i ^ flip) for i in range(8)])  19.8 us
    all_to_all x1, waiting for transfers between devices, body(): got = lax.all_to_all(sent, 'dp', 0, 0, tiled=True)  17.4 us
    all_to_all x2, starting transfers between devices, exchange(): return lax.all_to_all(tiles, ALL, 0, 0, tiled=True).reshape(-1, 128)  15.6 us
    pallas_call x1, Pallas kernels, experts_forward(): call(expert_kernel, (shaped((2 * tiles, 128), BF), row, unit, unit, unit)...  9.92 us
    unnamed x52, local copies, waits for them, and re-layouts  8.86 us
  transfers between devices with their start and end apart: 27, of which 8 were waited for; matrix products, arithmetic and copies ran while one was open for 2% of the time, Pallas kernels for 17%

profile of v2, /device:TPU:0, one launch (start us, length us, event | category | flops | bytes accessed | tf_op | source)
XLA Modules:
  0.0 225.2 jit_solution(3115726336874576875)
XLA Ops:
  0.6 1.7 collective-permute-start.1
  2.9 2.7 %shard_map.140 = bf16[5120,128]{1,0:T(8,128)(2,1)} custom-call(s32[2]{0:T(128)} %pad_add_fusion.me, s32[2,128]{1,0:T(2,128)} %bitcast.21, f32[2,128]{1,0:T(2,128)} %bitcast.26, bf16[128,2048]{1,0:T(8,128)(2,1)} %grad_out.3), custom_call_target="tpu_custom_call" | custom-call | flops 83886080 | bytes 1310720 | tf_op jit(solution)/shard_map/pallas_call | solution.py:183
  5.6 10.8 %all-to-all-start = ((bf16[128,40,128]{2,1,0:T(8,128)(2,1)}), bf16[128,40,128]{2,1,0:T(8,128)(2,1)S(1)}, u32[]{:S(2)}, u32[]{:S(2)}) async-start(bf16[128,40,128]{2,1,0:T(8,128)(2,1)} %bitcast.15), calls=%async_computation | async-start | bytes 2621440 | tf_op jit(solution)/shard_map/all_to_all | solution.py:514
  18.0 24.9 %collective-permute-done.7.w2 = bf16[128,2048]{1,0:T(8,128)(2,1)S(1)} collective-permute-done((bf16[128,2048]{1,0:T(8,128)(2,1)S(1)}, bf16[128,2048]{1,0:T(8,128)(2,1)S(1)}, u32[]{:S(2)}, u32[]{:S(2)}) %collective-permute-start.7) | collective-permute-done | bytes 524320 | tf_op jit(solution)/shard_map/ppermute | solution.py:501
  44.5 6.1 %shard_map.137 = (bf16[512,128]{1,0:T(8,128)(2,1)}, bf16[512,128]{1,0:T(8,128)(2,1)}, bf16[512,128]{1,0:T(8,128)(2,1)}, f32[512,512]{1,0:T(8,128)}, bf16[128,128...) custom-call(s32[2]{0:T(128)} %pad_add_fusion.me, ...), custom_call_target="tpu_custom_call" | custom-call | flops 939524096 | bytes 6815744 | tf_op jit(solution)/shard_map/pallas_call | solution.py:111
  52.6 2.8 %collective-permute-done.4.m2 = bf16[128,128]{1,0:T(8,128)(2,1)S(1)} collective-permute-done((bf16[128,128]{1,0:T(8,128)(2,1)}, bf16[128,128]{1,0:T(8,128)(2,1)S(1)}, u32[]{:S(2)}, u32[]{:S(2)}) %collective-permute-start.4) | collective-permute-done | bytes 32800 | tf_op jit(solution)/shard_map/ppermute | solution.py:501
  56.1 3.2 %shard_map.138 = (f32[128,1024]{1,0:T(8,128)}, bf16[128,1024]{1,0:T(8,128)(2,1)}) custom-call(s32[2]{0:T(128)} %pad_add_fusion.me, bf16[128,128]{1,0:T(8,128)(2,1)} %get-tuple-element.44.m0, bf16[128,128]{1,0:T(8,128)(2,1)} %copy-done.20, bf16[128,128]{1,0:T(8,128)(2,1)} %copy-done.21, bf16[128,128]{1,0:T(8,128)(2,1)} %copy-done.22, bf16[128,2048]{1,0:T(8,128)(2,1)} %w0.3, ...), custom_call_target="tpu_custom_call" | custom-call | flops 268435456 | bytes 2097152 | tf_op jit(solution)/shard_map/pallas_call | solution.py:138
  59.3 3.1 %collective-permute-start.9 = (bf16[128,1024]{1,0:T(8,128)(2,1)}, bf16[128,1024]{1,0:T(8,128)(2,1)S(1)}, u32[]{:S(2)}, u32[]{:S(2)}) collective-permute-start(bf16[128,1024]{1,0:T(8,128)(2,1)} %get-tuple-element.49), channel_id=1, source_target_pairs={{0,1},{1,0},{2,3},{3,2},{4,5},{5,4},{6,7},{7,6},{8,9},{9,8},{10,11... | collective-permute-start | bytes 786440 | tf_op jit(solution)/shard_map/ppermute | solution.py:501
  62.4 1.1 copy-done.2
  63.4 5.4 %shard_map.141 = (bf16[320,2048]{1,0:T(8,128)(2,1)}, f32[320,704]{1,0:T(8,128)}) custom-call(bf16[5120,128]{1,0:T(8,128)(2,1)} %bitcast.14, bf16[1,704,2048]{2,1,0:T(8,128)(2,1)} %w_down.1), custom_call_target="tpu_custom_call" | custom-call | flops 922746880 | bytes 2883584 | tf_op jit(solution)/shard_map/pallas_call | solution.py:229
  70.0 2.9 %shard_map.139 = (bf16[128,1024]{1,0:T(8,128)(2,1)}, bf16[5120,128]{1,0:T(8,128)(2,1)}) custom-call(s32[2]{0:T(128)} %pad_add_fusion.me, s32[2,128]{1,0:T(2,128)} %bitcast.22, bf16[128,2048]{1,0:T(8,128)(2,1)} %tokens.1, f32[128,1024]{1,0:T(8,128)} %get-tuple-element.48.mine, bf16[128,1024]{1,0:T(8,128)(2,1)} %copy-done.15), custom_call_target="tpu_custom_call" | custom-call | flops 83886080 | bytes 1310720 | tf_op jit(solution)/shard_map/pallas_call | solution.py:196
  73.0 32.5 %all_to_all.20 = bf16[128,40,128]{2,1,0:T(8,128)(2,1)} all-to-all(bf16[128,40,128]{2,1,0:T(8,128)(2,1)} %bitcast.19), channel_id=1, replica_groups=mesh['dp'=16,'head'=4,'group'=2] {'group','dp','head'}, dimensions={0} | all-to-all | bytes 2621440 | tf_op jit(solution)/shard_map/all_to_all | solution.py:514
  105.5 9.9 %shard_map.142 = (bf16[5120,128]{1,0:T(8,128)(2,1)}, bf16[320,2048]{1,0:T(8,128)(2,1)}, bf16[320,704]{1,0:T(8,128)(2,1)}, bf16[320,704]{1,0:T(8,128)(2,1)}, bf16[320,704]{1,0:T(8,128)(2,1)}) custom-call(bf16[5120,128]{1,0:T(8,128)(2,1)} %bitcast.18, f32[320,704]{1,0:T(8,128)} %get-tuple-element.56.upstream_ref, f32[1,2048]{1,0:T(1,128)} %bitcast.24, ...), custom_call_target="tpu_custom_call" | custom-call | flops 3690987520 | bytes 5767168 | tf_op jit(solution)/shard_map/pallas_call | solution.py:279
  115.4 4.8 %all-to-all-start.2 = ((bf16[128,40,128]{2,1,0:T(8,128)(2,1)}), bf16[128,40,128]{2,1,0:T(8,128)(2,1)S(1)}, u32[]{:S(2)}, u32[]{:S(2)}) async-start(bf16[128,40,128]{2,1,0:T(8,128)(2,1)} %bitcast.17), calls=%async_computation.2 | async-start | bytes 2621440 | tf_op jit(solution)/shard_map/all_to_all | solution.py:514
  120.2 2.4 %collective-permute-start.10 = (bf16[128,1024]{1,0:T(8,128)(2,1)S(1)}, bf16[128,1024]{1,0:T(8,128)(2,1)S(1)}, u32[]{:S(2)}, u32[]{:S(2)}) collective-permute-start(bf16[128,1024]{1,0:T(8,128)(2,1)S(1)} %copy-done.16), channel_id=1, source_target_pairs={{0,1},{1,0},{2,3},{3,2},{4,5},{5,4},{6,7},{7,6},{8,9},{9,8},{10,11... | collective-permute-start | bytes 786440 | tf_op jit(solution)/shard_map/ppermute | solution.py:501
  122.7 20.1 %all-to-all-done.2 = bf16[128,40,128]{2,1,0:T(8,128)(2,1)S(1)} async-done(((bf16[128,40,128]{2,1,0:T(8,128)(2,1)}), bf16[128,40,128]{2,1,0:T(8,128)(2,1)S(1)}, u32[]{:S(2)}, u32[]{:S(2)}) %all-to-all-start.2) | async-done | bytes 1310752 | tf_op jit(solution)/shard_map/all_to_all | solution.py:514
  142.7 1.1 copy-done.3
  143.8 2.7 %shard_map.143.normed_mine = bf16[128,1024]{1,0:T(8,128)(2,1)} custom-call(s32[2,128]{1,0:T(2,128)} %bitcast.23, bf16[5120,128]{1,0:T(8,128)(2,1)} %bitcast.16), custom_call_target="tpu_custom_call" | custom-call | flops 83886080 | bytes 1310720 | tf_op jit(solution)/shard_map/pallas_call | solution.py:339
  147.0 8.1 %collective-permute-done.11.normed_other = bf16[128,1024]{1,0:T(8,128)(2,1)S(1)} collective-permute-done((bf16[128,1024]{1,0:T(8,128)(2,1)}, bf16[128,1024]{1,0:T(8,128)(2,1)S(1)}, u32[]{:S(2)}, u32[]{:S(2)}) %collective-permute-start.11) | collective-permute-done | bytes 262176 | tf_op jit(solution)/shard_map/ppermute | solution.py:501
  155.8 3.9 %shard_map.144 = (f32[128,2048]{1,0:T(8,128)}, bf16[128,2048]{1,0:T(8,128)(2,1)}, bf16[128,128]{1,0:T(8,128)(2,1)}, bf16[128,128]{1,0:T(8,128)(2,1)}, bf16[128,1...) custom-call(s32[2]{0:T(128)} %pad_add_fusion.me, bf16[128,2048]{1,0:T(8,128)(2,1)} %grad_out.3, ...), custom_call_target="tpu_custom_call" | custom-call | flops 268435456 | bytes 4718592 | tf_op jit(solution)/shard_map/pallas_call | solution.py:374
  160.4 1.2 collective-permute-start.14
  162.2 2.1 collective-permute-done.13.g2
  164.9 5.6 %shard_map.145 = (bf16[512,384]{1,0:T(8,128)(2,1)}, f32[128,2048]{1,0:T(8,128)}, f32[128,2048]{1,0:T(8,128)}, bf16[128,2048]{1,0:T(8,128)(2,1)}, bf16[128,2048]{1,0:T(8,128)(2,1)}) custom-call(bf16[128,128]{1,0:T(8,128)(2,1)} %get-tuple-element.59.g0, bf16[128,128]{1,0:T(8,128)(2,1)} %copy-done.23, bf16[128,128]{1,0:T(8,128)(2,1)} %copy-done.24, ...), custom_call_target="tpu_custom_call" | custom-call | flops 1073741824 | bytes 5767168 | tf_op jit(solution)/shard_map/pallas_call | solution.py:407
  172.6 1.4 convert_add_fusion
  174.9 1.6 collective-permute-start.19
  177.7 2.7 %collective-permute-start.16 = (bf16[64,2048]{1,0:T(8,128)(2,1)}, bf16[64,2048]{1,0:T(8,128)(2,1)S(1)}, u32[]{:S(2)}, u32[]{:S(2)}) collective-permute-start(bf16[64,2048]{1,0:T(8,128)(2,1)} %dynamic-slice_convert_fusion.2), channel_id=1, source_target_pairs={{0,1},{1,0},{2,3},{3,2},{4,5},{5,4},{6,7},{7,6},{8,9},{9,8},{10,11... | collective-permute-start | bytes 786440 | tf_op jit(solution)/shard_map/ppermute | solution.py:501
  182.1 5.0 %shard_map.146 = bf16[16,512,128]{2,1,0:T(8,128)(2,1)} custom-call(bf16[512,384]{1,0:T(8,128)(2,1)} %get-tuple-element.71.acts, bf16[512,2048]{1,0:T(8,128)(2,1)} %get-tuple-element.72.normed, bf16[128,128]{1,0:T(8,128)(2,1)} %get-tuple-element.44.m0, bf16[128,128]{1,0:T(8,128)(2,1)} %get-tuple-element.45.m1, bf16[128,128]{1,0:T(8,128)(2,1)} %get-tuple-element.46.m2, ...), custom_call_target="tpu_custom_call" | custom-call | flops 1073741824 | bytes 6291456 | tf_op jit(solution)/shard_map/pallas_call | solution.py:430
  187.1 5.4 %all-to-all-start.3 = ((bf16[16,512,128]{2,1,0:T(8,128)(2,1)}), bf16[16,512,128]{2,1,0:T(8,128)(2,1)}, u32[]{:S(2)}, u32[]{:S(2)}) async-start(bf16[16,512,128]{2,1,0:T(8,128)(2,1)} %shard_map.146), calls=%async_computation.3 | async-start | bytes 4194304 | tf_op jit(solution)/shard_map/all_to_all | solution.py:560
  194.0 2.3 %collective-permute-start.20 = (bf16[64,2048]{1,0:T(8,128)(2,1)S(1)}, bf16[64,2048]{1,0:T(8,128)(2,1)S(1)}, u32[]{:S(2)}, u32[]{:S(2)}) collective-permute-start(bf16[64,2048]{1,0:T(8,128)(2,1)S(1)} %fusion.6), channel_id=1, source_target_pairs={{0,1},{1,0},{2,3},{3,2},{4,5},{5,4},{6,7},{7,6},{8,9},{9,8},{10,11... | collective-permute-start | bytes 786440 | tf_op jit(solution)/shard_map/ppermute | solution.py:501
  196.2 8.0 %shard_map.148 = (bf16[1,2,704,2048]{3,2,1,0:T(8,128)(2,1)}, bf16[1,704,2048]{2,1,0:T(8,128)(2,1)}) custom-call(bf16[320,2048]{1,0:T(8,128)(2,1)} %get-tuple-element.76.in_rows, bf16[320,2048]{1,0:T(8,128)(2,1)} %get-tuple-element.77.in_grads, bf16[320,704]{1,0:T(8,128)(2,1)} %get-tuple-element.78.product, bf16[320,704]{1,0:T(8,128)(2,1)} %get-tuple-element.79.gate_grad, ...), custom_call_target="tpu_custom_call" | custom-call | flops 2768240640 | bytes 8650752 | tf_op jit(solution)/shard_map/pallas_call | solution.py:306
  205.1 17.4 %all-to-all-done.3.got = bf16[16,512,128]{2,1,0:T(8,128)(2,1)} async-done(((bf16[16,512,128]{2,1,0:T(8,128)(2,1)}), bf16[16,512,128]{2,1,0:T(8,128)(2,1)}, u32[]{:S(2)}, u32[]{:S(2)}) %all-to-all-start.3) | async-done | bytes 2097184 | tf_op jit(solution)/shard_map/all_to_all | solution.py:560
  222.5 2.5 %shard_map.147 = (f32[3,128,128]{2,1,0:T(8,128)}, f32[128,128]{1,0:T(8,128)}) custom-call(bf16[16,512,128]{2,1,0:T(8,128)(2,1)} %all-to-all-done.3.got), custom_call_target="tpu_custom_call" | custom-call | flops 1048576 | bytes 2097152 | tf_op jit(solution)/shard_map/pallas_call | solution.py:456
  (99 shorter events, 18.9 us)
Async XLA Ops:
  0.6 16.8 %collective-permute-start.1 = (bf16[128,2048]{1,0:T(8,128)(2,1)}, bf16[128,2048]{1,0:T(8,128)(2,1)}, u32[]{:S(2)}, u32[]{:S(2)}) collective-permute-start(bf16[128,2048]{1,0:T(8,128)(2,1)} %tokens.1), channel_id=1, source_target_pairs={{0,4},{1,5},{2,7},{3,6},{4,0},{5,1},{6,3},{7,2},{8,12},{9,13},{10,... | collective-permute-start | bytes 1572872 | tf_op jit(solution)/shard_map/ppermute | solution.py:506
  5.6 10.8 %copy-start.4 = (bf16[128,2048]{1,0:T(8,128)(2,1)S(1)}, bf16[128,2048]{1,0:T(8,128)(2,1)}, u32[]{:S(2)}) copy-start(bf16[128,2048]{1,0:T(8,128)(2,1)} %w0.3) | copy-start | bytes 1572868
  5.6 11.8 %copy-start = (bf16[128,2048]{1,0:T(8,128)(2,1)S(1)}, bf16[128,2048]{1,0:T(8,128)(2,1)}, u32[]{:S(2)}) copy-start(bf16[128,2048]{1,0:T(8,128)(2,1)} %tokens.1) | copy-start | bytes 1572868
  5.6 56.8 %all-to-all-start = ((bf16[128,40,128]{2,1,0:T(8,128)(2,1)}), bf16[128,40,128]{2,1,0:T(8,128)(2,1)S(1)}, u32[]{:S(2)}, u32[]{:S(2)}) async-start(bf16[128,40,128]{2,1,0:T(8,128)(2,1)} %bitcast.15), calls=%async_computation | async-start | bytes 2621440 | tf_op jit(solution)/shard_map/all_to_all | solution.py:514
  16.4 26.5 %collective-permute-start.7 = (bf16[128,2048]{1,0:T(8,128)(2,1)S(1)}, bf16[128,2048]{1,0:T(8,128)(2,1)S(1)}, u32[]{:S(2)}, u32[]{:S(2)}) collective-permute-start(bf16[128,2048]{1,0:T(8,128)(2,1)S(1)} %copy-done.4), channel_id=1, source_target_pairs={{0,4},{1,5},{2,6},{3,7},{4,0},{5,1},{6,2},{7,3},{8,12},{9,13},{10,... | collective-permute-start | bytes 1572872 | tf_op jit(solution)/shard_map/ppermute | solution.py:501
  17.4 25.5 %collective-permute-start = (bf16[128,2048]{1,0:T(8,128)(2,1)S(1)}, bf16[128,2048]{1,0:T(8,128)(2,1)S(1)}, u32[]{:S(2)}, u32[]{:S(2)}) collective-permute-start(bf16[128,2048]{1,0:T(8,128)(2,1)S(1)} %copy-done), channel_id=1, source_target_pairs={{0,2},{1,3},{2,0},{3,1},{4,6},{5,7},{6,4},{7,5},{8,10},{9,11},{10,... | collective-permute-start | bytes 1572872 | tf_op jit(solution)/shard_map/ppermute | solution.py:501
  17.4 26.3 %collective-permute-start.2 = (bf16[128,2048]{1,0:T(8,128)(2,1)}, bf16[128,2048]{1,0:T(8,128)(2,1)S(1)}, u32[]{:S(2)}, u32[]{:S(2)}) collective-permute-start(bf16[128,2048]{1,0:T(8,128)(2,1)} %collective-permute-done.1.t2), channel_id=1, source_target_pairs={{0,2},{1,3},{2,0},{3,1},{4,6},{5,7},{6,4},{7,5},{8,10},{9,11},{10,... | collective-permute-start | bytes 1572872 | tf_op jit(solution)/shard_map/ppermute | solution.py:501
  17.9 34.7 %collective-permute-start.6 = (bf16[128,2048]{1,0:T(8,128)(2,1)S(1)}, bf16[128,2048]{1,0:T(8,128)(2,1)S(1)}, u32[]{:S(2)}, u32[]{:S(2)}) collective-permute-start(bf16[128,2048]{1,0:T(8,128)(2,1)S(1)} %copy-done.4), channel_id=1, source_target_pairs={{0,2},{1,3},{2,0},{3,1},{4,6},{5,7},{6,4},{7,5},{8,10},{9,11},{10,... | collective-permute-start | bytes 1572872 | tf_op jit(solution)/shard_map/ppermute | solution.py:501
  42.9 7.8 %copy-start.5 = (bf16[128,2048]{1,0:T(8,128)(2,1)}, bf16[128,2048]{1,0:T(8,128)(2,1)S(1)}, u32[]{:S(2)}) copy-start(bf16[128,2048]{1,0:T(8,128)(2,1)S(1)} %collective-permute-done.7.w2) | copy-start | bytes 1572868
  42.9 9.7 %collective-permute-start.8 = (bf16[128,2048]{1,0:T(8,128)(2,1)S(1)}, bf16[128,2048]{1,0:T(8,128)(2,1)}, u32[]{:S(2)}, u32[]{:S(2)}) collective-permute-start(bf16[128,2048]{1,0:T(8,128)(2,1)S(1)} %collective-permute-done.7.w2), channel_id=1, source_target_pairs={{0,2},{1,3},{2,0},{3,1},{4,6},{5,7},{6,4},{7,5},{8,10},{9,11},{10,... | collective-permute-start | bytes 1572872 | tf_op jit(solution)/shard_map/ppermute | solution.py:501
  50.7 1.9 collective-permute-start.3
  51.2 4.3 %collective-permute-start.4 = (bf16[128,128]{1,0:T(8,128)(2,1)}, bf16[128,128]{1,0:T(8,128)(2,1)S(1)}, u32[]{:S(2)}, u32[]{:S(2)}) collective-permute-start(bf16[128,128]{1,0:T(8,128)(2,1)} %get-tuple-element.46.m2), channel_id=1, source_target_pairs={{0,4},{1,5},{2,6},{3,7},{4,0},{5,1},{6,2},{7,3},{8,12},{9,13},{10,... | collective-permute-start | bytes 98312 | tf_op jit(solution)/shard_map/ppermute | solution.py:501
  51.5 3.9 %collective-permute-start.5 = (bf16[128,128]{1,0:T(8,128)(2,1)}, bf16[128,128]{1,0:T(8,128)(2,1)S(1)}, u32[]{:S(2)}, u32[]{:S(2)}) collective-permute-start(bf16[128,128]{1,0:T(8,128)(2,1)} %get-tuple-element.47.m3), channel_id=1, source_target_pairs={{0,6},{1,7},{2,4},{3,5},{4,2},{5,3},{6,0},{7,1},{8,14},{9,15},{10,... | collective-permute-start | bytes 98312 | tf_op jit(solution)/shard_map/ppermute | solution.py:501
  59.3 10.1 %collective-permute-start.9 = (bf16[128,1024]{1,0:T(8,128)(2,1)}, bf16[128,1024]{1,0:T(8,128)(2,1)S(1)}, u32[]{:S(2)}, u32[]{:S(2)}) collective-permute-start(bf16[128,1024]{1,0:T(8,128)(2,1)} %get-tuple-element.49), channel_id=1, source_target_pairs={{0,1},{1,0},{2,3},{3,2},{4,5},{5,4},{6,7},{7,6},{8,9},{9,8},{10,11... | collective-permute-start | bytes 786440 | tf_op jit(solution)/shard_map/ppermute | solution.py:501
  115.4 27.3 %all-to-all-start.2 = ((bf16[128,40,128]{2,1,0:T(8,128)(2,1)}), bf16[128,40,128]{2,1,0:T(8,128)(2,1)S(1)}, u32[]{:S(2)}, u32[]{:S(2)}) async-start(bf16[128,40,128]{2,1,0:T(8,128)(2,1)} %bitcast.17), calls=%async_computation.2 | async-start | bytes 2621440 | tf_op jit(solution)/shard_map/all_to_all | solution.py:514
  120.2 26.8 %collective-permute-start.10 = (bf16[128,1024]{1,0:T(8,128)(2,1)S(1)}, bf16[128,1024]{1,0:T(8,128)(2,1)S(1)}, u32[]{:S(2)}, u32[]{:S(2)}) collective-permute-start(bf16[128,1024]{1,0:T(8,128)(2,1)S(1)} %copy-done.16), channel_id=1, source_target_pairs={{0,1},{1,0},{2,3},{3,2},{4,5},{5,4},{6,7},{7,6},{8,9},{9,8},{10,11... | collective-permute-start | bytes 786440 | tf_op jit(solution)/shard_map/ppermute | solution.py:501
  146.5 8.6 %collective-permute-start.11 = (bf16[128,1024]{1,0:T(8,128)(2,1)}, bf16[128,1024]{1,0:T(8,128)(2,1)S(1)}, u32[]{:S(2)}, u32[]{:S(2)}) collective-permute-start(bf16[128,1024]{1,0:T(8,128)(2,1)} %shard_map.143.normed_mine), channel_id=1, source_target_pairs={{0,1},{1,0},{2,3},{3,2},{4,5},{5,4},{6,7},{7,6},{8,9},{9,8},{10,11... | collective-permute-start | bytes 786440 | tf_op jit(solution)/shard_map/ppermute | solution.py:501
  147.0 8.1 %copy-start.17 = (bf16[128,1024]{1,0:T(8,128)(2,1)}, bf16[128,1024]{1,0:T(8,128)(2,1)S(1)}, u32[]{:S(2)}) copy-start(bf16[128,1024]{1,0:T(8,128)(2,1)S(1)} %collective-permute-done.10.hidden_other) | copy-start | bytes 786436
  159.7 2.5 %collective-permute-start.12 = (bf16[128,128]{1,0:T(8,128)(2,1)}, bf16[128,128]{1,0:T(8,128)(2,1)S(1)}, u32[]{:S(2)}, u32[]{:S(2)}) collective-permute-start(bf16[128,128]{1,0:T(8,128)(2,1)} %get-tuple-element.60), channel_id=1, source_target_pairs={{0,2},{1,3},{2,0},{3,1},{4,6},{5,7},{6,4},{7,5},{8,10},{9,11},{10,... | collective-permute-start | bytes 98312 | tf_op jit(solution)/shard_map/ppermute | solution.py:501
  159.7 4.5 %collective-permute-start.13 = (bf16[128,128]{1,0:T(8,128)(2,1)}, bf16[128,128]{1,0:T(8,128)(2,1)S(1)}, u32[]{:S(2)}, u32[]{:S(2)}) collective-permute-start(bf16[128,128]{1,0:T(8,128)(2,1)} %get-tuple-element.61), channel_id=1, source_target_pairs={{0,4},{1,5},{2,6},{3,7},{4,0},{5,1},{6,2},{7,3},{8,12},{9,13},{10,... | collective-permute-start | bytes 98312 | tf_op jit(solution)/shard_map/ppermute | solution.py:501
  160.4 3.9 %collective-permute-start.14 = (bf16[128,128]{1,0:T(8,128)(2,1)}, bf16[128,128]{1,0:T(8,128)(2,1)S(1)}, u32[]{:S(2)}, u32[]{:S(2)}) collective-permute-start(bf16[128,128]{1,0:T(8,128)(2,1)} %get-tuple-element.62), channel_id=1, source_target_pairs={{0,6},{1,7},{2,4},{3,5},{4,2},{5,3},{6,0},{7,1},{8,14},{9,15},{10,... | collective-permute-start | bytes 98312 | tf_op jit(solution)/shard_map/ppermute | solution.py:501
  161.6 10.0 %collective-permute-start.22 = (bf16[128,2048]{1,0:T(8,128)(2,1)}, bf16[128,2048]{1,0:T(8,128)(2,1)S(1)}, u32[]{:S(2)}, u32[]{:S(2)}) collective-permute-start(bf16[128,2048]{1,0:T(8,128)(2,1)} %get-tuple-element.73.g0), channel_id=1, source_target_pairs={{0,4},{1,5},{2,7},{3,6},{4,0},{5,1},{6,3},{7,2},{8,12},{9,13},{10,... | collective-permute-start | bytes 1572872 | tf_op jit(solution)/shard_map/ppermute | solution.py:506
  164.9 5.9 %copy-start.10 = (bf16[128,2048]{1,0:T(8,128)(2,1)S(1)}, bf16[128,2048]{1,0:T(8,128)(2,1)}, u32[]{:S(2)}) copy-start(bf16[128,2048]{1,0:T(8,128)(2,1)} %get-tuple-element.73.g0) | copy-start | bytes 1572868
  170.5 2.1 collective-permute-start.17
  170.8 9.7 %collective-permute-start.21 = (bf16[128,2048]{1,0:T(8,128)(2,1)S(1)}, bf16[128,2048]{1,0:T(8,128)(2,1)S(1)}, u32[]{:S(2)}, u32[]{:S(2)}) collective-permute-start(bf16[128,2048]{1,0:T(8,128)(2,1)S(1)} %copy-done.10), channel_id=1, source_target_pairs={{0,2},{1,3},{2,0},{3,1},{4,6},{5,7},{6,4},{7,5},{8,10},{9,11},{10,... | collective-permute-start | bytes 1572872 | tf_op jit(solution)/shard_map/ppermute | solution.py:501
  171.4 5.4 %collective-permute-start.15 = (bf16[128,2048]{1,0:T(8,128)(2,1)}, bf16[128,2048]{1,0:T(8,128)(2,1)S(1)}, u32[]{:S(2)}, u32[]{:S(2)}) collective-permute-start(bf16[128,2048]{1,0:T(8,128)(2,1)} %get-tuple-element.68), channel_id=1, source_target_pairs={{0,2},{1,3},{2,0},{3,1},{4,6},{5,7},{6,4},{7,5},{8,10},{9,11},{10,... | collective-permute-start | bytes 1572872 | tf_op jit(solution)/shard_map/ppermute | solution.py:501
  171.6 8.9 %collective-permute-start.23 = (bf16[128,2048]{1,0:T(8,128)(2,1)S(1)}, bf16[128,2048]{1,0:T(8,128)(2,1)S(1)}, u32[]{:S(2)}, u32[]{:S(2)}) collective-permute-start(bf16[128,2048]{1,0:T(8,128)(2,1)S(1)} %collective-permute-done.22.g2), channel_id=1, source_target_pairs={{0,2},{1,3},{2,0},{3,1},{4,6},{5,7},{6,4},{7,5},{8,10},{9,11},{10,... | collective-permute-start | bytes 1572872 | tf_op jit(solution)/shard_map/ppermute | solution.py:501
  174.9 17.6 %collective-permute-start.19 = (bf16[64,2048]{1,0:T(8,128)(2,1)}, bf16[64,2048]{1,0:T(8,128)(2,1)S(1)}, u32[]{:S(2)}, u32[]{:S(2)}) collective-permute-start(bf16[64,2048]{1,0:T(8,128)(2,1)} %get-tuple-element.86), channel_id=1, source_target_pairs={{0,5},{1,4},{2,7},{3,6},{4,1},{5,0},{6,3},{7,2},{8,13},{9,12},{10,... | collective-permute-start | bytes 786440 | tf_op jit(solution)/shard_map/ppermute | solution.py:501
  176.5 16.0 %collective-permute-start.18 = (bf16[64,2048]{1,0:T(8,128)(2,1)}, bf16[64,2048]{1,0:T(8,128)(2,1)S(1)}, u32[]{:S(2)}, u32[]{:S(2)}) collective-permute-start(bf16[64,2048]{1,0:T(8,128)(2,1)} %get-tuple-element.85), channel_id=1, source_target_pairs={{0,4},{1,5},{2,6},{3,7},{4,0},{5,1},{6,2},{7,3},{8,12},{9,13},{10,... | collective-permute-start | bytes 786440 | tf_op jit(solution)/shard_map/ppermute | solution.py:501
  177.7 14.8 %collective-permute-start.16 = (bf16[64,2048]{1,0:T(8,128)(2,1)}, bf16[64,2048]{1,0:T(8,128)(2,1)S(1)}, u32[]{:S(2)}, u32[]{:S(2)}) collective-permute-start(bf16[64,2048]{1,0:T(8,128)(2,1)} %dynamic-slice_convert_fusion.2), channel_id=1, source_target_pairs={{0,1},{1,0},{2,3},{3,2},{4,5},{5,4},{6,7},{7,6},{8,9},{9,8},{10,11... | collective-permute-start | bytes 786440 | tf_op jit(solution)/shard_map/ppermute | solution.py:501
  187.1 35.4 %all-to-all-start.3 = ((bf16[16,512,128]{2,1,0:T(8,128)(2,1)}), bf16[16,512,128]{2,1,0:T(8,128)(2,1)}, u32[]{:S(2)}, u32[]{:S(2)}) async-start(bf16[16,512,128]{2,1,0:T(8,128)(2,1)} %shard_map.146), calls=%async_computation.3 | async-start | bytes 4194304 | tf_op jit(solution)/shard_map/all_to_all | solution.py:560
  194.0 10.2 %collective-permute-start.20 = (bf16[64,2048]{1,0:T(8,128)(2,1)S(1)}, bf16[64,2048]{1,0:T(8,128)(2,1)S(1)}, u32[]{:S(2)}, u32[]{:S(2)}) collective-permute-start(bf16[64,2048]{1,0:T(8,128)(2,1)S(1)} %fusion.6), channel_id=1, source_target_pairs={{0,1},{1,0},{2,3},{3,2},{4,5},{5,4},{6,7},{7,6},{8,9},{9,8},{10,11... | collective-permute-start | bytes 786440 | tf_op jit(solution)/shard_map/ppermute | solution.py:501
  (21 other events, 41.8 us)

commit v3 on v2

--- a/solution.py
+++ b/solution.py
@@ -10,9 +10,12 @@
 CAP = 5
 BF = jnp.bfloat16
 F32 = jnp.float32
-ALL = ("group", "dp", "head")
+ALL = ("head", "group", "dp")
+HEADS = 4
+DPS = 16
 HG = ("head", "group")
 EPSILON = 1e-06
+LIMIT = 66_400_000
 VMEM = pl.BlockSpec(memory_space=pltpu.VMEM)
 SMEM = pl.BlockSpec(memory_space=pltpu.SMEM)
 HBM = pl.BlockSpec(memory_space=pl.ANY)
@@ -55,8 +58,17 @@
         scratch[pl.ds(c, slots, stride=n), :] = values[:, c * 128 : (c + 1) * 128]
 
 
+def sections(tiles, group):
+    part = tiles // HEADS
+    return [
+        (slice(h * part, (h + 1) * part), slice((2 * h + group) * part, (2 * h + group + 1) * part))
+        for h in range(HEADS)
+    ]
+
+
 def targets_of(ids, axis):
     rows = ids.shape[1]
+    ids = (ids & (HEADS - 1)) * DPS + lax.shift_right_logical(ids, HEADS.bit_length() - 1)
     flat = [ids[k : k + 1, :].astype(F32) for k in range(2)]
     tall = [jnp.broadcast_to(f, (rows, rows)).T for f in flat]
     row_id = lax.broadcasted_iota(jnp.int32, (rows, rows), 0)
@@ -158,8 +170,9 @@
     spread(scratch, dot(picker, chosen) * scale)
     tiles = scratch[...].astype(BF)
     count = tiles.shape[0]
-    sent[:count, :] = tiles
-    sent[count:, :] = tiles
+    for group in range(2):
+        for one, every in sections(count, group):
+            sent[every, :] = tiles[one, :]
 
 
 def hidden_kernel(me, ids, tokens, mine, other, hidden, sent, scratch):
@@ -173,8 +186,9 @@
     spread(scratch, dot(picker, rows))
     tiles = scratch[...].astype(BF)
     count = tiles.shape[0]
-    sent[:count, :] = tiles
-    sent[count:, :] = tiles
+    for group in range(2):
+        for one, every in sections(count, group):
+            sent[every, :] = tiles[one, :]
 
 
 def send_grads(me, ids, gates, grad_out, experts):
@@ -208,16 +222,20 @@
     tiles = slots * n
     pieces = []
     for g in range(2):
-        scratch[...] = got[g * tiles : (g + 1) * tiles, :].astype(F32)
+        for one, every in sections(tiles, g):
+            scratch[one, :] = got[every, :].astype(F32)
         pieces.extend(scratch[pl.ds(c, slots, stride=n), :] for c in range(n))
     return jnp.concatenate(pieces, axis=1)
 
 
-def early_kernel(got_grads, w_down, in_grads, upstream, scratch, down_ref, sem):
-    copy = pltpu.make_async_copy(w_down.at[0], down_ref, sem)
+def early_kernel(got_grads, w_down, in_grads, upstream, scratch, held, down_ref, sems):
+    rows = pltpu.make_async_copy(got_grads, held, sems.at[0])
+    rows.start()
+    copy = pltpu.make_async_copy(w_down.at[0], down_ref, sems.at[1])
     copy.start()
     slots, width = in_grads.shape
-    in_grads[...] = gathered(scratch, got_grads, slots, width).astype(BF)
+    rows.wait()
+    in_grads[...] = gathered(scratch, held, slots, width).astype(BF)
     copy.wait()
     upstream[...] = dot(in_grads[...], down_ref[...], ((1,), (1,)))
 
@@ -229,10 +247,16 @@
     return call(
         early_kernel,
         (shaped((slots, width), BF), shaped((slots, inner), F32)),
-        [VMEM, HBM],
-        [pltpu.VMEM((tiles, 128), F32), pltpu.VMEM((inner, width), BF), pltpu.SemaphoreType.DMA],
+        [HBM, HBM],
+        [
+            pltpu.VMEM((tiles, 128), F32),
+            pltpu.VMEM((2 * tiles, 128), BF),
+            pltpu.VMEM((inner, width), BF),
+            pltpu.SemaphoreType.DMA((2,)),
+        ],
         flops=2 * slots * width * inner,
         moved=2 * width * inner,
+        limit=LIMIT,
     )(got_grads, w_down)
 
 
@@ -268,7 +292,8 @@
             up_grad[...], pair_ref[1, :, piece]
         )
         spread(scratch, returned)
-        sent[g * tiles : (g + 1) * tiles, :] = scratch[...].astype(BF)
+        for one, every in sections(tiles, g):
+            sent[every, :] = scratch[one, :].astype(BF)
 
 
 def experts_forward(got_hidden, upstream, gain, w_pair):
@@ -323,7 +348,8 @@
     tiles = scratch.shape[0]
     n = half // 128
     slots = tiles // n
-    scratch[...] = got[:tiles, :].astype(F32) + got[tiles:, :].astype(F32)
+    for (one, first), (_, second) in zip(sections(tiles, 0), sections(tiles, 1)):
+        scratch[one, :] = got[first, :].astype(F32) + got[second, :].astype(F32)
     values = jnp.concatenate(
         [scratch[pl.ds(c, slots, stride=n), :] for c in range(n)], axis=1
     ).astype(BF)
@@ -460,7 +486,7 @@
         [pltpu.VMEM(got.shape, BF), pltpu.SemaphoreType.DMA((got.shape[0],))],
         flops=got.size,
         moved=got.size * 2,
-        limit=65_000_000,
+        limit=LIMIT,
     )(got)
 
 

time: 226 us -> 224 us (level)
  starting transfers between devices: 43 us -> 46.1 us
    unnamed x52 -> x54, local copies, waits for them, and re-layouts: 8.86 us -> 7.81 us
  transfers between devices with their start and end apart: 27 -> 27, of which waited for: 8 -> 9; matrix products, arithmetic and copies ran while one was open for 2% -> 2% of each run, Pallas kernels for 17% -> 17%
where the time goes in v3:
time: 224 us; the launch traced here: 223 us
  waiting for transfers between devices  74.8 us (33%)
  Pallas kernels  57 us (25%)
  starting transfers between devices  46.1 us (21%)
  blocking collectives  31 us (14%)
  local copies, waits for them, and re-layouts  9.48 us (4%)
  other arithmetic  3.7 us (2%)
    ppermute x22, waiting for transfers between devices, swap(): return lax.ppermute(x, HG, [(i, i ^ flip) for i in range(8)])  39.2 us
    all_to_all x1, blocking collectives, exchange(): return lax.all_to_all(tiles, ALL, 0, 0, tiled=True).reshape(-1, 128)  31 us
    ppermute x22, starting transfers between devices, swap(): return lax.ppermute(x, HG, [(i, i ^ flip) for i in range(8)])  21.8 us
    all_to_all x2, waiting for transfers between devices, exchange(): return lax.all_to_all(tiles, ALL, 0, 0, tiled=True).reshape(-1, 128)  18.2 us
    all_to_all x1, waiting for transfers between devices, body(): got = lax.all_to_all(sent, 'dp', 0, 0, tiled=True)  17.4 us
    all_to_all x2, starting transfers between devices, exchange(): return lax.all_to_all(tiles, ALL, 0, 0, tiled=True).reshape(-1, 128)  16.9 us
    pallas_call x1, Pallas kernels, experts_forward(): call(expert_kernel, (shaped((2 * tiles, 128), BF), row, unit, unit, unit)...  9.92 us
    pallas_call x1, Pallas kernels, expert_grads(): pl.pallas_call(expert_grads_kernel, out_shape=(shaped((1, 2, inner, width...  7.96 us
  transfers between devices with their start and end apart: 27, of which 9 were waited for; matrix products, arithmetic and copies ran while one was open for 2% of the time, Pallas kernels for 17%

profile of v3, /device:TPU:0, one launch (start us, length us, event | category | flops | bytes accessed | tf_op | source)
XLA Modules:
  0.0 223.2 jit_solution(12841876601865787374)
XLA Ops:
  0.6 1.7 collective-permute-start.1
  2.9 2.7 %shard_map.140 = bf16[5120,128]{1,0:T(8,128)(2,1)} custom-call(s32[2]{0:T(128)} %pad_add_fusion.me, s32[2,128]{1,0:T(2,128)} %bitcast.20, f32[2,128]{1,0:T(2,128)} %bitcast.25, bf16[128,2048]{1,0:T(8,128)(2,1)} %grad_out.3), custom_call_target="tpu_custom_call" | custom-call | flops 83886080 | bytes 1310720 | tf_op jit(solution)/shard_map/pallas_call | solution.py:197
  5.6 11.2 %all-to-all-start = ((bf16[128,40,128]{2,1,0:T(8,128)(2,1)}), bf16[128,40,128]{2,1,0:T(8,128)(2,1)}, u32[]{:S(2)}, u32[]{:S(2)}) async-start(bf16[128,40,128]{2,1,0:T(8,128)(2,1)} %bitcast.14), calls=%async_computation | async-start | bytes 2621440 | tf_op jit(solution)/shard_map/all_to_all | solution.py:540
  18.5 24.5 %collective-permute-done.7.w2 = bf16[128,2048]{1,0:T(8,128)(2,1)S(1)} collective-permute-done((bf16[128,2048]{1,0:T(8,128)(2,1)S(1)}, bf16[128,2048]{1,0:T(8,128)(2,1)S(1)}, u32[]{:S(2)}, u32[]{:S(2)}) %collective-permute-start.7) | collective-permute-done | bytes 524320 | tf_op jit(solution)/shard_map/ppermute | solution.py:527
  44.6 6.1 %shard_map.137 = (bf16[512,128]{1,0:T(8,128)(2,1)}, bf16[512,128]{1,0:T(8,128)(2,1)}, bf16[512,128]{1,0:T(8,128)(2,1)}, f32[512,512]{1,0:T(8,128)}, bf16[128,128...) custom-call(s32[2]{0:T(128)} %pad_add_fusion.me, ...), custom_call_target="tpu_custom_call" | custom-call | flops 939524096 | bytes 6815744 | tf_op jit(solution)/shard_map/pallas_call | solution.py:123
  52.7 2.8 %collective-permute-done.4.m2 = bf16[128,128]{1,0:T(8,128)(2,1)S(1)} collective-permute-done((bf16[128,128]{1,0:T(8,128)(2,1)}, bf16[128,128]{1,0:T(8,128)(2,1)S(1)}, u32[]{:S(2)}, u32[]{:S(2)}) %collective-permute-start.4) | collective-permute-done | bytes 32800 | tf_op jit(solution)/shard_map/ppermute | solution.py:527
  56.1 3.2 %shard_map.138 = (f32[128,1024]{1,0:T(8,128)}, bf16[128,1024]{1,0:T(8,128)(2,1)}) custom-call(s32[2]{0:T(128)} %pad_add_fusion.me, bf16[128,128]{1,0:T(8,128)(2,1)} %get-tuple-element.44.m0, bf16[128,128]{1,0:T(8,128)(2,1)} %copy-done.21, bf16[128,128]{1,0:T(8,128)(2,1)} %copy-done.22, bf16[128,128]{1,0:T(8,128)(2,1)} %copy-done.23, bf16[128,2048]{1,0:T(8,128)(2,1)} %w0.3, ...), custom_call_target="tpu_custom_call" | custom-call | flops 268435456 | bytes 2097152 | tf_op jit(solution)/shard_map/pallas_call | solution.py:150
  59.3 3.1 %collective-permute-start.9 = (bf16[128,1024]{1,0:T(8,128)(2,1)}, bf16[128,1024]{1,0:T(8,128)(2,1)S(1)}, u32[]{:S(2)}, u32[]{:S(2)}) collective-permute-start(bf16[128,1024]{1,0:T(8,128)(2,1)} %get-tuple-element.49), channel_id=1, source_target_pairs={{0,1},{1,0},{2,3},{3,2},{4,5},{5,4},{6,7},{7,6},{8,9},{9,8},{10,11... | collective-permute-start | bytes 786440 | tf_op jit(solution)/shard_map/ppermute | solution.py:527
  62.4 4.4 %shard_map.141 = (bf16[320,2048]{1,0:T(8,128)(2,1)}, f32[320,704]{1,0:T(8,128)}) custom-call(bf16[5120,128]{1,0:T(8,128)(2,1)} %bitcast.6.got_grads, bf16[1,704,2048]{2,1,0:T(8,128)(2,1)} %w_down.1), custom_call_target="tpu_custom_call" | custom-call | flops 922746880 | bytes 2883584 | tf_op jit(solution)/shard_map/pallas_call | solution.py:247
  66.9 2.5 %collective-permute-done.9.other = bf16[128,1024]{1,0:T(8,128)(2,1)S(1)} collective-permute-done((bf16[128,1024]{1,0:T(8,128)(2,1)}, bf16[128,1024]{1,0:T(8,128)(2,1)S(1)}, u32[]{:S(2)}, u32[]{:S(2)}) %collective-permute-start.9) | collective-permute-done | bytes 262176 | tf_op jit(solution)/shard_map/ppermute | solution.py:527
  70.1 2.9 %shard_map.139 = (bf16[128,1024]{1,0:T(8,128)(2,1)}, bf16[5120,128]{1,0:T(8,128)(2,1)}) custom-call(s32[2]{0:T(128)} %pad_add_fusion.me, s32[2,128]{1,0:T(2,128)} %bitcast.21, bf16[128,2048]{1,0:T(8,128)(2,1)} %tokens.1, f32[128,1024]{1,0:T(8,128)} %get-tuple-element.48.mine, bf16[128,1024]{1,0:T(8,128)(2,1)} %copy-done.16), custom_call_target="tpu_custom_call" | custom-call | flops 83886080 | bytes 1310720 | tf_op jit(solution)/shard_map/pallas_call | solution.py:210
  73.1 31.0 %all_to_all.20 = bf16[128,40,128]{2,1,0:T(8,128)(2,1)} all-to-all(bf16[128,40,128]{2,1,0:T(8,128)(2,1)} %bitcast.18), channel_id=1, replica_groups=mesh['dp'=16,'head'=4,'group'=2] {'head','group','dp'}, dimensions={0} | all-to-all | bytes 2621440 | tf_op jit(solution)/shard_map/all_to_all | solution.py:540
  104.1 9.9 %shard_map.142 = (bf16[5120,128]{1,0:T(8,128)(2,1)}, bf16[320,2048]{1,0:T(8,128)(2,1)}, bf16[320,704]{1,0:T(8,128)(2,1)}, bf16[320,704]{1,0:T(8,128)(2,1)}, bf16[320,704]{1,0:T(8,128)(2,1)}) custom-call(bf16[5120,128]{1,0:T(8,128)(2,1)} %bitcast.17, f32[320,704]{1,0:T(8,128)} %get-tuple-element.56.upstream_ref, f32[1,2048]{1,0:T(1,128)} %bitcast.23, ...), custom_call_target="tpu_custom_call" | custom-call | flops 3690987520 | bytes 5767168 | tf_op jit(solution)/shard_map/pallas_call | solution.py:304
  114.0 5.7 %all-to-all-start.2 = ((bf16[128,40,128]{2,1,0:T(8,128)(2,1)}), bf16[128,40,128]{2,1,0:T(8,128)(2,1)S(1)}, u32[]{:S(2)}, u32[]{:S(2)}) async-start(bf16[128,40,128]{2,1,0:T(8,128)(2,1)} %bitcast.16), calls=%async_computation.2 | async-start | bytes 2621440 | tf_op jit(solution)/shard_map/all_to_all | solution.py:540
  119.7 2.5 %collective-permute-start.10 = (bf16[128,1024]{1,0:T(8,128)(2,1)S(1)}, bf16[128,1024]{1,0:T(8,128)(2,1)S(1)}, u32[]{:S(2)}, u32[]{:S(2)}) collective-permute-start(bf16[128,1024]{1,0:T(8,128)(2,1)S(1)} %copy-done.17), channel_id=1, source_target_pairs={{0,1},{1,0},{2,3},{3,2},{4,5},{5,4},{6,7},{7,6},{8,9},{9,8},{10,11... | collective-permute-start | bytes 786440 | tf_op jit(solution)/shard_map/ppermute | solution.py:527
  122.2 18.2 %all-to-all-done.2 = bf16[128,40,128]{2,1,0:T(8,128)(2,1)S(1)} async-done(((bf16[128,40,128]{2,1,0:T(8,128)(2,1)}), bf16[128,40,128]{2,1,0:T(8,128)(2,1)S(1)}, u32[]{:S(2)}, u32[]{:S(2)}) %all-to-all-start.2) | async-done | bytes 1310752 | tf_op jit(solution)/shard_map/all_to_all | solution.py:540
  140.4 1.1 copy-done.2
  141.4 2.7 %shard_map.143.normed_mine = bf16[128,1024]{1,0:T(8,128)(2,1)} custom-call(s32[2,128]{1,0:T(2,128)} %bitcast.22, bf16[5120,128]{1,0:T(8,128)(2,1)} %bitcast.15), custom_call_target="tpu_custom_call" | custom-call | flops 83886080 | bytes 1310720 | tf_op jit(solution)/shard_map/pallas_call | solution.py:365
  144.1 2.6 %collective-permute-start.11 = (bf16[128,1024]{1,0:T(8,128)(2,1)}, bf16[128,1024]{1,0:T(8,128)(2,1)S(1)}, u32[]{:S(2)}, u32[]{:S(2)}) collective-permute-start(bf16[128,1024]{1,0:T(8,128)(2,1)} %shard_map.143.normed_mine), channel_id=1, source_target_pairs={{0,1},{1,0},{2,3},{3,2},{4,5},{5,4},{6,7},{7,6},{8,9},{9,8},{10,11... | collective-permute-start | bytes 786440 | tf_op jit(solution)/shard_map/ppermute | solution.py:527
  146.7 6.8 %collective-permute-done.11.normed_other = bf16[128,1024]{1,0:T(8,128)(2,1)S(1)} collective-permute-done((bf16[128,1024]{1,0:T(8,128)(2,1)}, bf16[128,1024]{1,0:T(8,128)(2,1)S(1)}, u32[]{:S(2)}, u32[]{:S(2)}) %collective-permute-start.11) | collective-permute-done | bytes 262176 | tf_op jit(solution)/shard_map/ppermute | solution.py:527
  154.2 3.9 %shard_map.144 = (f32[128,2048]{1,0:T(8,128)}, bf16[128,2048]{1,0:T(8,128)(2,1)}, bf16[128,128]{1,0:T(8,128)(2,1)}, bf16[128,128]{1,0:T(8,128)(2,1)}, bf16[128,1...) custom-call(s32[2]{0:T(128)} %pad_add_fusion.me, bf16[128,2048]{1,0:T(8,128)(2,1)} %grad_out.3, ...), custom_call_target="tpu_custom_call" | custom-call | flops 268435456 | bytes 4718592 | tf_op jit(solution)/shard_map/pallas_call | solution.py:400
  160.9 1.5 collective-permute-done.13.g2
  163.4 5.6 %shard_map.145 = (bf16[512,384]{1,0:T(8,128)(2,1)}, f32[128,2048]{1,0:T(8,128)}, f32[128,2048]{1,0:T(8,128)}, bf16[128,2048]{1,0:T(8,128)(2,1)}, bf16[128,2048]{1,0:T(8,128)(2,1)}) custom-call(bf16[128,128]{1,0:T(8,128)(2,1)} %get-tuple-element.59.g0, bf16[128,128]{1,0:T(8,128)(2,1)} %copy-done.24, bf16[128,128]{1,0:T(8,128)(2,1)} %copy-done.25, ...), custom_call_target="tpu_custom_call" | custom-call | flops 1073741824 | bytes 5767168 | tf_op jit(solution)/shard_map/pallas_call | solution.py:433
  171.2 1.4 convert_add_fusion
  173.5 1.8 collective-permute-start.19
  176.8 2.3 %collective-permute-start.16 = (bf16[64,2048]{1,0:T(8,128)(2,1)}, bf16[64,2048]{1,0:T(8,128)(2,1)S(1)}, u32[]{:S(2)}, u32[]{:S(2)}) collective-permute-start(bf16[64,2048]{1,0:T(8,128)(2,1)} %dynamic-slice_convert_fusion.2), channel_id=1, source_target_pairs={{0,1},{1,0},{2,3},{3,2},{4,5},{5,4},{6,7},{7,6},{8,9},{9,8},{10,11... | collective-permute-start | bytes 786440 | tf_op jit(solution)/shard_map/ppermute | solution.py:527
  180.7 5.0 %shard_map.146 = bf16[16,512,128]{2,1,0:T(8,128)(2,1)} custom-call(bf16[512,384]{1,0:T(8,128)(2,1)} %get-tuple-element.71.acts, bf16[512,2048]{1,0:T(8,128)(2,1)} %get-tuple-element.72.normed, bf16[128,128]{1,0:T(8,128)(2,1)} %get-tuple-element.44.m0, bf16[128,128]{1,0:T(8,128)(2,1)} %get-tuple-element.45.m1, bf16[128,128]{1,0:T(8,128)(2,1)} %get-tuple-element.46.m2, ...), custom_call_target="tpu_custom_call" | custom-call | flops 1073741824 | bytes 6291456 | tf_op jit(solution)/shard_map/pallas_call | solution.py:456
  185.6 4.8 %all-to-all-start.3 = ((bf16[16,512,128]{2,1,0:T(8,128)(2,1)}), bf16[16,512,128]{2,1,0:T(8,128)(2,1)}, u32[]{:S(2)}, u32[]{:S(2)}) async-start(bf16[16,512,128]{2,1,0:T(8,128)(2,1)} %shard_map.146), calls=%async_computation.3 | async-start | bytes 4194304 | tf_op jit(solution)/shard_map/all_to_all | solution.py:586
  192.0 2.2 %collective-permute-start.20 = (bf16[64,2048]{1,0:T(8,128)(2,1)S(1)}, bf16[64,2048]{1,0:T(8,128)(2,1)S(1)}, u32[]{:S(2)}, u32[]{:S(2)}) collective-permute-start(bf16[64,2048]{1,0:T(8,128)(2,1)S(1)} %fusion.6), channel_id=1, source_target_pairs={{0,1},{1,0},{2,3},{3,2},{4,5},{5,4},{6,7},{7,6},{8,9},{9,8},{10,11... | collective-permute-start | bytes 786440 | tf_op jit(solution)/shard_map/ppermute | solution.py:527
  194.2 8.0 %shard_map.148 = (bf16[1,2,704,2048]{3,2,1,0:T(8,128)(2,1)}, bf16[1,704,2048]{2,1,0:T(8,128)(2,1)}) custom-call(bf16[320,2048]{1,0:T(8,128)(2,1)} %get-tuple-element.76.in_rows, bf16[320,2048]{1,0:T(8,128)(2,1)} %get-tuple-element.77.in_grads, bf16[320,704]{1,0:T(8,128)(2,1)} %get-tuple-element.78.product, bf16[320,704]{1,0:T(8,128)(2,1)} %get-tuple-element.79.gate_grad, ...), custom_call_target="tpu_custom_call" | custom-call | flops 2768240640 | bytes 8650752 | tf_op jit(solution)/shard_map/pallas_call | solution.py:331
  203.1 17.4 %all-to-all-done.3.got = bf16[16,512,128]{2,1,0:T(8,128)(2,1)} async-done(((bf16[16,512,128]{2,1,0:T(8,128)(2,1)}), bf16[16,512,128]{2,1,0:T(8,128)(2,1)}, u32[]{:S(2)}, u32[]{:S(2)}) %all-to-all-start.3) | async-done | bytes 2097184 | tf_op jit(solution)/shard_map/all_to_all | solution.py:586
  220.4 2.5 %shard_map.147 = (f32[3,128,128]{2,1,0:T(8,128)}, f32[128,128]{1,0:T(8,128)}) custom-call(bf16[16,512,128]{2,1,0:T(8,128)(2,1)} %all-to-all-done.3.got), custom_call_target="tpu_custom_call" | custom-call | flops 1048576 | bytes 2097152 | tf_op jit(solution)/shard_map/pallas_call | solution.py:482
  (101 shorter events, 20.0 us)
Async XLA Ops:
  0.6 17.2 %collective-permute-start.1 = (bf16[128,2048]{1,0:T(8,128)(2,1)}, bf16[128,2048]{1,0:T(8,128)(2,1)S(1)}, u32[]{:S(2)}, u32[]{:S(2)}) collective-permute-start(bf16[128,2048]{1,0:T(8,128)(2,1)} %tokens.1), channel_id=1, source_target_pairs={{0,4},{1,5},{2,7},{3,6},{4,0},{5,1},{6,3},{7,2},{8,12},{9,13},{10,... | collective-permute-start | bytes 1572872 | tf_op jit(solution)/shard_map/ppermute | solution.py:532
  5.6 11.2 %copy-start.3 = (bf16[128,2048]{1,0:T(8,128)(2,1)S(1)}, bf16[128,2048]{1,0:T(8,128)(2,1)}, u32[]{:S(2)}) copy-start(bf16[128,2048]{1,0:T(8,128)(2,1)} %w0.3) | copy-start | bytes 1572868
  5.6 12.2 %copy-start = (bf16[128,2048]{1,0:T(8,128)(2,1)S(1)}, bf16[128,2048]{1,0:T(8,128)(2,1)}, u32[]{:S(2)}) copy-start(bf16[128,2048]{1,0:T(8,128)(2,1)} %tokens.1) | copy-start | bytes 1572868
  5.6 56.8 %all-to-all-start = ((bf16[128,40,128]{2,1,0:T(8,128)(2,1)}), bf16[128,40,128]{2,1,0:T(8,128)(2,1)}, u32[]{:S(2)}, u32[]{:S(2)}) async-start(bf16[128,40,128]{2,1,0:T(8,128)(2,1)} %bitcast.14), calls=%async_computation | async-start | bytes 2621440 | tf_op jit(solution)/shard_map/all_to_all | solution.py:540
  16.9 26.1 %collective-permute-start.7 = (bf16[128,2048]{1,0:T(8,128)(2,1)S(1)}, bf16[128,2048]{1,0:T(8,128)(2,1)S(1)}, u32[]{:S(2)}, u32[]{:S(2)}) collective-permute-start(bf16[128,2048]{1,0:T(8,128)(2,1)S(1)} %copy-done.3), channel_id=1, source_target_pairs={{0,4},{1,5},{2,6},{3,7},{4,0},{5,1},{6,2},{7,3},{8,12},{9,13},{10,... | collective-permute-start | bytes 1572872 | tf_op jit(solution)/shard_map/ppermute | solution.py:527
  17.9 25.1 %collective-permute-start = (bf16[128,2048]{1,0:T(8,128)(2,1)S(1)}, bf16[128,2048]{1,0:T(8,128)(2,1)S(1)}, u32[]{:S(2)}, u32[]{:S(2)}) collective-permute-start(bf16[128,2048]{1,0:T(8,128)(2,1)S(1)} %copy-done), channel_id=1, source_target_pairs={{0,2},{1,3},{2,0},{3,1},{4,6},{5,7},{6,4},{7,5},{8,10},{9,11},{10,... | collective-permute-start | bytes 1572872 | tf_op jit(solution)/shard_map/ppermute | solution.py:527
  17.9 26.7 %copy-start.8 = (bf16[128,2048]{1,0:T(8,128)(2,1)}, bf16[128,2048]{1,0:T(8,128)(2,1)S(1)}, u32[]{:S(2)}) copy-start(bf16[128,2048]{1,0:T(8,128)(2,1)S(1)} %collective-permute-done.1.t2) | copy-start | bytes 1572868
  17.9 25.1 %collective-permute-start.2 = (bf16[128,2048]{1,0:T(8,128)(2,1)S(1)}, bf16[128,2048]{1,0:T(8,128)(2,1)S(1)}, u32[]{:S(2)}, u32[]{:S(2)}) collective-permute-start(bf16[128,2048]{1,0:T(8,128)(2,1)S(1)} %collective-permute-done.1.t2), channel_id=1, source_target_pairs={{0,2},{1,3},{2,0},{3,1},{4,6},{5,7},{6,4},{7,5},{8,10},{9,11},{10,... | collective-permute-start | bytes 1572872 | tf_op jit(solution)/shard_map/ppermute | solution.py:527
  18.4 34.3 %collective-permute-start.6 = (bf16[128,2048]{1,0:T(8,128)(2,1)S(1)}, bf16[128,2048]{1,0:T(8,128)(2,1)S(1)}, u32[]{:S(2)}, u32[]{:S(2)}) collective-permute-start(bf16[128,2048]{1,0:T(8,128)(2,1)S(1)} %copy-done.3), channel_id=1, source_target_pairs={{0,2},{1,3},{2,0},{3,1},{4,6},{5,7},{6,4},{7,5},{8,10},{9,11},{10,... | collective-permute-start | bytes 1572872 | tf_op jit(solution)/shard_map/ppermute | solution.py:527
  42.9 7.8 %copy-start.4 = (bf16[128,2048]{1,0:T(8,128)(2,1)}, bf16[128,2048]{1,0:T(8,128)(2,1)S(1)}, u32[]{:S(2)}) copy-start(bf16[128,2048]{1,0:T(8,128)(2,1)S(1)} %collective-permute-done.7.w2) | copy-start | bytes 1572868
  42.9 9.7 %collective-permute-start.8 = (bf16[128,2048]{1,0:T(8,128)(2,1)S(1)}, bf16[128,2048]{1,0:T(8,128)(2,1)S(1)}, u32[]{:S(2)}, u32[]{:S(2)}) collective-permute-start(bf16[128,2048]{1,0:T(8,128)(2,1)S(1)} %collective-permute-done.7.w2), channel_id=1, source_target_pairs={{0,2},{1,3},{2,0},{3,1},{4,6},{5,7},{6,4},{7,5},{8,10},{9,11},{10,... | collective-permute-start | bytes 1572872 | tf_op jit(solution)/shard_map/ppermute | solution.py:527
  50.7 1.9 collective-permute-start.3
  51.2 4.3 %collective-permute-start.4 = (bf16[128,128]{1,0:T(8,128)(2,1)}, bf16[128,128]{1,0:T(8,128)(2,1)S(1)}, u32[]{:S(2)}, u32[]{:S(2)}) collective-permute-start(bf16[128,128]{1,0:T(8,128)(2,1)} %get-tuple-element.46.m2), channel_id=1, source_target_pairs={{0,4},{1,5},{2,6},{3,7},{4,0},{5,1},{6,2},{7,3},{8,12},{9,13},{10,... | collective-permute-start | bytes 98312 | tf_op jit(solution)/shard_map/ppermute | solution.py:527
  51.6 3.9 %collective-permute-start.5 = (bf16[128,128]{1,0:T(8,128)(2,1)}, bf16[128,128]{1,0:T(8,128)(2,1)S(1)}, u32[]{:S(2)}, u32[]{:S(2)}) collective-permute-start(bf16[128,128]{1,0:T(8,128)(2,1)} %get-tuple-element.47.m3), channel_id=1, source_target_pairs={{0,6},{1,7},{2,4},{3,5},{4,2},{5,3},{6,0},{7,1},{8,14},{9,15},{10,... | collective-permute-start | bytes 98312 | tf_op jit(solution)/shard_map/ppermute | solution.py:527
  59.3 10.1 %collective-permute-start.9 = (bf16[128,1024]{1,0:T(8,128)(2,1)}, bf16[128,1024]{1,0:T(8,128)(2,1)S(1)}, u32[]{:S(2)}, u32[]{:S(2)}) collective-permute-start(bf16[128,1024]{1,0:T(8,128)(2,1)} %get-tuple-element.49), channel_id=1, source_target_pairs={{0,1},{1,0},{2,3},{3,2},{4,5},{5,4},{6,7},{7,6},{8,9},{9,8},{10,11... | collective-permute-start | bytes 786440 | tf_op jit(solution)/shard_map/ppermute | solution.py:527
  114.0 26.4 %all-to-all-start.2 = ((bf16[128,40,128]{2,1,0:T(8,128)(2,1)}), bf16[128,40,128]{2,1,0:T(8,128)(2,1)S(1)}, u32[]{:S(2)}, u32[]{:S(2)}) async-start(bf16[128,40,128]{2,1,0:T(8,128)(2,1)} %bitcast.16), calls=%async_computation.2 | async-start | bytes 2621440 | tf_op jit(solution)/shard_map/all_to_all | solution.py:540
  119.7 27.0 %collective-permute-start.10 = (bf16[128,1024]{1,0:T(8,128)(2,1)S(1)}, bf16[128,1024]{1,0:T(8,128)(2,1)S(1)}, u32[]{:S(2)}, u32[]{:S(2)}) collective-permute-start(bf16[128,1024]{1,0:T(8,128)(2,1)S(1)} %copy-done.17), channel_id=1, source_target_pairs={{0,1},{1,0},{2,3},{3,2},{4,5},{5,4},{6,7},{7,6},{8,9},{9,8},{10,11... | collective-permute-start | bytes 786440 | tf_op jit(solution)/shard_map/ppermute | solution.py:527
  144.1 9.4 %collective-permute-start.11 = (bf16[128,1024]{1,0:T(8,128)(2,1)}, bf16[128,1024]{1,0:T(8,128)(2,1)S(1)}, u32[]{:S(2)}, u32[]{:S(2)}) collective-permute-start(bf16[128,1024]{1,0:T(8,128)(2,1)} %shard_map.143.normed_mine), channel_id=1, source_target_pairs={{0,1},{1,0},{2,3},{3,2},{4,5},{5,4},{6,7},{7,6},{8,9},{9,8},{10,11... | collective-permute-start | bytes 786440 | tf_op jit(solution)/shard_map/ppermute | solution.py:527
  146.7 6.8 %copy-start.18 = (bf16[128,1024]{1,0:T(8,128)(2,1)}, bf16[128,1024]{1,0:T(8,128)(2,1)S(1)}, u32[]{:S(2)}) copy-start(bf16[128,1024]{1,0:T(8,128)(2,1)S(1)} %collective-permute-done.10.hidden_other) | copy-start | bytes 786436
  158.1 2.8 %collective-permute-start.12 = (bf16[128,128]{1,0:T(8,128)(2,1)}, bf16[128,128]{1,0:T(8,128)(2,1)S(1)}, u32[]{:S(2)}, u32[]{:S(2)}) collective-permute-start(bf16[128,128]{1,0:T(8,128)(2,1)} %get-tuple-element.60), channel_id=1, source_target_pairs={{0,2},{1,3},{2,0},{3,1},{4,6},{5,7},{6,4},{7,5},{8,10},{9,11},{10,... | collective-permute-start | bytes 98312 | tf_op jit(solution)/shard_map/ppermute | solution.py:527
  158.2 4.3 %collective-permute-start.13 = (bf16[128,128]{1,0:T(8,128)(2,1)}, bf16[128,128]{1,0:T(8,128)(2,1)S(1)}, u32[]{:S(2)}, u32[]{:S(2)}) collective-permute-start(bf16[128,128]{1,0:T(8,128)(2,1)} %get-tuple-element.61), channel_id=1, source_target_pairs={{0,4},{1,5},{2,6},{3,7},{4,0},{5,1},{6,2},{7,3},{8,12},{9,13},{10,... | collective-permute-start | bytes 98312 | tf_op jit(solution)/shard_map/ppermute | solution.py:527
  159.1 3.7 %collective-permute-start.14 = (bf16[128,128]{1,0:T(8,128)(2,1)}, bf16[128,128]{1,0:T(8,128)(2,1)S(1)}, u32[]{:S(2)}, u32[]{:S(2)}) collective-permute-start(bf16[128,128]{1,0:T(8,128)(2,1)} %get-tuple-element.62), channel_id=1, source_target_pairs={{0,6},{1,7},{2,4},{3,5},{4,2},{5,3},{6,0},{7,1},{8,14},{9,15},{10,... | collective-permute-start | bytes 98312 | tf_op jit(solution)/shard_map/ppermute | solution.py:527
  160.0 10.1 %collective-permute-start.22 = (bf16[128,2048]{1,0:T(8,128)(2,1)}, bf16[128,2048]{1,0:T(8,128)(2,1)S(1)}, u32[]{:S(2)}, u32[]{:S(2)}) collective-permute-start(bf16[128,2048]{1,0:T(8,128)(2,1)} %get-tuple-element.73.g0), channel_id=1, source_target_pairs={{0,4},{1,5},{2,7},{3,6},{4,0},{5,1},{6,3},{7,2},{8,12},{9,13},{10,... | collective-permute-start | bytes 1572872 | tf_op jit(solution)/shard_map/ppermute | solution.py:532
  169.0 2.1 collective-permute-start.17
  169.3 9.8 %collective-permute-start.21 = (bf16[128,2048]{1,0:T(8,128)(2,1)S(1)}, bf16[128,2048]{1,0:T(8,128)(2,1)S(1)}, u32[]{:S(2)}, u32[]{:S(2)}) collective-permute-start(bf16[128,2048]{1,0:T(8,128)(2,1)S(1)} %copy-done.11), channel_id=1, source_target_pairs={{0,2},{1,3},{2,0},{3,1},{4,6},{5,7},{6,4},{7,5},{8,10},{9,11},{10,... | collective-permute-start | bytes 1572872 | tf_op jit(solution)/shard_map/ppermute | solution.py:527
  170.0 5.9 %collective-permute-start.15 = (bf16[128,2048]{1,0:T(8,128)(2,1)}, bf16[128,2048]{1,0:T(8,128)(2,1)S(1)}, u32[]{:S(2)}, u32[]{:S(2)}) collective-permute-start(bf16[128,2048]{1,0:T(8,128)(2,1)} %get-tuple-element.68), channel_id=1, source_target_pairs={{0,2},{1,3},{2,0},{3,1},{4,6},{5,7},{6,4},{7,5},{8,10},{9,11},{10,... | collective-permute-start | bytes 1572872 | tf_op jit(solution)/shard_map/ppermute | solution.py:527
  170.1 9.0 %collective-permute-start.23 = (bf16[128,2048]{1,0:T(8,128)(2,1)S(1)}, bf16[128,2048]{1,0:T(8,128)(2,1)S(1)}, u32[]{:S(2)}, u32[]{:S(2)}) collective-permute-start(bf16[128,2048]{1,0:T(8,128)(2,1)S(1)} %collective-permute-done.22.g2), channel_id=1, source_target_pairs={{0,2},{1,3},{2,0},{3,1},{4,6},{5,7},{6,4},{7,5},{8,10},{9,11},{10,... | collective-permute-start | bytes 1572872 | tf_op jit(solution)/shard_map/ppermute | solution.py:527
  173.5 17.0 %collective-permute-start.19 = (bf16[64,2048]{1,0:T(8,128)(2,1)}, bf16[64,2048]{1,0:T(8,128)(2,1)S(1)}, u32[]{:S(2)}, u32[]{:S(2)}) collective-permute-start(bf16[64,2048]{1,0:T(8,128)(2,1)} %get-tuple-element.86), channel_id=1, source_target_pairs={{0,5},{1,4},{2,7},{3,6},{4,1},{5,0},{6,3},{7,2},{8,13},{9,12},{10,... | collective-permute-start | bytes 786440 | tf_op jit(solution)/shard_map/ppermute | solution.py:527
  175.2 15.3 %collective-permute-start.18 = (bf16[64,2048]{1,0:T(8,128)(2,1)}, bf16[64,2048]{1,0:T(8,128)(2,1)S(1)}, u32[]{:S(2)}, u32[]{:S(2)}) collective-permute-start(bf16[64,2048]{1,0:T(8,128)(2,1)} %get-tuple-element.85), channel_id=1, source_target_pairs={{0,4},{1,5},{2,6},{3,7},{4,0},{5,1},{6,2},{7,3},{8,12},{9,13},{10,... | collective-permute-start | bytes 786440 | tf_op jit(solution)/shard_map/ppermute | solution.py:527
  176.8 13.7 %collective-permute-start.16 = (bf16[64,2048]{1,0:T(8,128)(2,1)}, bf16[64,2048]{1,0:T(8,128)(2,1)S(1)}, u32[]{:S(2)}, u32[]{:S(2)}) collective-permute-start(bf16[64,2048]{1,0:T(8,128)(2,1)} %dynamic-slice_convert_fusion.2), channel_id=1, source_target_pairs={{0,1},{1,0},{2,3},{3,2},{4,5},{5,4},{6,7},{7,6},{8,9},{9,8},{10,11... | collective-permute-start | bytes 786440 | tf_op jit(solution)/shard_map/ppermute | solution.py:527
  185.6 34.8 %all-to-all-start.3 = ((bf16[16,512,128]{2,1,0:T(8,128)(2,1)}), bf16[16,512,128]{2,1,0:T(8,128)(2,1)}, u32[]{:S(2)}, u32[]{:S(2)}) async-start(bf16[16,512,128]{2,1,0:T(8,128)(2,1)} %shard_map.146), calls=%async_computation.3 | async-start | bytes 4194304 | tf_op jit(solution)/shard_map/all_to_all | solution.py:586
  192.0 10.2 %collective-permute-start.20 = (bf16[64,2048]{1,0:T(8,128)(2,1)S(1)}, bf16[64,2048]{1,0:T(8,128)(2,1)S(1)}, u32[]{:S(2)}, u32[]{:S(2)}) collective-permute-start(bf16[64,2048]{1,0:T(8,128)(2,1)S(1)} %fusion.6), channel_id=1, source_target_pairs={{0,1},{1,0},{2,3},{3,2},{4,5},{5,4},{6,7},{7,6},{8,9},{9,8},{10,11... | collective-permute-start | bytes 786440 | tf_op jit(solution)/shard_map/ppermute | solution.py:527
  (22 other events, 50.2 us)

commit v4 on v3

--- a/solution.py
+++ b/solution.py
@@ -527,8 +527,8 @@
     return lax.ppermute(x, HG, [(i, i ^ flip) for i in range(8)])
 
 
-def sequence(x):
-    pairs = [(i, i ^ 4 ^ (i >> 1 & 1)) for i in range(8)]
+def sequence(x, split):
+    pairs = [(i, i ^ 4 ^ (i >> 1 & 1 if split else 1)) for i in range(8)]
     far = lax.ppermute(x, HG, pairs)
     core = swap(x, 1, 0)
     return [x, core, far, swap(far, 1, 0)]
@@ -551,7 +551,7 @@
     w_pair = w_gate_up.transpose(0, 1, 3, 2)
     ids, gates = ids.T, gates.T
 
-    blocks = sequence(tokens)
+    blocks = sequence(tokens, False)
     tiles = send_grads(me, ids, gates, grad_out, experts)
     got_grads = exchange(tiles)
     w_far = swap(w_attn_out, 2, 0)
@@ -577,7 +577,7 @@
     grad_hidden, rounded, *grads = hidden_grad(
         me, grad_out, halves, gain_ffn, weights)
     grads = [grads[0]] + [swap(grads[k], k, 0) for k in range(1, 4)]
-    all_grads = sequence(rounded)
+    all_grads = sequence(rounded, True)
 
     acts, near, far, near_out, far_out = attention_back(grads, query, key, value, chances, w_qkv)
     near_in = swap(near_out, 1, 0)

time: 224 us -> 223 us (level)
  no operation moved by 1% of the time
where the time goes in v4:
time: 223 us
  waiting for transfers between devices  74.8 us (34%)
  Pallas kernels  57 us (26%)
  starting transfers between devices  45.5 us (20%)
  blocking collectives  31 us (14%)
  local copies, waits for them, and re-layouts  9.48 us (4%)
  other arithmetic  3.7 us (2%)
    ppermute x22, waiting for transfers between devices, swap(): return lax.ppermute(x, HG, [(i, i ^ flip) for i in range(8)])  39.2 us
    all_to_all x1, blocking collectives, exchange(): return lax.all_to_all(tiles, ALL, 0, 0, tiled=True).reshape(-1, 128)  31 us
    ppermute x22, starting transfers between devices, swap(): return lax.ppermute(x, HG, [(i, i ^ flip) for i in range(8)])  21.9 us
    all_to_all x2, waiting for transfers between devices, exchange(): return lax.all_to_all(tiles, ALL, 0, 0, tiled=True).reshape(-1, 128)  18.2 us
    all_to_all x1, waiting for transfers between devices, body(): got = lax.all_to_all(sent, 'dp', 0, 0, tiled=True)  17.4 us
    all_to_all x2, starting transfers between devices, exchange(): return lax.all_to_all(tiles, ALL, 0, 0, tiled=True).reshape(-1, 128)  15 us
    pallas_call x1, Pallas kernels, experts_forward(): call(expert_kernel, (shaped((2 * tiles, 128), BF), row, unit, unit, unit)...  9.92 us
    pallas_call x1, Pallas kernels, expert_grads(): pl.pallas_call(expert_grads_kernel, out_shape=(shaped((1, 2, inner, width...  7.96 us
  transfers between devices with their start and end apart: 27, of which 9 were waited for; matrix products, arithmetic and copies ran while one was open for 2% of the time, Pallas kernels for 17%

profile of v4, /device:TPU:0, one launch (start us, length us, event | category | flops | bytes accessed | tf_op | source)
XLA Modules:
  0.0 222.5 jit_solution(6807574008174325811)
XLA Ops:
  0.6 2.9 %collective-permute-start.1 = (bf16[128,2048]{1,0:T(8,128)(2,1)}, bf16[128,2048]{1,0:T(8,128)(2,1)S(1)}, u32[]{:S(2)}, u32[]{:S(2)}) collective-permute-start(bf16[128,2048]{1,0:T(8,128)(2,1)} %tokens.1), channel_id=1, source_target_pairs={{0,5},{1,4},{2,7},{3,6},{4,1},{5,0},{6,3},{7,2},{8,13},{9,12},{10,... | collective-permute-start | bytes 1572872 | tf_op jit(solution)/shard_map/ppermute | solution.py:532
  4.2 2.7 %shard_map.140 = bf16[5120,128]{1,0:T(8,128)(2,1)} custom-call(s32[2]{0:T(128)} %pad_add_fusion.me, s32[2,128]{1,0:T(2,128)} %bitcast.20, f32[2,128]{1,0:T(2,128)} %bitcast.25, bf16[128,2048]{1,0:T(8,128)(2,1)} %grad_out.3), custom_call_target="tpu_custom_call" | custom-call | flops 83886080 | bytes 1310720 | tf_op jit(solution)/shard_map/pallas_call | solution.py:197
  6.9 9.3 %all-to-all-start = ((bf16[128,40,128]{2,1,0:T(8,128)(2,1)}), bf16[128,40,128]{2,1,0:T(8,128)(2,1)}, u32[]{:S(2)}, u32[]{:S(2)}) async-start(bf16[128,40,128]{2,1,0:T(8,128)(2,1)} %bitcast.14), calls=%async_computation | async-start | bytes 2621440 | tf_op jit(solution)/shard_map/all_to_all | solution.py:540
  17.8 24.5 %collective-permute-done.7.w2 = bf16[128,2048]{1,0:T(8,128)(2,1)S(1)} collective-permute-done((bf16[128,2048]{1,0:T(8,128)(2,1)S(1)}, bf16[128,2048]{1,0:T(8,128)(2,1)S(1)}, u32[]{:S(2)}, u32[]{:S(2)}) %collective-permute-start.7) | collective-permute-done | bytes 524320 | tf_op jit(solution)/shard_map/ppermute | solution.py:527
  43.9 6.1 %shard_map.137 = (bf16[512,128]{1,0:T(8,128)(2,1)}, bf16[512,128]{1,0:T(8,128)(2,1)}, bf16[512,128]{1,0:T(8,128)(2,1)}, f32[512,512]{1,0:T(8,128)}, bf16[128,128...) custom-call(s32[2]{0:T(128)} %pad_add_fusion.me, ...), custom_call_target="tpu_custom_call" | custom-call | flops 939524096 | bytes 6815744 | tf_op jit(solution)/shard_map/pallas_call | solution.py:123
  52.0 2.8 %collective-permute-done.4.m2 = bf16[128,128]{1,0:T(8,128)(2,1)S(1)} collective-permute-done((bf16[128,128]{1,0:T(8,128)(2,1)}, bf16[128,128]{1,0:T(8,128)(2,1)S(1)}, u32[]{:S(2)}, u32[]{:S(2)}) %collective-permute-start.4) | collective-permute-done | bytes 32800 | tf_op jit(solution)/shard_map/ppermute | solution.py:527
  55.4 3.2 %shard_map.138 = (f32[128,1024]{1,0:T(8,128)}, bf16[128,1024]{1,0:T(8,128)(2,1)}) custom-call(s32[2]{0:T(128)} %pad_add_fusion.me, bf16[128,128]{1,0:T(8,128)(2,1)} %get-tuple-element.44.m0, bf16[128,128]{1,0:T(8,128)(2,1)} %copy-done.21, bf16[128,128]{1,0:T(8,128)(2,1)} %copy-done.22, bf16[128,128]{1,0:T(8,128)(2,1)} %copy-done.23, bf16[128,2048]{1,0:T(8,128)(2,1)} %w0.3, ...), custom_call_target="tpu_custom_call" | custom-call | flops 268435456 | bytes 2097152 | tf_op jit(solution)/shard_map/pallas_call | solution.py:150
  58.6 3.1 %collective-permute-start.9 = (bf16[128,1024]{1,0:T(8,128)(2,1)}, bf16[128,1024]{1,0:T(8,128)(2,1)S(1)}, u32[]{:S(2)}, u32[]{:S(2)}) collective-permute-start(bf16[128,1024]{1,0:T(8,128)(2,1)} %get-tuple-element.49), channel_id=1, source_target_pairs={{0,1},{1,0},{2,3},{3,2},{4,5},{5,4},{6,7},{7,6},{8,9},{9,8},{10,11... | collective-permute-start | bytes 786440 | tf_op jit(solution)/shard_map/ppermute | solution.py:527
  61.8 4.4 %shard_map.141 = (bf16[320,2048]{1,0:T(8,128)(2,1)}, f32[320,704]{1,0:T(8,128)}) custom-call(bf16[5120,128]{1,0:T(8,128)(2,1)} %bitcast.6.got_grads, bf16[1,704,2048]{2,1,0:T(8,128)(2,1)} %w_down.1), custom_call_target="tpu_custom_call" | custom-call | flops 922746880 | bytes 2883584 | tf_op jit(solution)/shard_map/pallas_call | solution.py:247
  66.2 2.5 %collective-permute-done.9.other = bf16[128,1024]{1,0:T(8,128)(2,1)S(1)} collective-permute-done((bf16[128,1024]{1,0:T(8,128)(2,1)}, bf16[128,1024]{1,0:T(8,128)(2,1)S(1)}, u32[]{:S(2)}, u32[]{:S(2)}) %collective-permute-start.9) | collective-permute-done | bytes 262176 | tf_op jit(solution)/shard_map/ppermute | solution.py:527
  69.5 3.0 %shard_map.139 = (bf16[128,1024]{1,0:T(8,128)(2,1)}, bf16[5120,128]{1,0:T(8,128)(2,1)}) custom-call(s32[2]{0:T(128)} %pad_add_fusion.me, s32[2,128]{1,0:T(2,128)} %bitcast.21, bf16[128,2048]{1,0:T(8,128)(2,1)} %tokens.1, f32[128,1024]{1,0:T(8,128)} %get-tuple-element.48.mine, bf16[128,1024]{1,0:T(8,128)(2,1)} %copy-done.16), custom_call_target="tpu_custom_call" | custom-call | flops 83886080 | bytes 1310720 | tf_op jit(solution)/shard_map/pallas_call | solution.py:210
  72.4 31.0 %all_to_all.20 = bf16[128,40,128]{2,1,0:T(8,128)(2,1)} all-to-all(bf16[128,40,128]{2,1,0:T(8,128)(2,1)} %bitcast.18), channel_id=1, replica_groups=mesh['dp'=16,'head'=4,'group'=2] {'head','group','dp'}, dimensions={0} | all-to-all | bytes 2621440 | tf_op jit(solution)/shard_map/all_to_all | solution.py:540
  103.4 9.9 %shard_map.142 = (bf16[5120,128]{1,0:T(8,128)(2,1)}, bf16[320,2048]{1,0:T(8,128)(2,1)}, bf16[320,704]{1,0:T(8,128)(2,1)}, bf16[320,704]{1,0:T(8,128)(2,1)}, bf16[320,704]{1,0:T(8,128)(2,1)}) custom-call(bf16[5120,128]{1,0:T(8,128)(2,1)} %bitcast.17, f32[320,704]{1,0:T(8,128)} %get-tuple-element.56.upstream_ref, f32[1,2048]{1,0:T(1,128)} %bitcast.23, ...), custom_call_target="tpu_custom_call" | custom-call | flops 3690987520 | bytes 5767168 | tf_op jit(solution)/shard_map/pallas_call | solution.py:304
  113.3 5.7 %all-to-all-start.2 = ((bf16[128,40,128]{2,1,0:T(8,128)(2,1)}), bf16[128,40,128]{2,1,0:T(8,128)(2,1)S(1)}, u32[]{:S(2)}, u32[]{:S(2)}) async-start(bf16[128,40,128]{2,1,0:T(8,128)(2,1)} %bitcast.16), calls=%async_computation.2 | async-start | bytes 2621440 | tf_op jit(solution)/shard_map/all_to_all | solution.py:540
  119.0 2.5 %collective-permute-start.10 = (bf16[128,1024]{1,0:T(8,128)(2,1)S(1)}, bf16[128,1024]{1,0:T(8,128)(2,1)S(1)}, u32[]{:S(2)}, u32[]{:S(2)}) collective-permute-start(bf16[128,1024]{1,0:T(8,128)(2,1)S(1)} %copy-done.17), channel_id=1, source_target_pairs={{0,1},{1,0},{2,3},{3,2},{4,5},{5,4},{6,7},{7,6},{8,9},{9,8},{10,11... | collective-permute-start | bytes 786440 | tf_op jit(solution)/shard_map/ppermute | solution.py:527
  121.6 18.2 %all-to-all-done.2 = bf16[128,40,128]{2,1,0:T(8,128)(2,1)S(1)} async-done(((bf16[128,40,128]{2,1,0:T(8,128)(2,1)}), bf16[128,40,128]{2,1,0:T(8,128)(2,1)S(1)}, u32[]{:S(2)}, u32[]{:S(2)}) %all-to-all-start.2) | async-done | bytes 1310752 | tf_op jit(solution)/shard_map/all_to_all | solution.py:540
  139.7 1.1 copy-done.2
  140.8 2.7 %shard_map.143.normed_mine = bf16[128,1024]{1,0:T(8,128)(2,1)} custom-call(s32[2,128]{1,0:T(2,128)} %bitcast.22, bf16[5120,128]{1,0:T(8,128)(2,1)} %bitcast.15), custom_call_target="tpu_custom_call" | custom-call | flops 83886080 | bytes 1310720 | tf_op jit(solution)/shard_map/pallas_call | solution.py:365
  143.4 2.6 %collective-permute-start.11 = (bf16[128,1024]{1,0:T(8,128)(2,1)}, bf16[128,1024]{1,0:T(8,128)(2,1)S(1)}, u32[]{:S(2)}, u32[]{:S(2)}) collective-permute-start(bf16[128,1024]{1,0:T(8,128)(2,1)} %shard_map.143.normed_mine), channel_id=1, source_target_pairs={{0,1},{1,0},{2,3},{3,2},{4,5},{5,4},{6,7},{7,6},{8,9},{9,8},{10,11... | collective-permute-start | bytes 786440 | tf_op jit(solution)/shard_map/ppermute | solution.py:527
  146.0 6.8 %collective-permute-done.11.normed_other = bf16[128,1024]{1,0:T(8,128)(2,1)S(1)} collective-permute-done((bf16[128,1024]{1,0:T(8,128)(2,1)}, bf16[128,1024]{1,0:T(8,128)(2,1)S(1)}, u32[]{:S(2)}, u32[]{:S(2)}) %collective-permute-start.11) | collective-permute-done | bytes 262176 | tf_op jit(solution)/shard_map/ppermute | solution.py:527
  153.6 3.9 %shard_map.144 = (f32[128,2048]{1,0:T(8,128)}, bf16[128,2048]{1,0:T(8,128)(2,1)}, bf16[128,128]{1,0:T(8,128)(2,1)}, bf16[128,128]{1,0:T(8,128)(2,1)}, bf16[128,1...) custom-call(s32[2]{0:T(128)} %pad_add_fusion.me, bf16[128,2048]{1,0:T(8,128)(2,1)} %grad_out.3, ...), custom_call_target="tpu_custom_call" | custom-call | flops 268435456 | bytes 4718592 | tf_op jit(solution)/shard_map/pallas_call | solution.py:400
  160.2 1.5 collective-permute-done.13.g2
  162.8 5.6 %shard_map.145 = (bf16[512,384]{1,0:T(8,128)(2,1)}, f32[128,2048]{1,0:T(8,128)}, f32[128,2048]{1,0:T(8,128)}, bf16[128,2048]{1,0:T(8,128)(2,1)}, bf16[128,2048]{1,0:T(8,128)(2,1)}) custom-call(bf16[128,128]{1,0:T(8,128)(2,1)} %get-tuple-element.59.g0, bf16[128,128]{1,0:T(8,128)(2,1)} %copy-done.24, bf16[128,128]{1,0:T(8,128)(2,1)} %copy-done.25, ...), custom_call_target="tpu_custom_call" | custom-call | flops 1073741824 | bytes 5767168 | tf_op jit(solution)/shard_map/pallas_call | solution.py:433
  170.5 1.4 convert_add_fusion
  172.8 1.8 collective-permute-start.19
  176.1 2.3 %collective-permute-start.16 = (bf16[64,2048]{1,0:T(8,128)(2,1)}, bf16[64,2048]{1,0:T(8,128)(2,1)S(1)}, u32[]{:S(2)}, u32[]{:S(2)}) collective-permute-start(bf16[64,2048]{1,0:T(8,128)(2,1)} %dynamic-slice_convert_fusion.2), channel_id=1, source_target_pairs={{0,1},{1,0},{2,3},{3,2},{4,5},{5,4},{6,7},{7,6},{8,9},{9,8},{10,11... | collective-permute-start | bytes 786440 | tf_op jit(solution)/shard_map/ppermute | solution.py:527
  180.0 5.0 %shard_map.146 = bf16[16,512,128]{2,1,0:T(8,128)(2,1)} custom-call(bf16[512,384]{1,0:T(8,128)(2,1)} %get-tuple-element.71.acts, bf16[512,2048]{1,0:T(8,128)(2,1)} %get-tuple-element.72.normed, bf16[128,128]{1,0:T(8,128)(2,1)} %get-tuple-element.44.m0, bf16[128,128]{1,0:T(8,128)(2,1)} %get-tuple-element.45.m1, bf16[128,128]{1,0:T(8,128)(2,1)} %get-tuple-element.46.m2, ...), custom_call_target="tpu_custom_call" | custom-call | flops 1073741824 | bytes 6291456 | tf_op jit(solution)/shard_map/pallas_call | solution.py:456
  185.0 4.8 %all-to-all-start.3 = ((bf16[16,512,128]{2,1,0:T(8,128)(2,1)}), bf16[16,512,128]{2,1,0:T(8,128)(2,1)}, u32[]{:S(2)}, u32[]{:S(2)}) async-start(bf16[16,512,128]{2,1,0:T(8,128)(2,1)} %shard_map.146), calls=%async_computation.3 | async-start | bytes 4194304 | tf_op jit(solution)/shard_map/all_to_all | solution.py:586
  191.3 2.2 %collective-permute-start.20 = (bf16[64,2048]{1,0:T(8,128)(2,1)S(1)}, bf16[64,2048]{1,0:T(8,128)(2,1)S(1)}, u32[]{:S(2)}, u32[]{:S(2)}) collective-permute-start(bf16[64,2048]{1,0:T(8,128)(2,1)S(1)} %fusion.6), channel_id=1, source_target_pairs={{0,1},{1,0},{2,3},{3,2},{4,5},{5,4},{6,7},{7,6},{8,9},{9,8},{10,11... | collective-permute-start | bytes 786440 | tf_op jit(solution)/shard_map/ppermute | solution.py:527
  193.5 8.0 %shard_map.148 = (bf16[1,2,704,2048]{3,2,1,0:T(8,128)(2,1)}, bf16[1,704,2048]{2,1,0:T(8,128)(2,1)}) custom-call(bf16[320,2048]{1,0:T(8,128)(2,1)} %get-tuple-element.76.in_rows, bf16[320,2048]{1,0:T(8,128)(2,1)} %get-tuple-element.77.in_grads, bf16[320,704]{1,0:T(8,128)(2,1)} %get-tuple-element.78.product, bf16[320,704]{1,0:T(8,128)(2,1)} %get-tuple-element.79.gate_grad, ...), custom_call_target="tpu_custom_call" | custom-call | flops 2768240640 | bytes 8650752 | tf_op jit(solution)/shard_map/pallas_call | solution.py:331
  202.4 17.4 %all-to-all-done.3.got = bf16[16,512,128]{2,1,0:T(8,128)(2,1)} async-done(((bf16[16,512,128]{2,1,0:T(8,128)(2,1)}), bf16[16,512,128]{2,1,0:T(8,128)(2,1)}, u32[]{:S(2)}, u32[]{:S(2)}) %all-to-all-start.3) | async-done | bytes 2097184 | tf_op jit(solution)/shard_map/all_to_all | solution.py:586
  219.8 2.5 %shard_map.147 = (f32[3,128,128]{2,1,0:T(8,128)}, f32[128,128]{1,0:T(8,128)}) custom-call(bf16[16,512,128]{2,1,0:T(8,128)(2,1)} %all-to-all-done.3.got), custom_call_target="tpu_custom_call" | custom-call | flops 1048576 | bytes 2097152 | tf_op jit(solution)/shard_map/pallas_call | solution.py:482
  (101 shorter events, 20.0 us)
Async XLA Ops:
  0.6 16.6 %collective-permute-start.1 = (bf16[128,2048]{1,0:T(8,128)(2,1)}, bf16[128,2048]{1,0:T(8,128)(2,1)S(1)}, u32[]{:S(2)}, u32[]{:S(2)}) collective-permute-start(bf16[128,2048]{1,0:T(8,128)(2,1)} %tokens.1), channel_id=1, source_target_pairs={{0,5},{1,4},{2,7},{3,6},{4,1},{5,0},{6,3},{7,2},{8,13},{9,12},{10,... | collective-permute-start | bytes 1572872 | tf_op jit(solution)/shard_map/ppermute | solution.py:532
  6.9 9.3 %copy-start.3 = (bf16[128,2048]{1,0:T(8,128)(2,1)S(1)}, bf16[128,2048]{1,0:T(8,128)(2,1)}, u32[]{:S(2)}) copy-start(bf16[128,2048]{1,0:T(8,128)(2,1)} %w0.3) | copy-start | bytes 1572868
  6.9 10.3 %copy-start = (bf16[128,2048]{1,0:T(8,128)(2,1)S(1)}, bf16[128,2048]{1,0:T(8,128)(2,1)}, u32[]{:S(2)}) copy-start(bf16[128,2048]{1,0:T(8,128)(2,1)} %tokens.1) | copy-start | bytes 1572868
  6.9 54.9 %all-to-all-start = ((bf16[128,40,128]{2,1,0:T(8,128)(2,1)}), bf16[128,40,128]{2,1,0:T(8,128)(2,1)}, u32[]{:S(2)}, u32[]{:S(2)}) async-start(bf16[128,40,128]{2,1,0:T(8,128)(2,1)} %bitcast.14), calls=%async_computation | async-start | bytes 2621440 | tf_op jit(solution)/shard_map/all_to_all | solution.py:540
  16.2 26.1 %collective-permute-start.7 = (bf16[128,2048]{1,0:T(8,128)(2,1)S(1)}, bf16[128,2048]{1,0:T(8,128)(2,1)S(1)}, u32[]{:S(2)}, u32[]{:S(2)}) collective-permute-start(bf16[128,2048]{1,0:T(8,128)(2,1)S(1)} %copy-done.3), channel_id=1, source_target_pairs={{0,4},{1,5},{2,6},{3,7},{4,0},{5,1},{6,2},{7,3},{8,12},{9,13},{10,... | collective-permute-start | bytes 1572872 | tf_op jit(solution)/shard_map/ppermute | solution.py:527
  17.2 25.1 %collective-permute-start = (bf16[128,2048]{1,0:T(8,128)(2,1)S(1)}, bf16[128,2048]{1,0:T(8,128)(2,1)S(1)}, u32[]{:S(2)}, u32[]{:S(2)}) collective-permute-start(bf16[128,2048]{1,0:T(8,128)(2,1)S(1)} %copy-done), channel_id=1, source_target_pairs={{0,2},{1,3},{2,0},{3,1},{4,6},{5,7},{6,4},{7,5},{8,10},{9,11},{10,... | collective-permute-start | bytes 1572872 | tf_op jit(solution)/shard_map/ppermute | solution.py:527
  17.2 26.7 %copy-start.8 = (bf16[128,2048]{1,0:T(8,128)(2,1)}, bf16[128,2048]{1,0:T(8,128)(2,1)S(1)}, u32[]{:S(2)}) copy-start(bf16[128,2048]{1,0:T(8,128)(2,1)S(1)} %collective-permute-done.1.t2) | copy-start | bytes 1572868
  17.2 25.1 %collective-permute-start.2 = (bf16[128,2048]{1,0:T(8,128)(2,1)S(1)}, bf16[128,2048]{1,0:T(8,128)(2,1)S(1)}, u32[]{:S(2)}, u32[]{:S(2)}) collective-permute-start(bf16[128,2048]{1,0:T(8,128)(2,1)S(1)} %collective-permute-done.1.t2), channel_id=1, source_target_pairs={{0,2},{1,3},{2,0},{3,1},{4,6},{5,7},{6,4},{7,5},{8,10},{9,11},{10,... | collective-permute-start | bytes 1572872 | tf_op jit(solution)/shard_map/ppermute | solution.py:527
  17.7 34.3 %collective-permute-start.6 = (bf16[128,2048]{1,0:T(8,128)(2,1)S(1)}, bf16[128,2048]{1,0:T(8,128)(2,1)S(1)}, u32[]{:S(2)}, u32[]{:S(2)}) collective-permute-start(bf16[128,2048]{1,0:T(8,128)(2,1)S(1)} %copy-done.3), channel_id=1, source_target_pairs={{0,2},{1,3},{2,0},{3,1},{4,6},{5,7},{6,4},{7,5},{8,10},{9,11},{10,... | collective-permute-start | bytes 1572872 | tf_op jit(solution)/shard_map/ppermute | solution.py:527
  42.3 7.8 %copy-start.4 = (bf16[128,2048]{1,0:T(8,128)(2,1)}, bf16[128,2048]{1,0:T(8,128)(2,1)S(1)}, u32[]{:S(2)}) copy-start(bf16[128,2048]{1,0:T(8,128)(2,1)S(1)} %collective-permute-done.7.w2) | copy-start | bytes 1572868
  42.3 9.7 %collective-permute-start.8 = (bf16[128,2048]{1,0:T(8,128)(2,1)S(1)}, bf16[128,2048]{1,0:T(8,128)(2,1)S(1)}, u32[]{:S(2)}, u32[]{:S(2)}) collective-permute-start(bf16[128,2048]{1,0:T(8,128)(2,1)S(1)} %collective-permute-done.7.w2), channel_id=1, source_target_pairs={{0,2},{1,3},{2,0},{3,1},{4,6},{5,7},{6,4},{7,5},{8,10},{9,11},{10,... | collective-permute-start | bytes 1572872 | tf_op jit(solution)/shard_map/ppermute | solution.py:527
  50.0 1.9 collective-permute-start.3
  50.5 4.3 %collective-permute-start.4 = (bf16[128,128]{1,0:T(8,128)(2,1)}, bf16[128,128]{1,0:T(8,128)(2,1)S(1)}, u32[]{:S(2)}, u32[]{:S(2)}) collective-permute-start(bf16[128,128]{1,0:T(8,128)(2,1)} %get-tuple-element.46.m2), channel_id=1, source_target_pairs={{0,4},{1,5},{2,6},{3,7},{4,0},{5,1},{6,2},{7,3},{8,12},{9,13},{10,... | collective-permute-start | bytes 98312 | tf_op jit(solution)/shard_map/ppermute | solution.py:527
  50.9 3.9 %collective-permute-start.5 = (bf16[128,128]{1,0:T(8,128)(2,1)}, bf16[128,128]{1,0:T(8,128)(2,1)S(1)}, u32[]{:S(2)}, u32[]{:S(2)}) collective-permute-start(bf16[128,128]{1,0:T(8,128)(2,1)} %get-tuple-element.47.m3), channel_id=1, source_target_pairs={{0,6},{1,7},{2,4},{3,5},{4,2},{5,3},{6,0},{7,1},{8,14},{9,15},{10,... | collective-permute-start | bytes 98312 | tf_op jit(solution)/shard_map/ppermute | solution.py:527
  58.6 10.1 %collective-permute-start.9 = (bf16[128,1024]{1,0:T(8,128)(2,1)}, bf16[128,1024]{1,0:T(8,128)(2,1)S(1)}, u32[]{:S(2)}, u32[]{:S(2)}) collective-permute-start(bf16[128,1024]{1,0:T(8,128)(2,1)} %get-tuple-element.49), channel_id=1, source_target_pairs={{0,1},{1,0},{2,3},{3,2},{4,5},{5,4},{6,7},{7,6},{8,9},{9,8},{10,11... | collective-permute-start | bytes 786440 | tf_op jit(solution)/shard_map/ppermute | solution.py:527
  113.3 26.4 %all-to-all-start.2 = ((bf16[128,40,128]{2,1,0:T(8,128)(2,1)}), bf16[128,40,128]{2,1,0:T(8,128)(2,1)S(1)}, u32[]{:S(2)}, u32[]{:S(2)}) async-start(bf16[128,40,128]{2,1,0:T(8,128)(2,1)} %bitcast.16), calls=%async_computation.2 | async-start | bytes 2621440 | tf_op jit(solution)/shard_map/all_to_all | solution.py:540
  119.0 27.0 %collective-permute-start.10 = (bf16[128,1024]{1,0:T(8,128)(2,1)S(1)}, bf16[128,1024]{1,0:T(8,128)(2,1)S(1)}, u32[]{:S(2)}, u32[]{:S(2)}) collective-permute-start(bf16[128,1024]{1,0:T(8,128)(2,1)S(1)} %copy-done.17), channel_id=1, source_target_pairs={{0,1},{1,0},{2,3},{3,2},{4,5},{5,4},{6,7},{7,6},{8,9},{9,8},{10,11... | collective-permute-start | bytes 786440 | tf_op jit(solution)/shard_map/ppermute | solution.py:527
  143.4 9.4 %collective-permute-start.11 = (bf16[128,1024]{1,0:T(8,128)(2,1)}, bf16[128,1024]{1,0:T(8,128)(2,1)S(1)}, u32[]{:S(2)}, u32[]{:S(2)}) collective-permute-start(bf16[128,1024]{1,0:T(8,128)(2,1)} %shard_map.143.normed_mine), channel_id=1, source_target_pairs={{0,1},{1,0},{2,3},{3,2},{4,5},{5,4},{6,7},{7,6},{8,9},{9,8},{10,11... | collective-permute-start | bytes 786440 | tf_op jit(solution)/shard_map/ppermute | solution.py:527
  146.0 6.8 %copy-start.18 = (bf16[128,1024]{1,0:T(8,128)(2,1)}, bf16[128,1024]{1,0:T(8,128)(2,1)S(1)}, u32[]{:S(2)}) copy-start(bf16[128,1024]{1,0:T(8,128)(2,1)S(1)} %collective-permute-done.10.hidden_other) | copy-start | bytes 786436
  157.5 2.8 %collective-permute-start.12 = (bf16[128,128]{1,0:T(8,128)(2,1)}, bf16[128,128]{1,0:T(8,128)(2,1)S(1)}, u32[]{:S(2)}, u32[]{:S(2)}) collective-permute-start(bf16[128,128]{1,0:T(8,128)(2,1)} %get-tuple-element.60), channel_id=1, source_target_pairs={{0,2},{1,3},{2,0},{3,1},{4,6},{5,7},{6,4},{7,5},{8,10},{9,11},{10,... | collective-permute-start | bytes 98312 | tf_op jit(solution)/shard_map/ppermute | solution.py:527
  157.5 4.3 %collective-permute-start.13 = (bf16[128,128]{1,0:T(8,128)(2,1)}, bf16[128,128]{1,0:T(8,128)(2,1)S(1)}, u32[]{:S(2)}, u32[]{:S(2)}) collective-permute-start(bf16[128,128]{1,0:T(8,128)(2,1)} %get-tuple-element.61), channel_id=1, source_target_pairs={{0,4},{1,5},{2,6},{3,7},{4,0},{5,1},{6,2},{7,3},{8,12},{9,13},{10,... | collective-permute-start | bytes 98312 | tf_op jit(solution)/shard_map/ppermute | solution.py:527
  158.5 3.7 %collective-permute-start.14 = (bf16[128,128]{1,0:T(8,128)(2,1)}, bf16[128,128]{1,0:T(8,128)(2,1)S(1)}, u32[]{:S(2)}, u32[]{:S(2)}) collective-permute-start(bf16[128,128]{1,0:T(8,128)(2,1)} %get-tuple-element.62), channel_id=1, source_target_pairs={{0,6},{1,7},{2,4},{3,5},{4,2},{5,3},{6,0},{7,1},{8,14},{9,15},{10,... | collective-permute-start | bytes 98312 | tf_op jit(solution)/shard_map/ppermute | solution.py:527
  159.4 10.1 %collective-permute-start.22 = (bf16[128,2048]{1,0:T(8,128)(2,1)}, bf16[128,2048]{1,0:T(8,128)(2,1)S(1)}, u32[]{:S(2)}, u32[]{:S(2)}) collective-permute-start(bf16[128,2048]{1,0:T(8,128)(2,1)} %get-tuple-element.73.g0), channel_id=1, source_target_pairs={{0,4},{1,5},{2,7},{3,6},{4,0},{5,1},{6,3},{7,2},{8,12},{9,13},{10,... | collective-permute-start | bytes 1572872 | tf_op jit(solution)/shard_map/ppermute | solution.py:532
  168.4 2.1 collective-permute-start.17
  168.6 9.8 %collective-permute-start.21 = (bf16[128,2048]{1,0:T(8,128)(2,1)S(1)}, bf16[128,2048]{1,0:T(8,128)(2,1)S(1)}, u32[]{:S(2)}, u32[]{:S(2)}) collective-permute-start(bf16[128,2048]{1,0:T(8,128)(2,1)S(1)} %copy-done.11), channel_id=1, source_target_pairs={{0,2},{1,3},{2,0},{3,1},{4,6},{5,7},{6,4},{7,5},{8,10},{9,11},{10,... | collective-permute-start | bytes 1572872 | tf_op jit(solution)/shard_map/ppermute | solution.py:527
  169.3 5.9 %collective-permute-start.15 = (bf16[128,2048]{1,0:T(8,128)(2,1)}, bf16[128,2048]{1,0:T(8,128)(2,1)S(1)}, u32[]{:S(2)}, u32[]{:S(2)}) collective-permute-start(bf16[128,2048]{1,0:T(8,128)(2,1)} %get-tuple-element.68), channel_id=1, source_target_pairs={{0,2},{1,3},{2,0},{3,1},{4,6},{5,7},{6,4},{7,5},{8,10},{9,11},{10,... | collective-permute-start | bytes 1572872 | tf_op jit(solution)/shard_map/ppermute | solution.py:527
  169.5 9.0 %collective-permute-start.23 = (bf16[128,2048]{1,0:T(8,128)(2,1)S(1)}, bf16[128,2048]{1,0:T(8,128)(2,1)S(1)}, u32[]{:S(2)}, u32[]{:S(2)}) collective-permute-start(bf16[128,2048]{1,0:T(8,128)(2,1)S(1)} %collective-permute-done.22.g2), channel_id=1, source_target_pairs={{0,2},{1,3},{2,0},{3,1},{4,6},{5,7},{6,4},{7,5},{8,10},{9,11},{10,... | collective-permute-start | bytes 1572872 | tf_op jit(solution)/shard_map/ppermute | solution.py:527
  172.8 17.0 %collective-permute-start.19 = (bf16[64,2048]{1,0:T(8,128)(2,1)}, bf16[64,2048]{1,0:T(8,128)(2,1)S(1)}, u32[]{:S(2)}, u32[]{:S(2)}) collective-permute-start(bf16[64,2048]{1,0:T(8,128)(2,1)} %get-tuple-element.86), channel_id=1, source_target_pairs={{0,5},{1,4},{2,7},{3,6},{4,1},{5,0},{6,3},{7,2},{8,13},{9,12},{10,... | collective-permute-start | bytes 786440 | tf_op jit(solution)/shard_map/ppermute | solution.py:527
  174.6 15.3 %collective-permute-start.18 = (bf16[64,2048]{1,0:T(8,128)(2,1)}, bf16[64,2048]{1,0:T(8,128)(2,1)S(1)}, u32[]{:S(2)}, u32[]{:S(2)}) collective-permute-start(bf16[64,2048]{1,0:T(8,128)(2,1)} %get-tuple-element.85), channel_id=1, source_target_pairs={{0,4},{1,5},{2,6},{3,7},{4,0},{5,1},{6,2},{7,3},{8,12},{9,13},{10,... | collective-permute-start | bytes 786440 | tf_op jit(solution)/shard_map/ppermute | solution.py:527
  176.1 13.7 %collective-permute-start.16 = (bf16[64,2048]{1,0:T(8,128)(2,1)}, bf16[64,2048]{1,0:T(8,128)(2,1)S(1)}, u32[]{:S(2)}, u32[]{:S(2)}) collective-permute-start(bf16[64,2048]{1,0:T(8,128)(2,1)} %dynamic-slice_convert_fusion.2), channel_id=1, source_target_pairs={{0,1},{1,0},{2,3},{3,2},{4,5},{5,4},{6,7},{7,6},{8,9},{9,8},{10,11... | collective-permute-start | bytes 786440 | tf_op jit(solution)/shard_map/ppermute | solution.py:527
  185.0 34.8 %all-to-all-start.3 = ((bf16[16,512,128]{2,1,0:T(8,128)(2,1)}), bf16[16,512,128]{2,1,0:T(8,128)(2,1)}, u32[]{:S(2)}, u32[]{:S(2)}) async-start(bf16[16,512,128]{2,1,0:T(8,128)(2,1)} %shard_map.146), calls=%async_computation.3 | async-start | bytes 4194304 | tf_op jit(solution)/shard_map/all_to_all | solution.py:586
  191.3 10.2 %collective-permute-start.20 = (bf16[64,2048]{1,0:T(8,128)(2,1)S(1)}, bf16[64,2048]{1,0:T(8,128)(2,1)S(1)}, u32[]{:S(2)}, u32[]{:S(2)}) collective-permute-start(bf16[64,2048]{1,0:T(8,128)(2,1)S(1)} %fusion.6), channel_id=1, source_target_pairs={{0,1},{1,0},{2,3},{3,2},{4,5},{5,4},{6,7},{7,6},{8,9},{9,8},{10,11... | collective-permute-start | bytes 786440 | tf_op jit(solution)/shard_map/ppermute | solution.py:527
  (22 other events, 50.2 us)
